TPU v7x, 1024 devices: a whole 4x8x16 slice. The times are simulated.
1024 devices in a mesh: group: 64 (over y, z_hi, core), tensor: 16 (over z_lo, x).
Axes of the slice: x: 4, y: 8, z: 16 (z_hi: 4, z_lo: 4; z = z_hi * 4 + z_lo), core: 2. Of those that a mesh axis runs over, the one named last changes fastest.
Arguments:
- latents: bfloat16 [64, 256, 3072], P('group', 'tensor'), may hold values from -6 to 6
- stored_sample: bfloat16 [64, 256, 3072], P('group', 'tensor'), may hold values from -6 to 6
- timestep: int32 [64], P('group'), may hold values from 0 to 7
- owner_map: int32 [64], replicated, may hold values from 0 to 63, each once
- mod_table: float32 [8, 3, 3072], replicated, may hold values from -3 to 3
- qkv_weight: bfloat16 [3072, 6144], P('group', 'tensor'), may hold values from -0.5412659 to 0.5412659
- out_weight: bfloat16 [2048, 3072], P('tensor', 'group'), may hold values from -0.125 to 0.125
Outputs:
- mean_next: bfloat16 [64, 256, 3072], P('group', 'tensor')
- log_prob: float32 [64], P('group')
Inputs may be any that keep to these rules, and one draw needn't show every extreme that they name: `owner_map`: each index of group holds exactly one slice.
All inputs are finite; a program needn't handle non-finite values.
Results may differ from a plain program's by a relative error of at most 0.0075.
Values may be sent and summed in bfloat16 or wider, within the bound.
No kernel may reach another device: no remote copies, remote signals or barrier semaphores. Data moves between devices by JAX's collectives and lax.ppermute only.
A program may use at most 32 MiB of HBM per device.

v0:
```python
import math

import jax
import jax.numpy as jnp
from jax import lax
from jax.sharding import PartitionSpec as P


def sent_to_all(x, axis):
    copies = jnp.broadcast_to(x, (lax.axis_size(axis), *x.shape))
    return lax.all_to_all(copies, axis, split_axis=0, concat_axis=0, tiled=True)


def laid_out(pieces, dim):
    pieces = jnp.moveaxis(pieces, 0, dim)
    lengths = pieces.shape
    return pieces.reshape(*lengths[:dim], lengths[dim] * lengths[dim + 1], *lengths[dim + 2 :])


def collect(x, axis, dim):
    pieces = sent_to_all(x, axis)
    return laid_out(pieces, dim)


def side_by_side(arrays, axis, dim, along):
    widths = [a.shape[along] for a in arrays]
    both = jnp.concatenate(arrays, axis=along)
    result = lax.all_gather(both, axis, axis=dim, tiled=True)
    return tuple(jnp.split(result, [sum(widths[:k]) for k in range(1, len(widths))], axis=along))


def in_blocks(x, dim, devices):
    before, after = (x.shape[:dim], x.shape[dim + 1 :])
    return jnp.moveaxis(x.reshape(*before, devices, -1, *after), dim, 0)


def sent_and_summed(x, axis, dim):
    pieces = in_blocks(x, dim, lax.axis_size(axis))
    arrived = lax.all_to_all(pieces, axis, split_axis=0, concat_axis=0, tiled=True)
    return arrived.astype(jnp.float32).sum(axis=0)


def of_everyone(x, axis):
    return sent_to_all(x, axis).sum(axis=0)


def shards(latents, stored_sample, timestep, owner_map, mod_table, qkv_weight, out_weight):
    groups = lax.axis_size("group")
    cycle_size = lax.axis_size("tensor")
    samples, tok_local, model_width = latents.shape
    slice_rows = qkv_weight.shape[0]
    head_dim = out_weight.shape[0]
    step_count = mod_table.shape[0]
    seq_len = tok_local * cycle_size
    onehot = (timestep[:, None] == jnp.arange(step_count, dtype=jnp.int32)[None, :]).astype(
        jnp.float32
    )
    modulation = jnp.einsum("bs,scd->bcd", onehot, mod_table, precision=lax.Precision.HIGHEST)
    shift_rows = modulation[:, 0][:, None, :]
    scale_rows = modulation[:, 1][:, None, :]
    gate_rows = modulation[:, 2][:, None, :]
    latent_f = latents.astype(jnp.float32)
    centred = latent_f - jnp.mean(latent_f, axis=-1, keepdims=True)
    variance = jnp.mean(centred * centred, axis=-1, keepdims=True)
    normed = centred * lax.rsqrt(variance + 1e-06)
    modulated = (normed * (1.0 + scale_rows) + shift_rows).astype(jnp.bfloat16)
    gathered = collect(modulated, "tensor", 1)
    flat_rows = gathered.reshape(samples * seq_len, model_width)
    matches = owner_map[None, :] == jnp.arange(groups, dtype=jnp.int32)[:, None]
    slot_of = jnp.sum(jnp.where(matches, jnp.arange(groups, dtype=jnp.int32)[None, :], 0), axis=1)
    qkv_zero = jnp.zeros((samples * seq_len, qkv_weight.shape[1]), jnp.float32)
    out_rows = out_weight.T
    placed_zero = jnp.zeros((model_width, head_dim), jnp.bfloat16)
    portions = side_by_side((qkv_weight, out_rows), "group", 0, 1)
    row_index = jnp.arange(portions[0].shape[0], dtype=jnp.int32)
    columns = slot_of[row_index // slice_rows] * slice_rows + row_index % slice_rows
    picked = jnp.take(flat_rows, columns, axis=1)
    running = jnp.dot(picked, portions[0], preferred_element_type=jnp.float32)
    positioned = (qkv_zero, placed_zero)[1].at[columns].set(portions[1])
    qkv = running.astype(jnp.bfloat16).reshape(samples, seq_len, 3, head_dim)
    query_rows = qkv[:, :, 0]
    key_matrix_rows = qkv[:, :, 1]
    value_matrix_rows = qkv[:, :, 2]
    attention_scores = jnp.einsum(
        "lph,lih->lpi", query_rows, key_matrix_rows, preferred_element_type=jnp.float32
    ) / math.sqrt(head_dim)
    attention_scores = attention_scores - jnp.max(attention_scores, axis=-1, keepdims=True)
    expo = jnp.exp(attention_scores)
    attention_probabilities = (expo / jnp.sum(expo, axis=-1, keepdims=True)).astype(jnp.bfloat16)
    attended = jnp.einsum(
        "ftn,fnv->ftv",
        attention_probabilities,
        value_matrix_rows,
        preferred_element_type=jnp.float32,
    ).astype(jnp.bfloat16)
    attended_flat = attended.reshape(samples * seq_len, head_dim)
    projected = lax.dot_general(
        attended_flat, positioned, (((1,), (1,)), ((), ())), preferred_element_type=jnp.float32
    )
    ordered = projected.reshape(samples, seq_len, model_width)
    head_term = ordered.astype(jnp.bfloat16)
    proj = sent_and_summed(head_term, "tensor", 1)
    hidden = latent_f + gate_rows * proj
    time_float = timestep.astype(jnp.float32)
    step_size = ((time_float + 1.0) / step_count)[:, None, None]
    mean = latent_f - step_size * hidden
    noise_sigma_scale = 0.3 + 0.1 * time_float
    residual = stored_sample.astype(jnp.float32) - mean
    partial_sums = jnp.sum(residual * residual, axis=(1, 2))
    totals = of_everyone(partial_sums, "tensor")
    log_prob = (
        -totals / (2.0 * noise_sigma_scale * noise_sigma_scale * seq_len * model_width)
        - jnp.log(noise_sigma_scale)
        - 0.5 * math.log(2.0 * math.pi)
    )
    return (mean.astype(jnp.bfloat16), log_prob)


def solution(mesh):
    in_specs = (
        P("group", "tensor", None),
        P("group", "tensor", None),
        P("group"),
        P(),
        P(),
        P("group", "tensor"),
        P("tensor", "group"),
    )
    out_specs = (P("group", "tensor", None), P("group"))
    return jax.shard_map(shards, mesh=mesh, in_specs=in_specs, out_specs=out_specs, check_vma=False)
```

profile of v0, /device:TPU:56, one launch (start us, length us, event | category | flops | bytes accessed | tf_op | source)
XLA Modules:
  0.0 219.6 jit_solution(14631482965977825674)
XLA Ops:
  7.2 1.4 pad_maximum_fusion
  9.4 0.3 fusion.33
  9.6 1.0 convert_reduce_fusion.1
  10.7 1.1 fusion.16
  11.8 1.0 fusion.26
  12.8 1.3 broadcast_in_dim.46
  14.1 10.0 %all-to-all-start = ((bf16[16,1,16,3072]{3,2,1,0:T(8,128)(2,1)}), bf16[16,1,16,3072]{3,2,1,0:T(8,128)(2,1)S(1)}, u32[]{:S(2)}, u32[]{:S(2)}) async-start(bf16[16,1,16,3072]{3,2,1,0:T(8,128)(2,1)} %broadcast_in_dim.46), calls=%async_computation | async-start | bytes 3145728 | tf_op jit(solution)/shard_map/all_to_all | solution.py:11
  24.1 0.1 compare_reduce_fusion
  24.2 0.1 compare_reduce_fusion.1
  24.3 0.1 compare_reduce_fusion.10
  24.4 0.1 compare_reduce_fusion.11
  24.8 0.1 compare_reduce_fusion.15
  24.9 0.1 compare_reduce_fusion.16
  25.0 0.1 compare_reduce_fusion.17
  25.3 0.1 compare_reduce_fusion.20
  25.4 0.1 compare_reduce_fusion.21
  25.5 0.1 compare_reduce_fusion.22
  25.9 0.1 compare_reduce_fusion.26
  26.0 0.1 compare_reduce_fusion.27
  26.1 0.1 compare_reduce_fusion.28
  26.2 0.1 compare_reduce_fusion.29
  26.6 0.1 compare_reduce_fusion.32
  26.7 0.1 compare_reduce_fusion.33
  26.8 0.1 compare_reduce_fusion.34
  27.1 0.1 compare_reduce_fusion.38
  29.5 0.1 select_reduce_fusion
  29.6 0.7 fusion.43
  30.3 0.7 fusion.40
  31.0 0.7 fusion.41
  31.7 0.7 fusion.42
  32.5 4.5 %compare_select_fusion.2 = s32[3072,1]{0,1:T(1,128)S(1)} fusion(s32[]{:T(128)} %bitcast.62, s32[]{:T(128)} %bitcast.63, s32[]{:T(128)} %bitcast.64, s32[]{:T(128)} %bitcast.65, s32[]{:T(128)} %bitcast.66, s32[]{:T(128)} %bitcast.68, s32[]{:T(128)} %bitcast.67), kind=kLoop, calls=%fused_computation.98 | loop fusion | flops 70656 | bytes 12316 | tf_op jit(solution)/shard_map/gather | solution.py:76
  36.9 35.8 %compare_and_fusion = (pred[3072]{0:T(1024)(128)(4,1)S(1)}, s32[3072]{0:T(1024)S(1)}) fusion(pred[3072]{0:T(1024)(128)(4,1)S(1)} %compare_reduce_fusion, pred[3072]{0:T(1024)(128)(4,1)S(1)} %compare_reduce_fusion.1, pred[3072]{0:T(1024)(128)(4,1)S(1)} %compare_reduce_fusion.2, pred[3072]{0:T(1024)(128)(4,1)S(1)} %compare_reduce_fusion.3, ...), kind=kLoop, calls=%fused_computation.122 | loop fusion | flops 218112 | bytes 202980 | tf_op jit(solution)/shard_map/jit(_take)/and | solution.py:77
  72.9 0.7 copy.27
  73.6 11.1 %gather_fusion = bf16[3072,256]{1,0:T(8,128)(2,1)S(1)} fusion(bf16[256,3072]{0,1:T(8,128)(2,1)S(1)} %copy.27, s32[3072]{0:T(1024)S(1)} %broadcast_clamp_fusion), kind=kCustom, calls=%fused_computation | custom fusion | bytes 3158016 | tf_op jit(solution)/shard_map/jit(_take)/gather | solution.py:77
  84.6 53.2 %all-gather.2.cloned.1.call-done = bf16[3072,512]{1,0:T(8,128)(2,1)} async-done(((bf16[48,512]{1,0:T(8,128)(2,1)}), bf16[3072,512]{1,0:T(8,128)(2,1)}) %all-gather.2.cloned.1.call-update) | async-done | bytes 3145744 | tf_op jit(solution)/shard_map/all_gather | solution.py:28
  137.9 3.6 %fusion.4 = bf16[256,384]{1,0:T(8,128)(2,1)S(1)} fusion(bf16[3072,512]{1,0:T(8,128)(2,1)} %all-gather.2.cloned.1.call-done, bf16[3072,256]{1,0:T(8,128)(2,1)S(1)} %gather_fusion, pred[3072]{0:T(1024)(128)(4,1)S(1)} %get-tuple-element.2), kind=kOutput, calls=%fused_computation.8 | convolution fusion | flops 604864512 | bytes 4131840 | tf_op jit(solution)/shard_map/dot_general | solution.py:78
  141.5 0.1 copy.28
  141.7 0.3 fusion.44
  142.0 8.8 %scatter_custom_fusion = bf16[3072,128]{1,0:T(8,128)(2,1)S(1)} fusion(s32[3072]{0:T(1024)S(1)} %bitcast.128, bf16[3072,512]{1,0:T(8,128)(2,1)} %all-gather.2.cloned.1.call-done, bf16[]{:T(256)} %constant.70.clone.1), kind=kCustom, calls=%fused_computation.11 | custom fusion | bytes 1573376 | tf_op jit(solution)/shard_map/scatter | solution.py:79
  150.8 1.9 convolution_convert_fusion
  152.7 4.4 %all-to-all-start.1 = ((bf16[16,1,16,3072]{3,2,1,0:T(8,128)(2,1)}), bf16[16,1,16,3072]{3,2,1,0:T(8,128)(2,1)S(1)}, u32[]{:S(2)}, u32[]{:S(2)}) async-start(bf16[16,1,16,3072]{3,2,1,0:T(8,128)(2,1)} %bitcast.82), calls=%async_computation.1 | async-start | bytes 3145728 | tf_op jit(solution)/shard_map/all_to_all | solution.py:39
  157.2 34.1 %all-to-all-done.1 = bf16[16,1,16,3072]{3,2,1,0:T(8,128)(2,1)S(1)} async-done(((bf16[16,1,16,3072]{3,2,1,0:T(8,128)(2,1)}), bf16[16,1,16,3072]{3,2,1,0:T(8,128)(2,1)S(1)}, u32[]{:S(2)}, u32[]{:S(2)}) %all-to-all-start.1) | async-done | bytes 1572896 | tf_op jit(solution)/shard_map/all_to_all | solution.py:39
  191.3 0.2 convert_reduce_fusion
  191.5 1.3 multiply_reduce_fusion
  192.8 1.2 broadcast_in_dim.49
  194.0 8.4 %all-to-all-start.2 = ((f32[16,1,1]{2,1,0:T(1,128)}), f32[16,1,1]{2,1,0:T(1,128)S(1)}, u32[]{:S(2)}, u32[]{:S(2)}) async-start(f32[16,1,1]{2,1,0:T(1,128)} %broadcast_in_dim.49), calls=%async_computation.2 | async-start | bytes 16384 | tf_op jit(solution)/shard_map/all_to_all | solution.py:11
  202.4 7.9 %all-to-all-done.2 = f32[16,1,1]{2,1,0:T(1,128)S(1)} async-done(((f32[16,1,1]{2,1,0:T(1,128)}), f32[16,1,1]{2,1,0:T(1,128)S(1)}, u32[]{:S(2)}, u32[]{:S(2)}) %all-to-all-start.2) | async-done | bytes 96 | tf_op jit(solution)/shard_map/all_to_all | solution.py:11
  210.3 0.6 reduce_sum.72
  (57 shorter events, 3.9 us)
Async XLA Ops:
  7.2 2.2 copy-start
  7.2 130.7 %all-gather.2.cloned.1.call-start = ((), (), s32[]{:S(2)}) async-start(), calls=%async_computation.3 | async-start | bytes 3194880 | tf_op jit(solution)/shard_map/all_gather | solution.py:28
  14.1 15.4 %copy-start.3 = (s32[64]{0:T(128)S(1)}, s32[64]{0:T(128)}, u32[]{:S(2)}) copy-start(s32[64]{0:T(128)} %param.10) | copy-start | bytes 772
  14.1 58.7 %all-to-all-start = ((bf16[16,1,16,3072]{3,2,1,0:T(8,128)(2,1)}), bf16[16,1,16,3072]{3,2,1,0:T(8,128)(2,1)S(1)}, u32[]{:S(2)}, u32[]{:S(2)}) async-start(bf16[16,1,16,3072]{3,2,1,0:T(8,128)(2,1)} %broadcast_in_dim.46), calls=%async_computation | async-start | bytes 3145728 | tf_op jit(solution)/shard_map/all_to_all | solution.py:11
  152.7 38.6 %all-to-all-start.1 = ((bf16[16,1,16,3072]{3,2,1,0:T(8,128)(2,1)}), bf16[16,1,16,3072]{3,2,1,0:T(8,128)(2,1)S(1)}, u32[]{:S(2)}, u32[]{:S(2)}) async-start(bf16[16,1,16,3072]{3,2,1,0:T(8,128)(2,1)} %bitcast.82), calls=%async_computation.1 | async-start | bytes 3145728 | tf_op jit(solution)/shard_map/all_to_all | solution.py:39
  157.1 34.4 %copy-start.1 = (bf16[1,16,3072]{2,1,0:T(8,128)(2,1)S(1)}, bf16[1,16,3072]{2,1,0:T(8,128)(2,1)}, u32[]{:S(2)}) copy-start(bf16[1,16,3072]{2,1,0:T(8,128)(2,1)} %param.7) | copy-start | bytes 294916
  157.1 34.4 %copy-start.2 = (bf16[1,16,3072]{2,1,0:T(8,128)(2,1)S(1)}, bf16[1,16,3072]{2,1,0:T(8,128)(2,1)}, u32[]{:S(2)}) copy-start(bf16[1,16,3072]{2,1,0:T(8,128)(2,1)} %param.8) | copy-start | bytes 294916
  194.0 16.3 %all-to-all-start.2 = ((f32[16,1,1]{2,1,0:T(1,128)}), f32[16,1,1]{2,1,0:T(1,128)S(1)}, u32[]{:S(2)}, u32[]{:S(2)}) async-start(f32[16,1,1]{2,1,0:T(1,128)} %broadcast_in_dim.49), calls=%async_computation.2 | async-start | bytes 16384 | tf_op jit(solution)/shard_map/all_to_all | solution.py:11
Sparse Core Ops, SparseCore 0:
  13.0 124.7 all-gather.1
where the time goes:
time: 221 us; the launch traced here: 220 us
  waiting for transfers between devices  95.3 us (43%)
  other arithmetic  52.7 us (24%)
  local copies, waits for them, and re-layouts  26.1 us (12%)
  starting transfers between devices  22.7 us (10%)
  between operations  16.8 us (8%)
  matrix products  6.02 us (3%)
    all_gather x1, waiting for transfers between devices, side_by_side(): result = lax.all_gather(both, axis, axis=dim, tiled=True)  53.2 us
    and x1, other arithmetic, shards(): picked = jnp.take(flat_rows, columns, axis=1)  35.8 us
    all_to_all x1, waiting for transfers between devices, sent_and_summed(): lax.all_to_all(pieces, axis, split_axis=0, concat_axis=0, tiled=True)  34.1 us
    all_to_all x2, starting transfers between devices, sent_to_all(): return lax.all_to_all(copies, axis, split_axis=0, concat_axis=0, tiled=True)  18.3 us
    gather x1, local copies, waits for them, and re-layouts, shards(): picked = jnp.take(flat_rows, columns, axis=1)  11.1 us
    gather x58, other arithmetic, shards(): slot_of[row_index // slice_rows] * slice_rows + row_index % slice_rows  9.84 us
    scatter x1, local copies, waits for them, and re-layouts, shards(): positioned = (qkv_zero, placed_zero)[1].at[columns].set(portions[1])  8.83 us
    all_to_all x2, waiting for transfers between devices, sent_to_all(): return lax.all_to_all(copies, axis, split_axis=0, concat_axis=0, tiled=True)  7.94 us
  transfers between devices with their start and end apart: 4, of which 3 were waited for; matrix products, arithmetic and copies ran while one was open for 30% of the time, Pallas kernels for 0%

commit v1 on v0

v1 whole, which is shorter than its diff:
```python
import functools
import math

import jax
import jax.numpy as jnp
from jax import lax
from jax.experimental import pallas as pl
from jax.experimental.pallas import tpu as pltpu
from jax.sharding import Mesh, PartitionSpec as P

GROUP = ("y", "zh", "core")
TENSOR = ("zl", "x")
NY, NZH, NCORE, NZL, NX = 8, 4, 2, 4, 4
NT = (((1,), (1,)), ((), ()))


def to_all(x, axis):
    copies = jnp.broadcast_to(x, (lax.axis_size(axis), *x.shape))
    return lax.all_to_all(copies, axis, split_axis=0, concat_axis=0, tiled=True)


def shifted(x, by):
    return lax.ppermute(x, "y", [(i, (i + by) % NY) for i in range(NY)])


def around_y(x):
    up = down = x
    found = [x]
    for step in range(NY // 2):
        up = shifted(up, 1)
        found.append(up)
        if step < NY // 2 - 1:
            down = shifted(down, -1)
            found.append(down)
    return jnp.concatenate(found, axis=0)


def norm_kernel(x_ref, mod_ref, o_ref):
    rows, width = x_ref.shape
    block = 32

    @pl.loop(0, rows // block)
    def _(i):
        here = pl.ds(pl.multiple_of(i * block, block), block)
        x = x_ref[here, :].astype(jnp.float32)
        centred = x - jnp.sum(x, axis=1, keepdims=True) / width
        variance = jnp.sum(centred * centred, axis=1, keepdims=True) / width
        normed = centred * lax.rsqrt(variance + 1e-06)
        o_ref[here, :] = (normed * (1.0 + mod_ref[1:2, :]) + mod_ref[0:1, :]).astype(jnp.bfloat16)


def normalised(tokens, mod):
    rows, width = tokens.shape
    vmem = pl.BlockSpec(memory_space=pltpu.VMEM)
    return pl.pallas_call(
        norm_kernel,
        out_shape=jax.ShapeDtypeStruct((rows, width), jnp.bfloat16),
        in_specs=[vmem, vmem],
        out_specs=vmem,
        compiler_params=pltpu.CompilerParams(vmem_limit_bytes=16 * 1024 * 1024),
        cost_estimate=pl.CostEstimate(
            flops=12 * rows * width, bytes_accessed=4 * rows * width, transcendentals=rows
        ),
    )(tokens, mod)


def head_kernel(at_ref, side_ref, x_ref, own_ref, other_ref, o_ref, w_ref):
    slices, rows = at_ref.shape[0], own_ref.shape[1]
    seq, width = x_ref.shape
    hd = own_ref.shape[2] // 4

    @pl.loop(0, slices)
    def _(s):
        here = pl.ds(pl.multiple_of(s * rows, rows), rows)

        @pl.when(side_ref[s] == 0)
        def _():
            w_ref[here, :] = own_ref[at_ref[s]]

        @pl.when(side_ref[s] != 0)
        def _():
            w_ref[here, :] = other_ref[at_ref[s]]

    qkv = jnp.dot(x_ref[...], w_ref[:, : 3 * hd], preferred_element_type=jnp.float32)
    qkv = qkv.astype(jnp.bfloat16)
    q, k, v = qkv[:, :hd], qkv[:, hd : 2 * hd], qkv[:, 2 * hd :]
    scores = lax.dot_general(q, k, NT, preferred_element_type=jnp.float32) / math.sqrt(hd)
    expo = jnp.exp(scores - jnp.max(scores, axis=1, keepdims=True))
    probs = (expo / jnp.sum(expo, axis=1, keepdims=True)).astype(jnp.bfloat16)
    attended = jnp.dot(probs, v, preferred_element_type=jnp.float32).astype(jnp.bfloat16)
    step = 512
    for at in range(0, width, step):
        w_out = w_ref[at : at + step, 3 * hd :]
        term = lax.dot_general(attended, w_out, NT, preferred_element_type=jnp.float32)
        term = term.astype(jnp.bfloat16).reshape(NZL, NX, seq // (NZL * NX), step)
        for x in range(NX):
            o_ref[x, :, :, at : at + step] = term[:, x]


def head_term(tokens, own, other, at, side):
    seq, width = tokens.shape
    smem = pl.BlockSpec(memory_space=pltpu.SMEM)
    vmem = pl.BlockSpec(memory_space=pltpu.VMEM)
    hd = own.shape[2] // 4
    return pl.pallas_call(
        head_kernel,
        out_shape=jax.ShapeDtypeStruct(
            (NX, NZL, seq // (NX * NZL), width), jnp.bfloat16
        ),
        in_specs=[smem, smem, vmem, vmem, vmem],
        out_specs=vmem,
        scratch_shapes=[pltpu.VMEM((width, own.shape[2]), jnp.bfloat16)],
        compiler_params=pltpu.CompilerParams(vmem_limit_bytes=48 * 1024 * 1024),
        cost_estimate=pl.CostEstimate(
            flops=8 * seq * width * hd, bytes_accessed=8 * seq * width, transcendentals=seq * seq
        ),
    )(at, side, tokens, own, other)


def shards(latents, stored_sample, timestep, owner_map, mod_table, qkv_weight, out_weight):
    samples, tok_local, width = latents.shape
    step_count = mod_table.shape[0]
    seq_len = tok_local * NZL * NX
    t = timestep[0]
    mod = lax.dynamic_index_in_dim(mod_table, t, 0, keepdims=False)

    weights = jnp.concatenate([qkv_weight, out_weight.T], axis=1)
    plane = lax.all_gather(weights, "zh")
    sent, plane = lax.optimization_barrier((latents[0], plane))
    tokens = to_all(sent, TENSOR).reshape(seq_len, width)
    own = around_y(plane)
    other = lax.ppermute(own, "core", [(0, 1), (1, 0)])

    far = (owner_map // (NZH * NCORE) - lax.axis_index("y")) % NY
    place = jnp.array([0, 2, 4, 6, 7, 5, 3, 1], jnp.int32)
    place_of = jnp.sum(
        jnp.where(far[:, None] == jnp.arange(NY)[None, :], place[None, :], 0), axis=1
    )
    at = (place_of * NZH + (owner_map // NCORE) % NZH).astype(jnp.int32)
    side = (owner_map % NCORE != lax.axis_index("core")).astype(jnp.int32)

    modulated = normalised(tokens, mod)
    terms = head_term(modulated, own, other, at, side)
    some = lax.all_to_all(terms, "x", split_axis=0, concat_axis=0, tiled=True)
    some = some.astype(jnp.float32).sum(axis=0).astype(jnp.bfloat16)
    parts = lax.all_to_all(some, "zl", split_axis=0, concat_axis=0, tiled=True)
    proj = parts.astype(jnp.float32).sum(axis=0)

    latent_f = latents[0].astype(jnp.float32)
    hidden = latent_f + mod[2:3] * proj
    time_float = t.astype(jnp.float32)
    step_size = (time_float + 1.0) / step_count
    mean = latent_f - step_size * hidden
    sigma = 0.3 + 0.1 * time_float
    residual = stored_sample[0].astype(jnp.float32) - mean
    total = to_all(jnp.sum(residual * residual), TENSOR).sum()
    log_prob = (
        -total / (2.0 * sigma * sigma * seq_len * width)
        - jnp.log(sigma)
        - 0.5 * math.log(2.0 * math.pi)
    )
    return (mean.astype(jnp.bfloat16)[None], log_prob[None])


def solution(mesh):
    fine = Mesh(mesh.devices.reshape(NY, NZH, NCORE, NZL, NX), GROUP + TENSOR)
    in_specs = (
        P(GROUP, TENSOR, None),
        P(GROUP, TENSOR, None),
        P(GROUP),
        P(),
        P(),
        P(GROUP, TENSOR),
        P(TENSOR, GROUP),
    )
    out_specs = (P(GROUP, TENSOR, None), P(GROUP))
    return jax.shard_map(shards, mesh=fine, in_specs=in_specs, out_specs=out_specs, check_vma=False)
```

time: 221 us -> 147 us (0.67)
  the two profiles are of different devices: /device:TPU:56 before, /device:TPU:32 now
where the time goes in v1:
time: 147 us; the launch traced here: 146 us
  blocking collectives  56.4 us (38%)
  starting transfers between devices  40.9 us (28%)
  waiting for transfers between devices  29.2 us (20%)
  Pallas kernels  7.35 us (5%)
  local copies, waits for them, and re-layouts  4.63 us (3%)
  other arithmetic  4.08 us (3%)
  between operations  3.45 us (2%)
    all_gather x1, blocking collectives, shards(): plane = lax.all_gather(weights, 'zh')  30.9 us
    all_to_all x1, blocking collectives, shards(): some = lax.all_to_all(terms, 'x', split_axis=0, concat_axis=0, tiled=True)  25.5 us
    ppermute x7, starting transfers between devices, shifted(): return lax.ppermute(x, 'y', [(i, (i + by) % NY) for i in range(NY)])  23 us
    all_to_all x2, starting transfers between devices, to_all(): return lax.all_to_all(copies, axis, split_axis=0, concat_axis=0, tiled=True)  11.3 us
    ppermute x7, waiting for transfers between devices, shifted(): return lax.ppermute(x, 'y', [(i, (i + by) % NY) for i in range(NY)])  11.1 us
    all_to_all x1, waiting for transfers between devices, shards(): parts = lax.all_to_all(some, 'zl', split_axis=0, concat_axis=0, tiled=True)  10.5 us
    all_to_all x2, waiting for transfers between devices, to_all(): return lax.all_to_all(copies, axis, split_axis=0, concat_axis=0, tiled=True)  7.24 us
    pallas_call x1, Pallas kernels, head_term(): pl.pallas_call(head_kernel, out_shape=jax.ShapeDtypeStruct((NX, NZL, seq...  5.08 us
  transfers between devices with their start and end apart: 11, of which 7 were waited for; matrix products, arithmetic and copies ran while one was open for 1% of the time, Pallas kernels for 2%

profile of v1, /device:TPU:32, one launch (start us, length us, event | category | flops | bytes accessed | tf_op | source)
XLA Modules:
  0.0 146.0 jit_solution(4256302372725242823)
XLA Ops:
  0.6 0.0 copy-start
  0.6 0.8 pad_maximum_fusion
  1.5 30.9 %all-gather = bf16[192,512]{1,0:T(8,128)(2,1)} all-gather(bf16[48,512]{1,0:T(8,128)(2,1)S(1)} %pad_maximum_fusion), channel_id=2, replica_groups=mesh['y'=8,'zh'=4,'core'=2,'zl'=4,'x'=4] {'zh'}, dimensions={0}, use_global_device_ids=true | all-gather | bytes 245760 | tf_op jit(solution)/shard_map/all_gather | solution.py:128
  32.3 2.2 %broadcast_in_dim.27 = bf16[16,16,3072]{2,1,0:T(8,128)(2,1)} broadcast(bf16[16,3072]{1,0:T(8,128)(2,1)} %bitcast.24), dimensions={1,2} | broadcast | bytes 1671168 | tf_op jit(solution)/shard_map/broadcast_in_dim | solution.py:18
  34.6 7.8 %all-to-all-start = ((bf16[16,16,3072]{2,1,0:T(8,128)(2,1)}), bf16[16,16,3072]{2,1,0:T(8,128)(2,1)S(1)}, u32[]{:S(2)}, u32[]{:S(2)}) async-start(bf16[16,16,3072]{2,1,0:T(8,128)(2,1)} %broadcast_in_dim.27), calls=%async_computation | async-start | bytes 3145728 | tf_op jit(solution)/shard_map/all_to_all | solution.py:19
  42.4 0.0 copy-start.3
  42.4 0.0 copy-start.4
  42.5 2.6 %collective-permute-start = (bf16[4,48,512]{2,1,0:T(8,128)(2,1)}, bf16[4,48,512]{2,1,0:T(8,128)(2,1)S(1)}, u32[]{:S(2)}, u32[]{:S(2)}) collective-permute-start(bf16[4,48,512]{2,1,0:T(8,128)(2,1)} %bitcast.4), channel_id=1, source_target_pairs={{0,128},{128,256},{256,384},{384,512},{512,640},{640,768},{768,896... | collective-permute-start | bytes 589832 | tf_op jit(solution)/shard_map/ppermute | solution.py:23
  45.0 4.5 %collective-permute-start.1 = (bf16[4,48,512]{2,1,0:T(8,128)(2,1)}, bf16[4,48,512]{2,1,0:T(8,128)(2,1)S(1)}, u32[]{:S(2)}, u32[]{:S(2)}) collective-permute-start(bf16[4,48,512]{2,1,0:T(8,128)(2,1)} %bitcast.4), channel_id=1, source_target_pairs={{0,896},{128,0},{256,128},{384,256},{512,384},{640,512},{768,640},... | collective-permute-start | bytes 589832 | tf_op jit(solution)/shard_map/ppermute | solution.py:23
  49.5 1.0 constant_dynamic-update-slice_fusion.7
  50.5 1.0 collective-permute-done
  51.4 1.9 %collective-permute-start.2 = (bf16[4,48,512]{2,1,0:T(8,128)(2,1)S(1)}, bf16[4,48,512]{2,1,0:T(8,128)(2,1)S(1)}, u32[]{:S(2)}, u32[]{:S(2)}) collective-permute-start(bf16[4,48,512]{2,1,0:T(8,128)(2,1)S(1)} %collective-permute-done), channel_id=1, source_target_pairs={{0,128},{128,256},{256,384},{384,512},{512,640},{640,768},{768,896... | collective-permute-start | bytes 589832 | tf_op jit(solution)/shard_map/ppermute | solution.py:23
  53.4 0.0 collective-permute-done.1
  53.4 5.1 %collective-permute-start.3 = (bf16[4,48,512]{2,1,0:T(8,128)(2,1)S(1)}, bf16[4,48,512]{2,1,0:T(8,128)(2,1)S(1)}, u32[]{:S(2)}, u32[]{:S(2)}) collective-permute-start(bf16[4,48,512]{2,1,0:T(8,128)(2,1)S(1)} %collective-permute-done.1), channel_id=1, source_target_pairs={{0,896},{128,0},{256,128},{384,256},{512,384},{640,512},{768,640},... | collective-permute-start | bytes 589832 | tf_op jit(solution)/shard_map/ppermute | solution.py:23
  58.5 1.6 %collective-permute-done.2 = bf16[4,48,512]{2,1,0:T(8,128)(2,1)S(1)} collective-permute-done((bf16[4,48,512]{2,1,0:T(8,128)(2,1)S(1)}, bf16[4,48,512]{2,1,0:T(8,128)(2,1)S(1)}, u32[]{:S(2)}, u32[]{:S(2)}) %collective-permute-start.2) | collective-permute-done | bytes 196640 | tf_op jit(solution)/shard_map/ppermute | solution.py:23
  60.2 1.9 %collective-permute-start.4 = (bf16[4,48,512]{2,1,0:T(8,128)(2,1)S(1)}, bf16[4,48,512]{2,1,0:T(8,128)(2,1)S(1)}, u32[]{:S(2)}, u32[]{:S(2)}) collective-permute-start(bf16[4,48,512]{2,1,0:T(8,128)(2,1)S(1)} %collective-permute-done.2), channel_id=1, source_target_pairs={{0,128},{128,256},{256,384},{384,512},{512,640},{640,768},{768,896... | collective-permute-start | bytes 589832 | tf_op jit(solution)/shard_map/ppermute | solution.py:23
  62.1 0.0 collective-permute-done.3
  62.1 5.1 %collective-permute-start.5 = (bf16[4,48,512]{2,1,0:T(8,128)(2,1)S(1)}, bf16[4,48,512]{2,1,0:T(8,128)(2,1)S(1)}, u32[]{:S(2)}, u32[]{:S(2)}) collective-permute-start(bf16[4,48,512]{2,1,0:T(8,128)(2,1)S(1)} %collective-permute-done.3), channel_id=1, source_target_pairs={{0,896},{128,0},{256,128},{384,256},{512,384},{640,512},{768,640},... | collective-permute-start | bytes 589832 | tf_op jit(solution)/shard_map/ppermute | solution.py:23
  67.3 1.6 %collective-permute-done.4 = bf16[4,48,512]{2,1,0:T(8,128)(2,1)S(1)} collective-permute-done((bf16[4,48,512]{2,1,0:T(8,128)(2,1)S(1)}, bf16[4,48,512]{2,1,0:T(8,128)(2,1)S(1)}, u32[]{:S(2)}, u32[]{:S(2)}) %collective-permute-start.4) | collective-permute-done | bytes 196640 | tf_op jit(solution)/shard_map/ppermute | solution.py:23
  69.0 1.9 %collective-permute-start.6 = (bf16[4,48,512]{2,1,0:T(8,128)(2,1)S(1)}, bf16[4,48,512]{2,1,0:T(8,128)(2,1)S(1)}, u32[]{:S(2)}, u32[]{:S(2)}) collective-permute-start(bf16[4,48,512]{2,1,0:T(8,128)(2,1)S(1)} %collective-permute-done.4), channel_id=1, source_target_pairs={{0,128},{128,256},{256,384},{384,512},{512,640},{640,768},{768,896... | collective-permute-start | bytes 589832 | tf_op jit(solution)/shard_map/ppermute | solution.py:23
  70.9 0.0 collective-permute-done.5
  70.9 6.8 %collective-permute-done.6 = bf16[4,48,512]{2,1,0:T(8,128)(2,1)S(1)} collective-permute-done((bf16[4,48,512]{2,1,0:T(8,128)(2,1)S(1)}, bf16[4,48,512]{2,1,0:T(8,128)(2,1)S(1)}, u32[]{:S(2)}, u32[]{:S(2)}) %collective-permute-start.6) | collective-permute-done | bytes 196640 | tf_op jit(solution)/shard_map/ppermute | solution.py:23
  77.7 1.9 %collective-permute-start.7 = (bf16[32,48,512]{2,1,0:T(8,128)(2,1)S(1)}, bf16[32,48,512]{2,1,0:T(8,128)(2,1)}, u32[]{:S(2)}, u32[]{:S(2)}) collective-permute-start(bf16[32,48,512]{2,1,0:T(8,128)(2,1)S(1)} %constant_dynamic-update-slice_fusion.own_ref), channel_id=1, source_target_pairs={{0,16},{16,0},{1,17},{17,1},{2,18},{18,2},{3,19},{19,3},{4,20},{20... | collective-permute-start | bytes 4718600 | tf_op jit(solution)/shard_map/ppermute | solution.py:132
  80.3 0.0 copy-done
  80.4 0.0 copy-done.3
  80.4 0.0 copy-done.4
  80.4 0.1 select_reduce_fusion
  80.6 0.0 all-to-all-done
  80.6 2.3 %shard_map.95.x_ref = bf16[256,3072]{1,0:T(8,128)(2,1)S(1)} custom-call(bf16[256,3072]{1,0:T(8,128)(2,1)S(1)} %bitcast.22, f32[3,3072]{1,0:T(4,128)S(1)} %bitcast.23), custom_call_target="tpu_custom_call" | custom-call | flops 9437184 | bytes 3145728 | tf_op jit(solution)/shard_map/pallas_call | solution.py:55
  82.8 0.3 collective-permute-done.7.other_ref
  83.2 5.1 %shard_map.96 = bf16[4,4,16,3072]{3,2,1,0:T(8,128)(2,1)S(1)} custom-call(s32[64]{0:T(128)S(1)} %fusion.6.at_ref, s32[64]{0:T(128)S(1)} %compare_convert_fusion.side_ref, bf16[256,3072]{1,0:T(8,128)(2,1)S(1)} %shard_map.95.x_ref, bf16[32,48,512]{2,1,0:T(8,128)(2,1)S(1)} %constant_dynamic-update-slice_fusion.own_ref, ...), custom_call_target="tpu_custom_call" | custom-call | flops 805306368 | bytes 6291456 | tf_op jit(solution)/shard_map/pallas_call | solution.py:105
  88.3 25.5 %all_to_all.21 = bf16[4,4,16,3072]{3,2,1,0:T(8,128)(2,1)S(1)} all-to-all(bf16[4,4,16,3072]{3,2,1,0:T(8,128)(2,1)S(1)} %shard_map.96), channel_id=1, replica_groups=mesh['y'=8,'zh'=4,'core'=2,'zl'=4,'x'=4] {'x'}, dimensions={0} | all-to-all | bytes 3145728 | tf_op jit(solution)/shard_map/all_to_all | solution.py:144
  113.8 0.0 copy-start.1
  113.8 0.0 copy-start.2
  113.8 1.1 reduce_sum.51
  114.9 4.6 %all-to-all-start.2 = ((bf16[4,16,3072]{2,1,0:T(8,128)(2,1)}), bf16[4,16,3072]{2,1,0:T(8,128)(2,1)S(1)}, u32[]{:S(2)}, u32[]{:S(2)}) async-start(bf16[4,16,3072]{2,1,0:T(8,128)(2,1)} %reduce_sum.51), calls=%async_computation.2 | async-start | bytes 786432 | tf_op jit(solution)/shard_map/all_to_all | solution.py:146
  119.6 10.5 %all-to-all-done.2 = bf16[4,16,3072]{2,1,0:T(8,128)(2,1)S(1)} async-done(((bf16[4,16,3072]{2,1,0:T(8,128)(2,1)}), bf16[4,16,3072]{2,1,0:T(8,128)(2,1)S(1)}, u32[]{:S(2)}, u32[]{:S(2)}) %all-to-all-start.2) | async-done | bytes 393248 | tf_op jit(solution)/shard_map/all_to_all | solution.py:146
  130.2 0.0 copy-done.1
  130.2 0.0 copy-done.2
  130.2 0.7 fusion.5
  130.9 1.2 broadcast_in_dim.28
  132.1 3.4 %all-to-all-start.3 = ((f32[16,1,1]{2,1,0:T(1,128)}), f32[16,1,1]{2,1,0:T(1,128)S(1)}, u32[]{:S(2)}, u32[]{:S(2)}) async-start(f32[16,1,1]{2,1,0:T(1,128)} %broadcast_in_dim.28), calls=%async_computation.3 | async-start | bytes 16384 | tf_op jit(solution)/shard_map/all_to_all | solution.py:19
  135.6 0.7 fusion.1
  136.3 7.2 %all-to-all-done.3 = f32[16,1,1]{2,1,0:T(1,128)S(1)} async-done(((f32[16,1,1]{2,1,0:T(1,128)}), f32[16,1,1]{2,1,0:T(1,128)S(1)}, u32[]{:S(2)}, u32[]{:S(2)}) %all-to-all-start.3) | async-done | bytes 96 | tf_op jit(solution)/shard_map/all_to_all | solution.py:19
  143.5 0.6 reduce_sum.55
  (14 shorter events, 0.3 us)
Async XLA Ops:
  0.6 79.7 %copy-start = (f32[8,3,3072]{2,0,1:T(8,128)S(1)}, f32[8,3,3072]{2,0,1:T(8,128)}, u32[]{:S(2)}) copy-start(f32[8,3,3072]{2,0,1:T(8,128)} %param.12) | copy-start | bytes 884740
  34.6 46.0 %all-to-all-start = ((bf16[16,16,3072]{2,1,0:T(8,128)(2,1)}), bf16[16,16,3072]{2,1,0:T(8,128)(2,1)S(1)}, u32[]{:S(2)}, u32[]{:S(2)}) async-start(bf16[16,16,3072]{2,1,0:T(8,128)(2,1)} %broadcast_in_dim.27), calls=%async_computation | async-start | bytes 3145728 | tf_op jit(solution)/shard_map/all_to_all | solution.py:19
  42.4 38.0 %copy-start.3 = (s32[64]{0:T(128)S(1)}, s32[64]{0:T(128)}, u32[]{:S(2)}) copy-start(s32[64]{0:T(128)} %param.11) | copy-start | bytes 772
  42.4 38.0 %copy-start.4 = (s32[8]{0:T(128)S(1)}, s32[8]{0:T(128)}, u32[]{:S(2)}) copy-start(s32[8]{0:T(128)} %constant.97.clone) | copy-start | bytes 100
  42.5 9.0 %collective-permute-start = (bf16[4,48,512]{2,1,0:T(8,128)(2,1)}, bf16[4,48,512]{2,1,0:T(8,128)(2,1)S(1)}, u32[]{:S(2)}, u32[]{:S(2)}) collective-permute-start(bf16[4,48,512]{2,1,0:T(8,128)(2,1)} %bitcast.4), channel_id=1, source_target_pairs={{0,128},{128,256},{256,384},{384,512},{512,640},{640,768},{768,896... | collective-permute-start | bytes 589832 | tf_op jit(solution)/shard_map/ppermute | solution.py:23
  45.0 8.3 %collective-permute-start.1 = (bf16[4,48,512]{2,1,0:T(8,128)(2,1)}, bf16[4,48,512]{2,1,0:T(8,128)(2,1)S(1)}, u32[]{:S(2)}, u32[]{:S(2)}) collective-permute-start(bf16[4,48,512]{2,1,0:T(8,128)(2,1)} %bitcast.4), channel_id=1, source_target_pairs={{0,896},{128,0},{256,128},{384,256},{512,384},{640,512},{768,640},... | collective-permute-start | bytes 589832 | tf_op jit(solution)/shard_map/ppermute | solution.py:23
  51.4 8.8 %collective-permute-start.2 = (bf16[4,48,512]{2,1,0:T(8,128)(2,1)S(1)}, bf16[4,48,512]{2,1,0:T(8,128)(2,1)S(1)}, u32[]{:S(2)}, u32[]{:S(2)}) collective-permute-start(bf16[4,48,512]{2,1,0:T(8,128)(2,1)S(1)} %collective-permute-done), channel_id=1, source_target_pairs={{0,128},{128,256},{256,384},{384,512},{512,640},{640,768},{768,896... | collective-permute-start | bytes 589832 | tf_op jit(solution)/shard_map/ppermute | solution.py:23
  53.4 8.8 %collective-permute-start.3 = (bf16[4,48,512]{2,1,0:T(8,128)(2,1)S(1)}, bf16[4,48,512]{2,1,0:T(8,128)(2,1)S(1)}, u32[]{:S(2)}, u32[]{:S(2)}) collective-permute-start(bf16[4,48,512]{2,1,0:T(8,128)(2,1)S(1)} %collective-permute-done.1), channel_id=1, source_target_pairs={{0,896},{128,0},{256,128},{384,256},{512,384},{640,512},{768,640},... | collective-permute-start | bytes 589832 | tf_op jit(solution)/shard_map/ppermute | solution.py:23
  60.2 8.8 %collective-permute-start.4 = (bf16[4,48,512]{2,1,0:T(8,128)(2,1)S(1)}, bf16[4,48,512]{2,1,0:T(8,128)(2,1)S(1)}, u32[]{:S(2)}, u32[]{:S(2)}) collective-permute-start(bf16[4,48,512]{2,1,0:T(8,128)(2,1)S(1)} %collective-permute-done.2), channel_id=1, source_target_pairs={{0,128},{128,256},{256,384},{384,512},{512,640},{640,768},{768,896... | collective-permute-start | bytes 589832 | tf_op jit(solution)/shard_map/ppermute | solution.py:23
  62.1 8.8 %collective-permute-start.5 = (bf16[4,48,512]{2,1,0:T(8,128)(2,1)S(1)}, bf16[4,48,512]{2,1,0:T(8,128)(2,1)S(1)}, u32[]{:S(2)}, u32[]{:S(2)}) collective-permute-start(bf16[4,48,512]{2,1,0:T(8,128)(2,1)S(1)} %collective-permute-done.3), channel_id=1, source_target_pairs={{0,896},{128,0},{256,128},{384,256},{512,384},{640,512},{768,640},... | collective-permute-start | bytes 589832 | tf_op jit(solution)/shard_map/ppermute | solution.py:23
  69.0 8.8 %collective-permute-start.6 = (bf16[4,48,512]{2,1,0:T(8,128)(2,1)S(1)}, bf16[4,48,512]{2,1,0:T(8,128)(2,1)S(1)}, u32[]{:S(2)}, u32[]{:S(2)}) collective-permute-start(bf16[4,48,512]{2,1,0:T(8,128)(2,1)S(1)} %collective-permute-done.4), channel_id=1, source_target_pairs={{0,128},{128,256},{256,384},{384,512},{512,640},{640,768},{768,896... | collective-permute-start | bytes 589832 | tf_op jit(solution)/shard_map/ppermute | solution.py:23
  77.7 5.4 %collective-permute-start.7 = (bf16[32,48,512]{2,1,0:T(8,128)(2,1)S(1)}, bf16[32,48,512]{2,1,0:T(8,128)(2,1)}, u32[]{:S(2)}, u32[]{:S(2)}) collective-permute-start(bf16[32,48,512]{2,1,0:T(8,128)(2,1)S(1)} %constant_dynamic-update-slice_fusion.own_ref), channel_id=1, source_target_pairs={{0,16},{16,0},{1,17},{17,1},{2,18},{18,2},{3,19},{19,3},{4,20},{20... | collective-permute-start | bytes 4718600 | tf_op jit(solution)/shard_map/ppermute | solution.py:132
  113.8 16.4 %copy-start.1 = (bf16[1,16,3072]{2,1,0:T(8,128)(2,1)S(1)}, bf16[1,16,3072]{2,1,0:T(8,128)(2,1)}, u32[]{:S(2)}) copy-start(bf16[1,16,3072]{2,1,0:T(8,128)(2,1)} %param.8) | copy-start | bytes 294916
  113.8 16.4 %copy-start.2 = (bf16[1,16,3072]{2,1,0:T(8,128)(2,1)S(1)}, bf16[1,16,3072]{2,1,0:T(8,128)(2,1)}, u32[]{:S(2)}) copy-start(bf16[1,16,3072]{2,1,0:T(8,128)(2,1)} %param.9) | copy-start | bytes 294916
  114.9 15.2 %all-to-all-start.2 = ((bf16[4,16,3072]{2,1,0:T(8,128)(2,1)}), bf16[4,16,3072]{2,1,0:T(8,128)(2,1)S(1)}, u32[]{:S(2)}, u32[]{:S(2)}) async-start(bf16[4,16,3072]{2,1,0:T(8,128)(2,1)} %reduce_sum.51), calls=%async_computation.2 | async-start | bytes 786432 | tf_op jit(solution)/shard_map/all_to_all | solution.py:146
  132.1 11.4 %all-to-all-start.3 = ((f32[16,1,1]{2,1,0:T(1,128)}), f32[16,1,1]{2,1,0:T(1,128)S(1)}, u32[]{:S(2)}, u32[]{:S(2)}) async-start(f32[16,1,1]{2,1,0:T(1,128)} %broadcast_in_dim.28), calls=%async_computation.3 | async-start | bytes 16384 | tf_op jit(solution)/shard_map/all_to_all | solution.py:19

commit v2 on v1

v2 whole, which is shorter than its diff:
```python
import math

import jax
import jax.numpy as jnp
from jax import lax
from jax.experimental import pallas as pl
from jax.experimental.pallas import tpu as pltpu
from jax.sharding import Mesh, PartitionSpec as P


GROUP = ("y", "zh", "core")
TENSOR = ("zl", "x")
NY, NZH, NCORE, NZL, NX = 8, 4, 2, 4, 4
NT = (((1,), (1,)), ((), ()))


def to_all(x, axis):
    copies = jnp.broadcast_to(x, (lax.axis_size(axis), *x.shape))
    return lax.all_to_all(copies, axis, split_axis=0, concat_axis=0, tiled=True)


def shifted(x, by):
    return lax.ppermute(x, "y", [(i, (i + by) % NY) for i in range(NY)])


def swapped(x):
    return lax.ppermute(x, "core", [(0, 1), (1, 0)])


PLACE = (0, 2, 6, 5, 3, 7, 4, 1)


def around_y(x):
    below = shifted(x, 1)
    above = shifted(x, -1)
    across = shifted(x, 4)
    near = jnp.concatenate([x, below, above, across], axis=0)
    up = shifted(jnp.concatenate([below, across], axis=0), 1)
    down = shifted(jnp.concatenate([above, across], axis=0), -1)
    return near, jnp.concatenate([up, down], axis=0)


def norm_kernel(x_ref, mod_ref, o_ref):
    rows, width = x_ref.shape
    block = 32

    @pl.loop(0, rows // block)
    def _(i):
        here = pl.ds(pl.multiple_of(i * block, block), block)
        x = x_ref[here, :].astype(jnp.float32)
        centred = x - jnp.sum(x, axis=1, keepdims=True) / width
        variance = jnp.sum(centred * centred, axis=1, keepdims=True) / width
        normed = centred * lax.rsqrt(variance + 1e-06)
        o_ref[here, :] = (normed * (1.0 + mod_ref[1:2, :]) + mod_ref[0:1, :]).astype(jnp.bfloat16)


def normalised(tokens, mod):
    rows, width = tokens.shape
    vmem = pl.BlockSpec(memory_space=pltpu.VMEM)
    return pl.pallas_call(
        norm_kernel,
        out_shape=jax.ShapeDtypeStruct((rows, width), jnp.bfloat16),
        in_specs=[vmem, vmem],
        out_specs=vmem,
        compiler_params=pltpu.CompilerParams(vmem_limit_bytes=16 * 1024 * 1024),
        cost_estimate=pl.CostEstimate(
            flops=12 * rows * width, bytes_accessed=4 * rows * width, transcendentals=rows
        ),
    )(tokens, mod)


def head_kernel(at_ref, x_ref, own0, own1, other0, other1, o_ref, w_ref):
    slices, (count, rows, columns) = at_ref.shape[0], own0.shape
    width = x_ref.shape[1]
    hd = columns // 4

    @pl.loop(0, slices)
    def _(s):
        here = pl.ds(pl.multiple_of(s * rows, rows), rows)
        at = at_ref[s]
        for part, ref in enumerate((own0, own1, other0, other1)):

            @pl.when(at // count == part)
            def _():
                w_ref[here, :] = ref[at % count]

    qkv = jnp.dot(x_ref[...], w_ref[:, : 3 * hd], preferred_element_type=jnp.float32)
    qkv = qkv.astype(jnp.bfloat16)
    q, k, v = qkv[:, :hd], qkv[:, hd : 2 * hd], qkv[:, 2 * hd :]
    scores = lax.dot_general(q, k, NT, preferred_element_type=jnp.float32) / math.sqrt(hd)
    expo = jnp.exp(scores - jnp.max(scores, axis=1, keepdims=True))
    probs = (expo / jnp.sum(expo, axis=1, keepdims=True)).astype(jnp.bfloat16)
    attended = jnp.dot(probs, v, preferred_element_type=jnp.float32).astype(jnp.bfloat16)
    step = 512
    for c in range(0, width, step):
        w_out = w_ref[c : c + step, 3 * hd :]
        term = lax.dot_general(attended, w_out, NT, preferred_element_type=jnp.float32)
        o_ref[:, c : c + step] = term.astype(jnp.bfloat16)


def head_term(tokens, pieces, at):
    seq, width = tokens.shape
    smem = pl.BlockSpec(memory_space=pltpu.SMEM)
    vmem = pl.BlockSpec(memory_space=pltpu.VMEM)
    columns = pieces[0].shape[2]
    return pl.pallas_call(
        head_kernel,
        out_shape=jax.ShapeDtypeStruct((seq, width), jnp.bfloat16),
        in_specs=[smem] + [vmem] * 5,
        out_specs=vmem,
        scratch_shapes=[pltpu.VMEM((width, columns), jnp.bfloat16)],
        compiler_params=pltpu.CompilerParams(vmem_limit_bytes=40 * 1024 * 1024),
        cost_estimate=pl.CostEstimate(
            flops=2 * seq * width * columns,
            bytes_accessed=8 * seq * width,
            transcendentals=seq * seq,
        ),
    )(at, tokens, *pieces)


def mean_kernel(dt_ref, parts_ref, latent_ref, stored_ref, gate_ref, mean_ref, sum_ref):
    dt = dt_ref[0]
    devices, rows, width = parts_ref.shape
    step = 512
    squares = jnp.zeros((rows, step), jnp.float32)
    for c in range(0, width, step):
        here = slice(c, c + step)
        proj = parts_ref[0, :, here].astype(jnp.float32)
        for k in range(1, devices):
            proj = proj + parts_ref[k, :, here].astype(jnp.float32)
        latent = latent_ref[:, here].astype(jnp.float32)
        mean = latent - dt * (latent + gate_ref[:, here] * proj)
        mean_ref[:, here] = mean.astype(jnp.bfloat16)
        residual = stored_ref[:, here].astype(jnp.float32) - mean
        squares = squares + residual * residual
    total = jnp.sum(squares, axis=(0, 1), keepdims=True)
    sum_ref[...] = jnp.broadcast_to(total[None], sum_ref.shape)


def mean_and_squares(dt, parts, latent, stored, gate):
    devices, rows, width = parts.shape
    vmem = pl.BlockSpec(memory_space=pltpu.VMEM)
    return pl.pallas_call(
        mean_kernel,
        out_shape=(
            jax.ShapeDtypeStruct((rows, width), jnp.bfloat16),
            jax.ShapeDtypeStruct((devices, 1, 128), jnp.float32),
        ),
        in_specs=[pl.BlockSpec(memory_space=pltpu.SMEM)] + [vmem] * 4,
        out_specs=(vmem, vmem),
        compiler_params=pltpu.CompilerParams(vmem_limit_bytes=16 * 1024 * 1024),
        cost_estimate=pl.CostEstimate(
            flops=30 * rows * width, bytes_accessed=40 * rows * width, transcendentals=0
        ),
    )(dt, parts, latent, stored, gate)


def one_device(latents, stored_sample, timestep, owner_map, mod_table, qkv_weight, out_weight):
    _, tok_local, width = latents.shape
    step_count = mod_table.shape[0]
    seq_len = tok_local * NZL * NX
    t = timestep[0]
    time_float = t.astype(jnp.float32)
    mod = lax.dynamic_index_in_dim(mod_table, t, 0, keepdims=False)

    weights = jnp.concatenate([qkv_weight, out_weight.T], axis=1)
    plane = lax.all_gather(weights, "zh", tiled=False)
    sent, plane = lax.optimization_barrier((latents[0], plane))
    tokens = to_all(sent, TENSOR).reshape(seq_len, width)
    near, far = around_y(plane)
    pieces = (near, far, swapped(near), swapped(far))

    ahead = (owner_map // (NZH * NCORE) - lax.axis_index("y")) % NY
    place = jnp.zeros_like(ahead)
    for distance, where in enumerate(PLACE):
        place = jnp.where(ahead == distance, where, place)
    side = (owner_map % NCORE != lax.axis_index("core")).astype(jnp.int32)
    at = ((side * NY + place) * NZH + (owner_map // NCORE) % NZH).astype(jnp.int32)

    modulated = normalised(tokens, mod)
    terms = head_term(modulated, pieces, at)
    parts = lax.all_to_all(
        terms.reshape(NZL * NX, tok_local, width), TENSOR, split_axis=0, concat_axis=0, tiled=True
    )
    dt = (timestep.astype(jnp.float32) + 1.0) / step_count
    mean, squares = mean_and_squares(dt, parts, latents[0], stored_sample[0], mod[2:3])
    squares = lax.all_to_all(squares, TENSOR, split_axis=0, concat_axis=0, tiled=True)
    total = jnp.sum(squares[:, :, :1])
    sigma = 0.3 + 0.1 * time_float
    log_prob = (
        -total / (2.0 * sigma * sigma * seq_len * width)
        - jnp.log(sigma)
        - 0.5 * math.log(2.0 * math.pi)
    )
    return (mean[None], log_prob[None])


def solution(mesh):
    fine = Mesh(mesh.devices.reshape(NY, NZH, NCORE, NZL, NX), GROUP + TENSOR)
    in_specs = (
        P(GROUP, TENSOR, None),
        P(GROUP, TENSOR, None),
        P(GROUP),
        P(),
        P(),
        P(GROUP, TENSOR),
        P(TENSOR, GROUP),
    )
    out_specs = (P(GROUP, TENSOR, None), P(GROUP))
    return jax.shard_map(one_device, mesh=fine, in_specs=in_specs, out_specs=out_specs, check_vma=False)
```

time: 147 us -> 151 us (1.027)
  the two profiles are of different devices: /device:TPU:32 before, /device:TPU:56 now
where the time goes in v2:
time: 151 us
  waiting for transfers between devices  57.9 us (38%)
  starting transfers between devices  44.8 us (30%)
  blocking collectives  30.2 us (20%)
  Pallas kernels  10.3 us (7%)
  between operations  3.4 us (2%)
  local copies, waits for them, and re-layouts  2.45 us (2%)
  other arithmetic  1.54 us (1%)
    all_to_all x1, waiting for transfers between devices, one_device(): lax.all_to_all(terms.reshape(NZL * NX, tok_local, width), TENSOR, split_a...  34.2 us
    all_gather x1, blocking collectives, one_device(): plane = lax.all_gather(weights, 'zh', tiled=False)  30.2 us
    ppermute x5, starting transfers between devices, shifted(): return lax.ppermute(x, 'y', [(i, (i + by) % NY) for i in range(NY)])  17.2 us
    ppermute x5, waiting for transfers between devices, shifted(): return lax.ppermute(x, 'y', [(i, (i + by) % NY) for i in range(NY)])  15.8 us
    all_to_all x1, starting transfers between devices, one_device(): lax.all_to_all(squares, TENSOR, split_axis=0, concat_axis=0, tiled=True)  8.57 us
    all_to_all x1, waiting for transfers between devices, one_device(): lax.all_to_all(squares, TENSOR, split_axis=0, concat_axis=0, tiled=True)  7.88 us
    all_to_all x1, starting transfers between devices, one_device(): lax.all_to_all(terms.reshape(NZL * NX, tok_local, width), TENSOR, split_a...  7.62 us
    all_to_all x1, starting transfers between devices, to_all(): return lax.all_to_all(copies, axis, split_axis=0, concat_axis=0, tiled=True)  7.59 us
  transfers between devices with their start and end apart: 10, of which 5 were waited for; matrix products, arithmetic and copies ran while one was open for 0% of the time, Pallas kernels for 2%

profile of v2, /device:TPU:56, one launch (start us, length us, event | category | flops | bytes accessed | tf_op | source)
XLA Modules:
  0.0 150.7 jit_solution(14501922889761902780)
XLA Ops:
  0.6 0.0 copy-start
  0.6 0.8 pad_maximum_fusion.2
  1.5 30.2 %all-gather = bf16[192,512]{1,0:T(8,128)(2,1)S(1)} all-gather(bf16[48,512]{1,0:T(8,128)(2,1)S(1)} %pad_maximum_fusion.2), channel_id=2, replica_groups=mesh['y'=8,'zh'=4,'core'=2,'zl'=4,'x'=4] {'zh'}, dimensions={0}, use_global_device_ids=true | all-gather | bytes 245760 | tf_op jit(solution)/shard_map/all_gather | solution.py:167
  31.7 2.2 %broadcast_in_dim.21 = bf16[16,16,3072]{2,1,0:T(8,128)(2,1)} broadcast(bf16[16,3072]{1,0:T(8,128)(2,1)} %bitcast.19), dimensions={1,2} | broadcast | bytes 1671168 | tf_op jit(solution)/shard_map/broadcast_in_dim | solution.py:18
  34.0 7.6 %all-to-all-start = ((bf16[16,16,3072]{2,1,0:T(8,128)(2,1)}), bf16[16,16,3072]{2,1,0:T(8,128)(2,1)S(1)}, u32[]{:S(2)}, u32[]{:S(2)}) async-start(bf16[16,16,3072]{2,1,0:T(8,128)(2,1)} %broadcast_in_dim.21), calls=%async_computation | async-start | bytes 3145728 | tf_op jit(solution)/shard_map/all_to_all | solution.py:19
  41.6 1.9 %collective-permute-start = (bf16[4,48,512]{2,1,0:T(8,128)(2,1)S(1)}, bf16[4,48,512]{2,1,0:T(8,128)(2,1)S(1)}, u32[]{:S(2)}, u32[]{:S(2)}) collective-permute-start(bf16[4,48,512]{2,1,0:T(8,128)(2,1)S(1)} %bitcast.23), channel_id=1, source_target_pairs={{0,128},{128,256},{256,384},{384,512},{512,640},{640,768},{768,896... | collective-permute-start | bytes 589832 | tf_op jit(solution)/shard_map/ppermute | solution.py:23
  43.5 3.9 %collective-permute-start.1 = (bf16[4,48,512]{2,1,0:T(8,128)(2,1)S(1)}, bf16[4,48,512]{2,1,0:T(8,128)(2,1)S(1)}, u32[]{:S(2)}, u32[]{:S(2)}) collective-permute-start(bf16[4,48,512]{2,1,0:T(8,128)(2,1)S(1)} %bitcast.24), channel_id=1, source_target_pairs={{0,896},{128,0},{256,128},{384,256},{512,384},{640,512},{768,640},... | collective-permute-start | bytes 589832 | tf_op jit(solution)/shard_map/ppermute | solution.py:23
  47.4 5.5 %collective-permute-start.2 = (bf16[4,48,512]{2,1,0:T(8,128)(2,1)S(1)}, bf16[4,48,512]{2,1,0:T(8,128)(2,1)S(1)}, u32[]{:S(2)}, u32[]{:S(2)}) collective-permute-start(bf16[4,48,512]{2,1,0:T(8,128)(2,1)S(1)} %bitcast.25), channel_id=1, source_target_pairs={{0,512},{128,640},{256,768},{384,896},{512,0},{640,128},{768,256},... | collective-permute-start | bytes 589832 | tf_op jit(solution)/shard_map/ppermute | solution.py:23
  52.9 0.0 collective-permute-done
  52.9 0.0 collective-permute-done.1
  52.9 10.0 %collective-permute-done.2 = bf16[4,48,512]{2,1,0:T(8,128)(2,1)S(1)} collective-permute-done((bf16[4,48,512]{2,1,0:T(8,128)(2,1)S(1)}, bf16[4,48,512]{2,1,0:T(8,128)(2,1)S(1)}, u32[]{:S(2)}, u32[]{:S(2)}) %collective-permute-start.2) | collective-permute-done | bytes 196640 | tf_op jit(solution)/shard_map/ppermute | solution.py:23
  62.9 0.1 pad_maximum_fusion
  63.0 0.0 copy-start.3
  63.0 1.9 %collective-permute-start.3 = (bf16[8,48,512]{2,1,0:T(8,128)(2,1)S(1)}, bf16[8,48,512]{2,1,0:T(8,128)(2,1)S(1)}, u32[]{:S(2)}, u32[]{:S(2)}) collective-permute-start(bf16[8,48,512]{2,1,0:T(8,128)(2,1)S(1)} %get-tuple-element.11), channel_id=1, source_target_pairs={{0,128},{128,256},{256,384},{384,512},{512,640},{640,768},{768,896... | collective-permute-start | bytes 1179656 | tf_op jit(solution)/shard_map/ppermute | solution.py:23
  65.0 3.9 %collective-permute-start.4 = (bf16[8,48,512]{2,1,0:T(8,128)(2,1)S(1)}, bf16[8,48,512]{2,1,0:T(8,128)(2,1)S(1)}, u32[]{:S(2)}, u32[]{:S(2)}) collective-permute-start(bf16[8,48,512]{2,1,0:T(8,128)(2,1)S(1)} %get-tuple-element.10), channel_id=1, source_target_pairs={{0,896},{128,0},{256,128},{384,256},{512,384},{640,512},{768,640},... | collective-permute-start | bytes 1179656 | tf_op jit(solution)/shard_map/ppermute | solution.py:23
  69.0 1.9 %collective-permute-start.5 = (bf16[16,48,512]{2,1,0:T(8,128)(2,1)S(1)}, bf16[16,48,512]{2,1,0:T(8,128)(2,1)}, u32[]{:S(2)}, u32[]{:S(2)}) collective-permute-start(bf16[16,48,512]{2,1,0:T(8,128)(2,1)S(1)} %constant_dynamic-update-slice_fusion.own0), channel_id=1, source_target_pairs={{0,16},{16,0},{1,17},{17,1},{2,18},{18,2},{3,19},{19,3},{4,20},{20... | collective-permute-start | bytes 2359304 | tf_op jit(solution)/shard_map/ppermute | solution.py:27
  70.9 2.7 %collective-permute-done.3 = bf16[8,48,512]{2,1,0:T(8,128)(2,1)S(1)} collective-permute-done((bf16[8,48,512]{2,1,0:T(8,128)(2,1)S(1)}, bf16[8,48,512]{2,1,0:T(8,128)(2,1)S(1)}, u32[]{:S(2)}, u32[]{:S(2)}) %collective-permute-start.3) | collective-permute-done | bytes 393248 | tf_op jit(solution)/shard_map/ppermute | solution.py:23
  73.6 3.1 %collective-permute-done.4 = bf16[8,48,512]{2,1,0:T(8,128)(2,1)S(1)} collective-permute-done((bf16[8,48,512]{2,1,0:T(8,128)(2,1)S(1)}, bf16[8,48,512]{2,1,0:T(8,128)(2,1)S(1)}, u32[]{:S(2)}, u32[]{:S(2)}) %collective-permute-start.4) | collective-permute-done | bytes 393248 | tf_op jit(solution)/shard_map/ppermute | solution.py:23
  76.8 1.9 %collective-permute-start.6 = (bf16[16,48,512]{2,1,0:T(8,128)(2,1)S(1)}, bf16[16,48,512]{2,1,0:T(8,128)(2,1)}, u32[]{:S(2)}, u32[]{:S(2)}) collective-permute-start(bf16[16,48,512]{2,1,0:T(8,128)(2,1)S(1)} %constant_dynamic-update-slice_fusion.4.own1), channel_id=1, source_target_pairs={{0,16},{16,0},{1,17},{17,1},{2,18},{18,2},{3,19},{19,3},{4,20},{20... | collective-permute-start | bytes 2359304 | tf_op jit(solution)/shard_map/ppermute | solution.py:27
  79.3 0.0 copy-done
  79.4 0.0 copy-done.3
  79.5 0.0 all-to-all-done
  79.5 2.3 %shard_map.86.x_ref = bf16[256,3072]{1,0:T(8,128)(2,1)S(1)} custom-call(bf16[256,3072]{1,0:T(8,128)(2,1)S(1)} %bitcast.18, f32[3,3072]{1,0:T(4,128)S(1)} %bitcast.21), custom_call_target="tpu_custom_call" | custom-call | flops 9437184 | bytes 3145728 | tf_op jit(solution)/shard_map/pallas_call | solution.py:60
  81.7 0.0 collective-permute-done.5.other0
  81.8 0.0 collective-permute-done.6.other1
  81.8 7.1 %shard_map.87 = bf16[256,3072]{1,0:T(8,128)(2,1)} custom-call(s32[64]{0:T(128)S(1)} %fusion.at_ref, bf16[256,3072]{1,0:T(8,128)(2,1)S(1)} %shard_map.86.x_ref, bf16[16,48,512]{2,1,0:T(8,128)(2,1)S(1)} %constant_dynamic-update-slice_fusion.own0, bf16[16,48,512]{2,1,0:T(8,128)(2,1)S(1)} %constant_dynamic-update-slice_fusion.4.own1, ...), custom_call_target="tpu_custom_call" | custom-call | flops 805306368 | bytes 6291456 | tf_op jit(solution)/shard_map/pallas_call | solution.py:106
  88.9 0.0 copy-start.1
  88.9 0.0 copy-start.2
  88.9 7.6 %all-to-all-start.1 = ((bf16[16,16,3072]{2,1,0:T(8,128)(2,1)}), bf16[16,16,3072]{2,1,0:T(8,128)(2,1)S(1)}, u32[]{:S(2)}, u32[]{:S(2)}) async-start(bf16[16,16,3072]{2,1,0:T(8,128)(2,1)} %bitcast.5), calls=%async_computation.1 | async-start | bytes 3145728 | tf_op jit(solution)/shard_map/all_to_all | solution.py:182
  96.5 34.2 %all-to-all-done.1.parts_ref = bf16[16,16,3072]{2,1,0:T(8,128)(2,1)S(1)} async-done(((bf16[16,16,3072]{2,1,0:T(8,128)(2,1)}), bf16[16,16,3072]{2,1,0:T(8,128)(2,1)S(1)}, u32[]{:S(2)}, u32[]{:S(2)}) %all-to-all-start.1) | async-done | bytes 1572896 | tf_op jit(solution)/shard_map/all_to_all | solution.py:182
  130.7 0.0 copy-done.1
  130.7 0.0 copy-done.2
  130.8 1.0 shard_map.88
  131.7 8.6 %all-to-all-start.2 = ((f32[16,1,128]{2,1,0:T(1,128)}), f32[16,1,128]{2,1,0:T(1,128)S(1)}, u32[]{:S(2)}, u32[]{:S(2)}) async-start(f32[16,1,128]{2,1,0:T(1,128)} %get-tuple-element.9), calls=%async_computation.2 | async-start | bytes 16384 | tf_op jit(solution)/shard_map/all_to_all | solution.py:187
  140.4 7.9 %all-to-all-done.2 = f32[16,1,128]{2,1,0:T(1,128)S(1)} async-done(((f32[16,1,128]{2,1,0:T(1,128)}), f32[16,1,128]{2,1,0:T(1,128)S(1)}, u32[]{:S(2)}, u32[]{:S(2)}) %all-to-all-start.2) | async-done | bytes 8224 | tf_op jit(solution)/shard_map/all_to_all | solution.py:187
  148.2 0.6 slice_reduce_fusion
  (10 shorter events, 0.2 us)
Async XLA Ops:
  0.6 78.7 %copy-start = (f32[8,3,3072]{2,0,1:T(8,128)S(1)}, f32[8,3,3072]{2,0,1:T(8,128)}, u32[]{:S(2)}) copy-start(f32[8,3,3072]{2,0,1:T(8,128)} %param.11) | copy-start | bytes 884740
  34.0 45.5 %all-to-all-start = ((bf16[16,16,3072]{2,1,0:T(8,128)(2,1)}), bf16[16,16,3072]{2,1,0:T(8,128)(2,1)S(1)}, u32[]{:S(2)}, u32[]{:S(2)}) async-start(bf16[16,16,3072]{2,1,0:T(8,128)(2,1)} %broadcast_in_dim.21), calls=%async_computation | async-start | bytes 3145728 | tf_op jit(solution)/shard_map/all_to_all | solution.py:19
  41.6 11.4 %collective-permute-start = (bf16[4,48,512]{2,1,0:T(8,128)(2,1)S(1)}, bf16[4,48,512]{2,1,0:T(8,128)(2,1)S(1)}, u32[]{:S(2)}, u32[]{:S(2)}) collective-permute-start(bf16[4,48,512]{2,1,0:T(8,128)(2,1)S(1)} %bitcast.23), channel_id=1, source_target_pairs={{0,128},{128,256},{256,384},{384,512},{512,640},{640,768},{768,896... | collective-permute-start | bytes 589832 | tf_op jit(solution)/shard_map/ppermute | solution.py:23
  43.5 9.4 %collective-permute-start.1 = (bf16[4,48,512]{2,1,0:T(8,128)(2,1)S(1)}, bf16[4,48,512]{2,1,0:T(8,128)(2,1)S(1)}, u32[]{:S(2)}, u32[]{:S(2)}) collective-permute-start(bf16[4,48,512]{2,1,0:T(8,128)(2,1)S(1)} %bitcast.24), channel_id=1, source_target_pairs={{0,896},{128,0},{256,128},{384,256},{512,384},{640,512},{768,640},... | collective-permute-start | bytes 589832 | tf_op jit(solution)/shard_map/ppermute | solution.py:23
  47.4 15.5 %collective-permute-start.2 = (bf16[4,48,512]{2,1,0:T(8,128)(2,1)S(1)}, bf16[4,48,512]{2,1,0:T(8,128)(2,1)S(1)}, u32[]{:S(2)}, u32[]{:S(2)}) collective-permute-start(bf16[4,48,512]{2,1,0:T(8,128)(2,1)S(1)} %bitcast.25), channel_id=1, source_target_pairs={{0,512},{128,640},{256,768},{384,896},{512,0},{640,128},{768,256},... | collective-permute-start | bytes 589832 | tf_op jit(solution)/shard_map/ppermute | solution.py:23
  63.0 16.4 %copy-start.3 = (s32[64]{0:T(128)S(1)}, s32[64]{0:T(128)}, u32[]{:S(2)}) copy-start(s32[64]{0:T(128)} %param.10) | copy-start | bytes 772
  63.0 10.5 %collective-permute-start.3 = (bf16[8,48,512]{2,1,0:T(8,128)(2,1)S(1)}, bf16[8,48,512]{2,1,0:T(8,128)(2,1)S(1)}, u32[]{:S(2)}, u32[]{:S(2)}) collective-permute-start(bf16[8,48,512]{2,1,0:T(8,128)(2,1)S(1)} %get-tuple-element.11), channel_id=1, source_target_pairs={{0,128},{128,256},{256,384},{384,512},{512,640},{640,768},{768,896... | collective-permute-start | bytes 1179656 | tf_op jit(solution)/shard_map/ppermute | solution.py:23
  65.0 11.8 %collective-permute-start.4 = (bf16[8,48,512]{2,1,0:T(8,128)(2,1)S(1)}, bf16[8,48,512]{2,1,0:T(8,128)(2,1)S(1)}, u32[]{:S(2)}, u32[]{:S(2)}) collective-permute-start(bf16[8,48,512]{2,1,0:T(8,128)(2,1)S(1)} %get-tuple-element.10), channel_id=1, source_target_pairs={{0,896},{128,0},{256,128},{384,256},{512,384},{640,512},{768,640},... | collective-permute-start | bytes 1179656 | tf_op jit(solution)/shard_map/ppermute | solution.py:23
  69.0 12.8 %collective-permute-start.5 = (bf16[16,48,512]{2,1,0:T(8,128)(2,1)S(1)}, bf16[16,48,512]{2,1,0:T(8,128)(2,1)}, u32[]{:S(2)}, u32[]{:S(2)}) collective-permute-start(bf16[16,48,512]{2,1,0:T(8,128)(2,1)S(1)} %constant_dynamic-update-slice_fusion.own0), channel_id=1, source_target_pairs={{0,16},{16,0},{1,17},{17,1},{2,18},{18,2},{3,19},{19,3},{4,20},{20... | collective-permute-start | bytes 2359304 | tf_op jit(solution)/shard_map/ppermute | solution.py:27
  76.8 5.0 %collective-permute-start.6 = (bf16[16,48,512]{2,1,0:T(8,128)(2,1)S(1)}, bf16[16,48,512]{2,1,0:T(8,128)(2,1)}, u32[]{:S(2)}, u32[]{:S(2)}) collective-permute-start(bf16[16,48,512]{2,1,0:T(8,128)(2,1)S(1)} %constant_dynamic-update-slice_fusion.4.own1), channel_id=1, source_target_pairs={{0,16},{16,0},{1,17},{17,1},{2,18},{18,2},{3,19},{19,3},{4,20},{20... | collective-permute-start | bytes 2359304 | tf_op jit(solution)/shard_map/ppermute | solution.py:27
  88.9 41.9 %copy-start.1 = (bf16[1,16,3072]{2,1,0:T(8,128)(2,1)S(1)}, bf16[1,16,3072]{2,1,0:T(8,128)(2,1)}, u32[]{:S(2)}) copy-start(bf16[1,16,3072]{2,1,0:T(8,128)(2,1)} %param.7) | copy-start | bytes 294916
  88.9 41.9 %copy-start.2 = (bf16[1,16,3072]{2,1,0:T(8,128)(2,1)S(1)}, bf16[1,16,3072]{2,1,0:T(8,128)(2,1)}, u32[]{:S(2)}) copy-start(bf16[1,16,3072]{2,1,0:T(8,128)(2,1)} %param.8) | copy-start | bytes 294916
  88.9 41.9 %all-to-all-start.1 = ((bf16[16,16,3072]{2,1,0:T(8,128)(2,1)}), bf16[16,16,3072]{2,1,0:T(8,128)(2,1)S(1)}, u32[]{:S(2)}, u32[]{:S(2)}) async-start(bf16[16,16,3072]{2,1,0:T(8,128)(2,1)} %bitcast.5), calls=%async_computation.1 | async-start | bytes 3145728 | tf_op jit(solution)/shard_map/all_to_all | solution.py:182
  131.7 16.5 %all-to-all-start.2 = ((f32[16,1,128]{2,1,0:T(1,128)}), f32[16,1,128]{2,1,0:T(1,128)S(1)}, u32[]{:S(2)}, u32[]{:S(2)}) async-start(f32[16,1,128]{2,1,0:T(1,128)} %get-tuple-element.9), calls=%async_computation.2 | async-start | bytes 16384 | tf_op jit(solution)/shard_map/all_to_all | solution.py:187

commit v3 on v2

--- a/solution.py
+++ b/solution.py
@@ -7,7 +7,6 @@
 from jax.experimental.pallas import tpu as pltpu
 from jax.sharding import Mesh, PartitionSpec as P
 
-
 GROUP = ("y", "zh", "core")
 TENSOR = ("zl", "x")
 NY, NZH, NCORE, NZL, NX = 8, 4, 2, 4, 4
@@ -19,8 +18,9 @@
     return lax.all_to_all(copies, axis, split_axis=0, concat_axis=0, tiled=True)
 
 
-def shifted(x, by):
-    return lax.ppermute(x, "y", [(i, (i + by) % NY) for i in range(NY)])
+def shifted(x, by, name):
+    with jax.named_scope(name):
+        return lax.ppermute(x, "y", [(i, (i + by) % NY) for i in range(NY)])
 
 
 def swapped(x):
@@ -31,12 +31,12 @@
 
 
 def around_y(x):
-    below = shifted(x, 1)
-    above = shifted(x, -1)
-    across = shifted(x, 4)
+    below = shifted(x, 1, "w_up")
+    above = shifted(x, -1, "w_down")
+    across = shifted(x, 4, "w_four")
     near = jnp.concatenate([x, below, above, across], axis=0)
-    up = shifted(jnp.concatenate([below, across], axis=0), 1)
-    down = shifted(jnp.concatenate([above, across], axis=0), -1)
+    up = shifted(jnp.concatenate([below, across], axis=0), 1, "w_up2")
+    down = shifted(jnp.concatenate([above, across], axis=0), -1, "w_down2")
     return near, jnp.concatenate([up, down], axis=0)
 
 
@@ -69,20 +69,14 @@
     )(tokens, mod)
 
 
-def head_kernel(at_ref, x_ref, own0, own1, other0, other1, o_ref, w_ref):
-    slices, (count, rows, columns) = at_ref.shape[0], own0.shape
+def head_kernel(to_ref, x_ref, own0, own1, other0, other1, o_ref, w_ref):
+    count, rows, columns = own0.shape
     width = x_ref.shape[1]
     hd = columns // 4
-
-    @pl.loop(0, slices)
-    def _(s):
-        here = pl.ds(pl.multiple_of(s * rows, rows), rows)
-        at = at_ref[s]
-        for part, ref in enumerate((own0, own1, other0, other1)):
-
-            @pl.when(at // count == part)
-            def _():
-                w_ref[here, :] = ref[at % count]
+    for part, ref in enumerate((own0, own1, other0, other1)):
+        for k in range(count):
+            first = pl.multiple_of(to_ref[part * count + k] * rows, rows)
+            w_ref[pl.ds(first, rows), :] = ref[k]
 
     qkv = jnp.dot(x_ref[...], w_ref[:, : 3 * hd], preferred_element_type=jnp.float32)
     qkv = qkv.astype(jnp.bfloat16)
@@ -98,7 +92,7 @@
         o_ref[:, c : c + step] = term.astype(jnp.bfloat16)
 
 
-def head_term(tokens, pieces, at):
+def head_term(tokens, pieces, slots):
     seq, width = tokens.shape
     smem = pl.BlockSpec(memory_space=pltpu.SMEM)
     vmem = pl.BlockSpec(memory_space=pltpu.VMEM)
@@ -115,7 +109,7 @@
             bytes_accessed=8 * seq * width,
             transcendentals=seq * seq,
         ),
-    )(at, tokens, *pieces)
+    )(slots, tokens, *pieces)
 
 
 def mean_kernel(dt_ref, parts_ref, latent_ref, stored_ref, gate_ref, mean_ref, sum_ref):
@@ -155,13 +149,18 @@
     )(dt, parts, latent, stored, gate)
 
 
-def one_device(latents, stored_sample, timestep, owner_map, mod_table, qkv_weight, out_weight):
-    _, tok_local, width = latents.shape
+def shards(latents, stored_sample, timestep, owner_map, mod_table, qkv_weight, out_weight):
+    samples, tok_local, width = latents.shape
     step_count = mod_table.shape[0]
     seq_len = tok_local * NZL * NX
     t = timestep[0]
     time_float = t.astype(jnp.float32)
     mod = lax.dynamic_index_in_dim(mod_table, t, 0, keepdims=False)
+
+    sigma = 0.3 + 0.1 * time_float
+    dt = (timestep.astype(jnp.float32) + 1.0) / step_count
+    spread = 2.0 * sigma * sigma * seq_len * width
+    offset = jnp.log(sigma) + 0.5 * math.log(2.0 * math.pi)
 
     weights = jnp.concatenate([qkv_weight, out_weight.T], axis=1)
     plane = lax.all_gather(weights, "zh", tiled=False)
@@ -175,23 +174,22 @@
     for distance, where in enumerate(PLACE):
         place = jnp.where(ahead == distance, where, place)
     side = (owner_map % NCORE != lax.axis_index("core")).astype(jnp.int32)
-    at = ((side * NY + place) * NZH + (owner_map // NCORE) % NZH).astype(jnp.int32)
+    at = (side * NY + place) * NZH + (owner_map // NCORE) % NZH
+    slices = jnp.arange(at.shape[0], dtype=jnp.int32)
+    slots = jnp.sum(jnp.where(at[None, :] == slices[:, None], slices[None, :], 0), axis=1)
 
     modulated = normalised(tokens, mod)
-    terms = head_term(modulated, pieces, at)
+    terms = head_term(modulated, pieces, slots)
+    terms, latent, stored, gate, dt, spread, offset = lax.optimization_barrier(
+        (terms, latents[0], stored_sample[0], mod[2:3], dt, spread, offset)
+    )
     parts = lax.all_to_all(
         terms.reshape(NZL * NX, tok_local, width), TENSOR, split_axis=0, concat_axis=0, tiled=True
     )
-    dt = (timestep.astype(jnp.float32) + 1.0) / step_count
-    mean, squares = mean_and_squares(dt, parts, latents[0], stored_sample[0], mod[2:3])
+    mean, squares = mean_and_squares(dt, parts, latent, stored, gate)
+    mean, squares = lax.optimization_barrier((mean, squares))
     squares = lax.all_to_all(squares, TENSOR, split_axis=0, concat_axis=0, tiled=True)
-    total = jnp.sum(squares[:, :, :1])
-    sigma = 0.3 + 0.1 * time_float
-    log_prob = (
-        -total / (2.0 * sigma * sigma * seq_len * width)
-        - jnp.log(sigma)
-        - 0.5 * math.log(2.0 * math.pi)
-    )
+    log_prob = -jnp.sum(squares[:, :, :1]) / spread - offset
     return (mean[None], log_prob[None])
 
 
@@ -207,4 +205,4 @@
         P(TENSOR, GROUP),
     )
     out_specs = (P(GROUP, TENSOR, None), P(GROUP))
-    return jax.shard_map(one_device, mesh=fine, in_specs=in_specs, out_specs=out_specs, check_vma=False)
+    return jax.shard_map(shards, mesh=fine, in_specs=in_specs, out_specs=out_specs, check_vma=False)

time: 151 us -> 149 us (0.987)
  blocking collectives: 30.2 us -> 88.4 us
  waiting for transfers between devices: 57.9 us -> 15 us
  starting transfers between devices: 44.8 us -> 28.6 us
  Pallas kernels: 10.3 us -> 6.73 us
    all_to_all x0 -> x2, blocking collectives: none -> 58.2 us  [the longest x1 45.7 us: shards(): lax.all_to_all(terms.reshape(NZL * NX, tok_local, width), TENSOR, split_a...]
    all_to_all x2 -> x0, waiting for transfers between devices: 42.1 us -> none  [the longest x1 34.2 us: one_device(): lax.all_to_all(terms.reshape(NZL * NX, tok_local, width), TENSOR, split_a...]
    all_to_all x2 -> x0, starting transfers between devices: 16.2 us -> none  [the longest x1 8.57 us: one_device(): lax.all_to_all(squares, TENSOR, split_axis=0, concat_axis=0, tiled=True)]
    pallas_call x1, Pallas kernels: 7.1 us -> 3.56 us  [head_term(): pl.pallas_call(head_kernel, out_shape=jax.ShapeDtypeStruct((seq, width),...]
  transfers between devices with their start and end apart: 10 -> 8, of which waited for: 5 -> 3; matrix products, arithmetic and copies ran while one was open for 0% -> 2% of each run, Pallas kernels for 2% -> 2%
where the time goes in v3:
time: 149 us; the launch traced here: 148 us
  blocking collectives  88.4 us (59%)
  starting transfers between devices  28.6 us (19%)
  waiting for transfers between devices  15 us (10%)
  Pallas kernels  6.73 us (5%)
  local copies, waits for them, and re-layouts  3.42 us (2%)
  between operations  3.42 us (2%)
  other arithmetic  2.53 us (2%)
    all_to_all x1, blocking collectives, shards(): lax.all_to_all(terms.reshape(NZL * NX, tok_local, width), TENSOR, split_a...  45.7 us
    all_gather x1, blocking collectives, shards(): plane = lax.all_gather(weights, 'zh', tiled=False)  30.2 us
    ppermute x5, starting transfers between devices, shifted(): return lax.ppermute(x, 'y', [(i, (i + by) % NY) for i in range(NY)])  17.2 us
    ppermute x5, waiting for transfers between devices, shifted(): return lax.ppermute(x, 'y', [(i, (i + by) % NY) for i in range(NY)])  15 us
    all_to_all x1, blocking collectives, shards(): lax.all_to_all(squares, TENSOR, split_axis=0, concat_axis=0, tiled=True)  12.5 us
    all_to_all x1, starting transfers between devices, to_all(): return lax.all_to_all(copies, axis, split_axis=0, concat_axis=0, tiled=True)  7.59 us
    ppermute x2, starting transfers between devices, swapped(): return lax.ppermute(x, 'core', [(0, 1), (1, 0)])  3.84 us
    pallas_call x1, Pallas kernels, head_term(): pl.pallas_call(head_kernel, out_shape=jax.ShapeDtypeStruct((seq, width),...  3.56 us
  transfers between devices with their start and end apart: 8, of which 3 were waited for; matrix products, arithmetic and copies ran while one was open for 2% of the time, Pallas kernels for 2%

profile of v3, /device:TPU:56, one launch (start us, length us, event | category | flops | bytes accessed | tf_op | source)
XLA Modules:
  0.0 148.1 jit_solution(28766607012266166)
XLA Ops:
  0.6 0.0 copy-start
  0.6 0.8 pad_maximum_fusion.2
  1.5 30.2 %all-gather = bf16[192,512]{1,0:T(8,128)(2,1)S(1)} all-gather(bf16[48,512]{1,0:T(8,128)(2,1)S(1)} %pad_maximum_fusion.2), channel_id=2, replica_groups=mesh['y'=8,'zh'=4,'core'=2,'zl'=4,'x'=4] {'zh'}, dimensions={0}, use_global_device_ids=true | all-gather | bytes 245760 | tf_op jit(solution)/shard_map/all_gather | solution.py:166
  31.7 2.2 %broadcast_in_dim.38 = bf16[16,16,3072]{2,1,0:T(8,128)(2,1)} broadcast(bf16[16,3072]{1,0:T(8,128)(2,1)} %bitcast.20), dimensions={1,2} | broadcast | bytes 1671168 | tf_op jit(solution)/shard_map/broadcast_in_dim | solution.py:17
  33.9 7.6 %all-to-all-start = ((bf16[16,16,3072]{2,1,0:T(8,128)(2,1)}), bf16[16,16,3072]{2,1,0:T(8,128)(2,1)S(1)}, u32[]{:S(2)}, u32[]{:S(2)}) async-start(bf16[16,16,3072]{2,1,0:T(8,128)(2,1)} %broadcast_in_dim.38), calls=%async_computation | async-start | bytes 3145728 | tf_op jit(solution)/shard_map/all_to_all | solution.py:18
  41.5 1.9 %collective-permute-start = (bf16[4,48,512]{2,1,0:T(8,128)(2,1)S(1)}, bf16[4,48,512]{2,1,0:T(8,128)(2,1)S(1)}, u32[]{:S(2)}, u32[]{:S(2)}) collective-permute-start(bf16[4,48,512]{2,1,0:T(8,128)(2,1)S(1)} %bitcast.24), channel_id=1, source_target_pairs={{0,128},{128,256},{256,384},{384,512},{512,640},{640,768},{768,896... | collective-permute-start | bytes 589832 | tf_op jit(solution)/shard_map/w_up/ppermute | solution.py:23
  43.5 3.9 %collective-permute-start.1 = (bf16[4,48,512]{2,1,0:T(8,128)(2,1)S(1)}, bf16[4,48,512]{2,1,0:T(8,128)(2,1)S(1)}, u32[]{:S(2)}, u32[]{:S(2)}) collective-permute-start(bf16[4,48,512]{2,1,0:T(8,128)(2,1)S(1)} %bitcast.25), channel_id=1, source_target_pairs={{0,896},{128,0},{256,128},{384,256},{512,384},{640,512},{768,640},... | collective-permute-start | bytes 589832 | tf_op jit(solution)/shard_map/w_down/ppermute | solution.py:23
  47.4 5.5 %collective-permute-start.2 = (bf16[4,48,512]{2,1,0:T(8,128)(2,1)S(1)}, bf16[4,48,512]{2,1,0:T(8,128)(2,1)S(1)}, u32[]{:S(2)}, u32[]{:S(2)}) collective-permute-start(bf16[4,48,512]{2,1,0:T(8,128)(2,1)S(1)} %bitcast.26), channel_id=1, source_target_pairs={{0,512},{128,640},{256,768},{384,896},{512,0},{640,128},{768,256},... | collective-permute-start | bytes 589832 | tf_op jit(solution)/shard_map/w_four/ppermute | solution.py:23
  52.9 0.0 collective-permute-done
  52.9 0.0 collective-permute-done.1
  52.9 10.0 %collective-permute-done.2 = bf16[4,48,512]{2,1,0:T(8,128)(2,1)S(1)} collective-permute-done((bf16[4,48,512]{2,1,0:T(8,128)(2,1)S(1)}, bf16[4,48,512]{2,1,0:T(8,128)(2,1)S(1)}, u32[]{:S(2)}, u32[]{:S(2)}) %collective-permute-start.2) | collective-permute-done | bytes 196640 | tf_op jit(solution)/shard_map/w_four/ppermute | solution.py:23
  62.9 0.9 pad_maximum_fusion
  63.9 1.9 %collective-permute-start.3 = (bf16[8,48,512]{2,1,0:T(8,128)(2,1)}, bf16[8,48,512]{2,1,0:T(8,128)(2,1)}, u32[]{:S(2)}, u32[]{:S(2)}) collective-permute-start(bf16[8,48,512]{2,1,0:T(8,128)(2,1)} %get-tuple-element.25), channel_id=1, source_target_pairs={{0,128},{128,256},{256,384},{384,512},{512,640},{640,768},{768,896... | collective-permute-start | bytes 1179656 | tf_op jit(solution)/shard_map/w_up2/ppermute | solution.py:23
  65.8 0.0 copy-start.3
  66.5 3.9 %collective-permute-start.4 = (bf16[8,48,512]{2,1,0:T(8,128)(2,1)}, bf16[8,48,512]{2,1,0:T(8,128)(2,1)S(1)}, u32[]{:S(2)}, u32[]{:S(2)}) collective-permute-start(bf16[8,48,512]{2,1,0:T(8,128)(2,1)} %get-tuple-element.24), channel_id=1, source_target_pairs={{0,896},{128,0},{256,128},{384,256},{512,384},{640,512},{768,640},... | collective-permute-start | bytes 1179656 | tf_op jit(solution)/shard_map/w_down2/ppermute | solution.py:23
  70.5 1.9 %collective-permute-start.5 = (bf16[16,48,512]{2,1,0:T(8,128)(2,1)S(1)}, bf16[16,48,512]{2,1,0:T(8,128)(2,1)}, u32[]{:S(2)}, u32[]{:S(2)}) collective-permute-start(bf16[16,48,512]{2,1,0:T(8,128)(2,1)S(1)} %constant_dynamic-update-slice_fusion.own0), channel_id=1, source_target_pairs={{0,16},{16,0},{1,17},{17,1},{2,18},{18,2},{3,19},{19,3},{4,20},{20... | collective-permute-start | bytes 2359304 | tf_op jit(solution)/shard_map/ppermute | solution.py:27
  72.4 2.3 %collective-permute-done.3 = bf16[8,48,512]{2,1,0:T(8,128)(2,1)} collective-permute-done((bf16[8,48,512]{2,1,0:T(8,128)(2,1)}, bf16[8,48,512]{2,1,0:T(8,128)(2,1)}, u32[]{:S(2)}, u32[]{:S(2)}) %collective-permute-start.3) | collective-permute-done | bytes 393248 | tf_op jit(solution)/shard_map/w_up2/ppermute | solution.py:23
  74.7 1.0 constant_dynamic-update-slice_fusion.5
  75.7 2.7 %collective-permute-done.4 = bf16[8,48,512]{2,1,0:T(8,128)(2,1)S(1)} collective-permute-done((bf16[8,48,512]{2,1,0:T(8,128)(2,1)}, bf16[8,48,512]{2,1,0:T(8,128)(2,1)S(1)}, u32[]{:S(2)}, u32[]{:S(2)}) %collective-permute-start.4) | collective-permute-done | bytes 393248 | tf_op jit(solution)/shard_map/w_down2/ppermute | solution.py:23
  78.5 1.9 %collective-permute-start.6 = (bf16[16,48,512]{2,1,0:T(8,128)(2,1)S(1)}, bf16[16,48,512]{2,1,0:T(8,128)(2,1)}, u32[]{:S(2)}, u32[]{:S(2)}) collective-permute-start(bf16[16,48,512]{2,1,0:T(8,128)(2,1)S(1)} %constant_dynamic-update-slice_fusion.4.own1), channel_id=1, source_target_pairs={{0,16},{16,0},{1,17},{17,1},{2,18},{18,2},{3,19},{19,3},{4,20},{20... | collective-permute-start | bytes 2359304 | tf_op jit(solution)/shard_map/ppermute | solution.py:27
  80.4 0.0 copy-done
  80.5 0.0 copy-done.3
  80.6 0.1 select_reduce_fusion.to_ref
  80.7 0.0 all-to-all-done
  80.7 2.3 %shard_map.86.x_ref = bf16[256,3072]{1,0:T(8,128)(2,1)S(1)} custom-call(bf16[256,3072]{1,0:T(8,128)(2,1)S(1)} %bitcast.18, f32[3,3072]{1,0:T(4,128)S(1)} %bitcast.22), custom_call_target="tpu_custom_call" | custom-call | flops 9437184 | bytes 3145728 | tf_op jit(solution)/shard_map/pallas_call | solution.py:60
  83.0 0.0 collective-permute-done.5.other0
  83.0 0.0 collective-permute-done.6.other1
  83.0 3.6 %shard_map.87 = bf16[256,3072]{1,0:T(8,128)(2,1)S(1)} custom-call(s32[64]{0:T(128)S(1)} %select_reduce_fusion.to_ref, bf16[256,3072]{1,0:T(8,128)(2,1)S(1)} %shard_map.86.x_ref, bf16[16,48,512]{2,1,0:T(8,128)(2,1)S(1)} %constant_dynamic-update-slice_fusion.own0, bf16[16,48,512]{2,1,0:T(8,128)(2,1)S(1)} %constant_dynamic-update-slice_fusion.4.own1, ...), custom_call_target="tpu_custom_call" | custom-call | flops 805306368 | bytes 6291456 | tf_op jit(solution)/shard_map/pallas_call | solution.py:100
  86.6 0.0 copy-start.1
  86.6 0.0 copy-start.2
  86.6 45.7 %all_to_all.15.parts_ref = bf16[16,16,3072]{2,1,0:T(8,128)(2,1)S(1)} all-to-all(bf16[16,16,3072]{2,1,0:T(8,128)(2,1)S(1)} %bitcast.19), channel_id=1, replica_groups=mesh['y'=8,'zh'=4,'core'=2,'zl'=4,'x'=4] {'zl','x'}, dimensions={0} | all-to-all | bytes 3145728 | tf_op jit(solution)/shard_map/all_to_all | solution.py:186
  132.3 0.0 copy-done.1
  132.3 0.0 copy-done.2
  132.3 0.9 shard_map.88
  133.2 12.5 %all_to_all.16 = f32[16,1,128]{2,1,0:T(1,128)S(1)} all-to-all(f32[16,1,128]{2,1,0:T(1,128)S(1)} %get-tuple-element.21), channel_id=1, replica_groups=mesh['y'=8,'zh'=4,'core'=2,'zl'=4,'x'=4] {'zl','x'}, dimensions={0} | all-to-all | bytes 16384 | tf_op jit(solution)/shard_map/all_to_all | solution.py:191
  145.7 0.6 slice_reduce_fusion
  (9 shorter events, 0.2 us)
Async XLA Ops:
  0.6 79.8 %copy-start = (f32[8,3,3072]{2,0,1:T(8,128)S(1)}, f32[8,3,3072]{2,0,1:T(8,128)}, u32[]{:S(2)}) copy-start(f32[8,3,3072]{2,0,1:T(8,128)} %param.11) | copy-start | bytes 884740
  33.9 46.8 %all-to-all-start = ((bf16[16,16,3072]{2,1,0:T(8,128)(2,1)}), bf16[16,16,3072]{2,1,0:T(8,128)(2,1)S(1)}, u32[]{:S(2)}, u32[]{:S(2)}) async-start(bf16[16,16,3072]{2,1,0:T(8,128)(2,1)} %broadcast_in_dim.38), calls=%async_computation | async-start | bytes 3145728 | tf_op jit(solution)/shard_map/all_to_all | solution.py:18
  41.5 11.4 %collective-permute-start = (bf16[4,48,512]{2,1,0:T(8,128)(2,1)S(1)}, bf16[4,48,512]{2,1,0:T(8,128)(2,1)S(1)}, u32[]{:S(2)}, u32[]{:S(2)}) collective-permute-start(bf16[4,48,512]{2,1,0:T(8,128)(2,1)S(1)} %bitcast.24), channel_id=1, source_target_pairs={{0,128},{128,256},{256,384},{384,512},{512,640},{640,768},{768,896... | collective-permute-start | bytes 589832 | tf_op jit(solution)/shard_map/w_up/ppermute | solution.py:23
  43.5 9.4 %collective-permute-start.1 = (bf16[4,48,512]{2,1,0:T(8,128)(2,1)S(1)}, bf16[4,48,512]{2,1,0:T(8,128)(2,1)S(1)}, u32[]{:S(2)}, u32[]{:S(2)}) collective-permute-start(bf16[4,48,512]{2,1,0:T(8,128)(2,1)S(1)} %bitcast.25), channel_id=1, source_target_pairs={{0,896},{128,0},{256,128},{384,256},{512,384},{640,512},{768,640},... | collective-permute-start | bytes 589832 | tf_op jit(solution)/shard_map/w_down/ppermute | solution.py:23
  47.4 15.5 %collective-permute-start.2 = (bf16[4,48,512]{2,1,0:T(8,128)(2,1)S(1)}, bf16[4,48,512]{2,1,0:T(8,128)(2,1)S(1)}, u32[]{:S(2)}, u32[]{:S(2)}) collective-permute-start(bf16[4,48,512]{2,1,0:T(8,128)(2,1)S(1)} %bitcast.26), channel_id=1, source_target_pairs={{0,512},{128,640},{256,768},{384,896},{512,0},{640,128},{768,256},... | collective-permute-start | bytes 589832 | tf_op jit(solution)/shard_map/w_four/ppermute | solution.py:23
  63.9 10.9 %collective-permute-start.3 = (bf16[8,48,512]{2,1,0:T(8,128)(2,1)}, bf16[8,48,512]{2,1,0:T(8,128)(2,1)}, u32[]{:S(2)}, u32[]{:S(2)}) collective-permute-start(bf16[8,48,512]{2,1,0:T(8,128)(2,1)} %get-tuple-element.25), channel_id=1, source_target_pairs={{0,128},{128,256},{256,384},{384,512},{512,640},{640,768},{768,896... | collective-permute-start | bytes 1179656 | tf_op jit(solution)/shard_map/w_up2/ppermute | solution.py:23
  65.8 14.7 %copy-start.3 = (s32[64]{0:T(128)S(1)}, s32[64]{0:T(128)}, u32[]{:S(2)}) copy-start(s32[64]{0:T(128)} %param.10) | copy-start | bytes 772
  66.5 12.0 %collective-permute-start.4 = (bf16[8,48,512]{2,1,0:T(8,128)(2,1)}, bf16[8,48,512]{2,1,0:T(8,128)(2,1)S(1)}, u32[]{:S(2)}, u32[]{:S(2)}) collective-permute-start(bf16[8,48,512]{2,1,0:T(8,128)(2,1)} %get-tuple-element.24), channel_id=1, source_target_pairs={{0,896},{128,0},{256,128},{384,256},{512,384},{640,512},{768,640},... | collective-permute-start | bytes 1179656 | tf_op jit(solution)/shard_map/w_down2/ppermute | solution.py:23
  70.5 12.5 %collective-permute-start.5 = (bf16[16,48,512]{2,1,0:T(8,128)(2,1)S(1)}, bf16[16,48,512]{2,1,0:T(8,128)(2,1)}, u32[]{:S(2)}, u32[]{:S(2)}) collective-permute-start(bf16[16,48,512]{2,1,0:T(8,128)(2,1)S(1)} %constant_dynamic-update-slice_fusion.own0), channel_id=1, source_target_pairs={{0,16},{16,0},{1,17},{17,1},{2,18},{18,2},{3,19},{19,3},{4,20},{20... | collective-permute-start | bytes 2359304 | tf_op jit(solution)/shard_map/ppermute | solution.py:27
  78.5 4.5 %collective-permute-start.6 = (bf16[16,48,512]{2,1,0:T(8,128)(2,1)S(1)}, bf16[16,48,512]{2,1,0:T(8,128)(2,1)}, u32[]{:S(2)}, u32[]{:S(2)}) collective-permute-start(bf16[16,48,512]{2,1,0:T(8,128)(2,1)S(1)} %constant_dynamic-update-slice_fusion.4.own1), channel_id=1, source_target_pairs={{0,16},{16,0},{1,17},{17,1},{2,18},{18,2},{3,19},{19,3},{4,20},{20... | collective-permute-start | bytes 2359304 | tf_op jit(solution)/shard_map/ppermute | solution.py:27
  86.6 45.7 %copy-start.1 = (bf16[1,16,3072]{2,1,0:T(8,128)(2,1)S(1)}, bf16[1,16,3072]{2,1,0:T(8,128)(2,1)}, u32[]{:S(2)}) copy-start(bf16[1,16,3072]{2,1,0:T(8,128)(2,1)} %param.7) | copy-start | bytes 294916
  86.6 45.7 %copy-start.2 = (bf16[1,16,3072]{2,1,0:T(8,128)(2,1)S(1)}, bf16[1,16,3072]{2,1,0:T(8,128)(2,1)}, u32[]{:S(2)}) copy-start(bf16[1,16,3072]{2,1,0:T(8,128)(2,1)} %param.8) | copy-start | bytes 294916

commit v4 on v3

--- a/solution.py
+++ b/solution.py
@@ -69,7 +69,8 @@
     )(tokens, mod)
 
 
-def head_kernel(to_ref, x_ref, own0, own1, other0, other1, o_ref, w_ref):
+def head_kernel(to_ref, row_ref, x_ref, own0, own1, other0, other1, *rest):
+    outs, (w_ref, a_ref) = rest[:NX], rest[NX:]
     count, rows, columns = own0.shape
     width = x_ref.shape[1]
     hd = columns // 4
@@ -84,44 +85,86 @@
     scores = lax.dot_general(q, k, NT, preferred_element_type=jnp.float32) / math.sqrt(hd)
     expo = jnp.exp(scores - jnp.max(scores, axis=1, keepdims=True))
     probs = (expo / jnp.sum(expo, axis=1, keepdims=True)).astype(jnp.bfloat16)
-    attended = jnp.dot(probs, v, preferred_element_type=jnp.float32).astype(jnp.bfloat16)
+    attended = jnp.dot(probs, v, preferred_element_type=jnp.float32)
+    a_ref[...] = attended.astype(jnp.bfloat16)
+    blocks = row_ref.shape[0]
+    tok = a_ref.shape[0] // blocks
+    ordered = jnp.concatenate(
+        [a_ref[pl.ds(pl.multiple_of(row_ref[i], tok), tok), :] for i in range(blocks)], axis=0
+    )
     step = 512
+    part = ordered.shape[0] // NX
     for c in range(0, width, step):
         w_out = w_ref[c : c + step, 3 * hd :]
-        term = lax.dot_general(attended, w_out, NT, preferred_element_type=jnp.float32)
-        o_ref[:, c : c + step] = term.astype(jnp.bfloat16)
-
-
-def head_term(tokens, pieces, slots):
+        term = lax.dot_general(ordered, w_out, NT, preferred_element_type=jnp.float32)
+        term = term.astype(jnp.bfloat16)
+        for r, o_ref in enumerate(outs):
+            o_ref[:, c : c + step] = term[r * part : (r + 1) * part]
+
+
+def head_term(tokens, pieces, slots, first_rows):
     seq, width = tokens.shape
     smem = pl.BlockSpec(memory_space=pltpu.SMEM)
     vmem = pl.BlockSpec(memory_space=pltpu.VMEM)
     columns = pieces[0].shape[2]
     return pl.pallas_call(
         head_kernel,
-        out_shape=jax.ShapeDtypeStruct((seq, width), jnp.bfloat16),
-        in_specs=[smem] + [vmem] * 5,
-        out_specs=vmem,
-        scratch_shapes=[pltpu.VMEM((width, columns), jnp.bfloat16)],
+        out_shape=[jax.ShapeDtypeStruct((seq // NX, width), jnp.bfloat16)] * NX,
+        in_specs=[smem] * 2 + [vmem] * 5,
+        out_specs=[vmem] * NX,
+        scratch_shapes=[
+            pltpu.VMEM((width, columns), jnp.bfloat16),
+            pltpu.VMEM((seq, columns // 4), jnp.bfloat16),
+        ],
         compiler_params=pltpu.CompilerParams(vmem_limit_bytes=40 * 1024 * 1024),
         cost_estimate=pl.CostEstimate(
             flops=2 * seq * width * columns,
             bytes_accessed=8 * seq * width,
             transcendentals=seq * seq,
         ),
-    )(slots, tokens, *pieces)
-
-
-def mean_kernel(dt_ref, parts_ref, latent_ref, stored_ref, gate_ref, mean_ref, sum_ref):
+    )(slots, first_rows, tokens, *pieces)
+
+
+def sum_kernel(*refs):
+    ins, outs = refs[:NX], refs[NX:]
+    rows = outs[0].shape[0]
+    step = 1024
+    for k, o_ref in enumerate(outs):
+        for c in range(0, o_ref.shape[1], step):
+            here = (slice(k * rows, (k + 1) * rows), slice(c, c + step))
+            total = ins[0][here].astype(jnp.float32)
+            for ref in ins[1:]:
+                total = total + ref[here].astype(jnp.float32)
+            o_ref[:, c : c + step] = total.astype(o_ref.dtype)
+
+
+def summed(blocks):
+    rows, width = blocks[0].shape
+    vmem = pl.BlockSpec(memory_space=pltpu.VMEM)
+    shape = (rows // NZL, width)
+    return pl.pallas_call(
+        sum_kernel,
+        out_shape=[jax.ShapeDtypeStruct(shape, jnp.float32)]
+        + [jax.ShapeDtypeStruct(shape, jnp.bfloat16)] * (NZL - 1),
+        in_specs=[vmem] * NX,
+        out_specs=[vmem] * NZL,
+        compiler_params=pltpu.CompilerParams(vmem_limit_bytes=16 * 1024 * 1024),
+        cost_estimate=pl.CostEstimate(
+            flops=4 * rows * width, bytes_accessed=10 * rows * width, transcendentals=0
+        ),
+    )(*blocks)
+
+
+def mean_kernel(dt_ref, p0, p1, p2, p3, latent_ref, stored_ref, gate_ref, mean_ref, sum_ref):
     dt = dt_ref[0]
-    devices, rows, width = parts_ref.shape
+    rows, width = p0.shape
     step = 512
     squares = jnp.zeros((rows, step), jnp.float32)
     for c in range(0, width, step):
         here = slice(c, c + step)
-        proj = parts_ref[0, :, here].astype(jnp.float32)
-        for k in range(1, devices):
-            proj = proj + parts_ref[k, :, here].astype(jnp.float32)
+        proj = p0[:, here]
+        for ref in (p1, p2, p3):
+            proj = proj + ref[:, here].astype(jnp.float32)
         latent = latent_ref[:, here].astype(jnp.float32)
         mean = latent - dt * (latent + gate_ref[:, here] * proj)
         mean_ref[:, here] = mean.astype(jnp.bfloat16)
@@ -132,21 +175,21 @@
 
 
 def mean_and_squares(dt, parts, latent, stored, gate):
-    devices, rows, width = parts.shape
+    rows, width = latent.shape
     vmem = pl.BlockSpec(memory_space=pltpu.VMEM)
     return pl.pallas_call(
         mean_kernel,
         out_shape=(
             jax.ShapeDtypeStruct((rows, width), jnp.bfloat16),
-            jax.ShapeDtypeStruct((devices, 1, 128), jnp.float32),
-        ),
-        in_specs=[pl.BlockSpec(memory_space=pltpu.SMEM)] + [vmem] * 4,
+            jax.ShapeDtypeStruct((NZL * NX, 1, 128), jnp.float32),
+        ),
+        in_specs=[pl.BlockSpec(memory_space=pltpu.SMEM)] + [vmem] * 7,
         out_specs=(vmem, vmem),
         compiler_params=pltpu.CompilerParams(vmem_limit_bytes=16 * 1024 * 1024),
         cost_estimate=pl.CostEstimate(
-            flops=30 * rows * width, bytes_accessed=40 * rows * width, transcendentals=0
-        ),
-    )(dt, parts, latent, stored, gate)
+            flops=16 * rows * width, bytes_accessed=16 * rows * width, transcendentals=0
+        ),
+    )(dt, *parts, latent, stored, gate)
 
 
 def shards(latents, stored_sample, timestep, owner_map, mod_table, qkv_weight, out_weight):
@@ -178,16 +221,22 @@
     slices = jnp.arange(at.shape[0], dtype=jnp.int32)
     slots = jnp.sum(jnp.where(at[None, :] == slices[:, None], slices[None, :], 0), axis=1)
 
+    turn = jnp.arange(NX * NZL, dtype=jnp.int32)
+    to_x = (lax.axis_index("x") + turn // NZL) % NX
+    to_z = lax.axis_index("zl") ^ (turn % NZL)
+    first_rows = ((to_z * NX + to_x) * tok_local).astype(jnp.int32)
+
     modulated = normalised(tokens, mod)
-    terms = head_term(modulated, pieces, slots)
-    terms, latent, stored, gate, dt, spread, offset = lax.optimization_barrier(
-        (terms, latents[0], stored_sample[0], mod[2:3], dt, spread, offset)
-    )
-    parts = lax.all_to_all(
-        terms.reshape(NZL * NX, tok_local, width), TENSOR, split_axis=0, concat_axis=0, tiled=True
-    )
-    mean, squares = mean_and_squares(dt, parts, latent, stored, gate)
-    mean, squares = lax.optimization_barrier((mean, squares))
+    terms = head_term(modulated, pieces, slots, first_rows)
+    by_x = [terms[0]] + [
+        lax.ppermute(terms[r], "x", [(i, (i + r) % NX) for i in range(NX)]) for r in (2, 1, 3)
+    ]
+    some = summed(by_x)
+    by_z = [some[0]] + [
+        lax.ppermute(some[k], "zl", [(i, i ^ k) for i in range(NZL)]) for k in (2, 3, 1)
+    ]
+    mean, squares = mean_and_squares(dt, by_z, latents[0], stored_sample[0], mod[2:3])
+    mean, squares, spread, offset = lax.optimization_barrier((mean, squares, spread, offset))
     squares = lax.all_to_all(squares, TENSOR, split_axis=0, concat_axis=0, tiled=True)
     log_prob = -jnp.sum(squares[:, :, :1]) / spread - offset
     return (mean[None], log_prob[None])

time: 149 us -> 145 us (0.973)
  blocking collectives: 88.4 us -> 44.2 us
  starting transfers between devices: 28.6 us -> 50.7 us
  waiting for transfers between devices: 15 us -> 31.6 us
    all_to_all x1 -> x0, blocking collectives: 45.7 us -> none  [shards(): lax.all_to_all(terms.reshape(NZL * NX, tok_local, width), TENSOR, split_a...]
    ppermute x0 -> x6, starting transfers between devices: none -> 22.1 us  [the longest x3 12.5 us: shards(): lax.ppermute(terms[r], 'x', [(i, (i + r) % NX) for i in range(NX)])]
    ppermute x0 -> x6, waiting for transfers between devices: none -> 16.6 us  [the longest x3 11.6 us: shards(): lax.ppermute(terms[r], 'x', [(i, (i + r) % NX) for i in range(NX)])]
    pallas_call x1 -> x2, Pallas kernels: 3.56 us -> 4.83 us  [the longest x1 4.64 us: head_term(): pl.pallas_call(head_kernel, out_shape=[jax.ShapeDtypeStruct((seq // NX, w...]
  transfers between devices with their start and end apart: 8 -> 14, of which waited for: 3 -> 8; matrix products, arithmetic and copies ran while one was open for 2% -> 2% of each run, Pallas kernels for 2% -> 2%
where the time goes in v4:
time: 145 us; the launch traced here: 144 us
  starting transfers between devices  50.7 us (35%)
  blocking collectives  44.2 us (30%)
  waiting for transfers between devices  31.6 us (22%)
  Pallas kernels  7.84 us (5%)
  between operations  3.46 us (2%)
  local copies, waits for them, and re-layouts  3.44 us (2%)
  other arithmetic  2.55 us (2%)
    all_gather x1, blocking collectives, shards(): plane = lax.all_gather(weights, 'zh', tiled=False)  30.2 us
    ppermute x5, starting transfers between devices, shifted(): return lax.ppermute(x, 'y', [(i, (i + by) % NY) for i in range(NY)])  17.2 us
    ppermute x5, waiting for transfers between devices, shifted(): return lax.ppermute(x, 'y', [(i, (i + by) % NY) for i in range(NY)])  15 us
    all_to_all x1, blocking collectives, shards(): lax.all_to_all(squares, TENSOR, split_axis=0, concat_axis=0, tiled=True)  14 us
    ppermute x3, starting transfers between devices, shards(): lax.ppermute(terms[r], 'x', [(i, (i + r) % NX) for i in range(NX)])  12.5 us
    ppermute x3, waiting for transfers between devices, shards(): lax.ppermute(terms[r], 'x', [(i, (i + r) % NX) for i in range(NX)])  11.6 us
    ppermute x3, starting transfers between devices, shards(): lax.ppermute(some[k], 'zl', [(i, i ^ k) for i in range(NZL)])  9.58 us
    all_to_all x1, starting transfers between devices, to_all(): return lax.all_to_all(copies, axis, split_axis=0, concat_axis=0, tiled=True)  7.59 us
  transfers between devices with their start and end apart: 14, of which 8 were waited for; matrix products, arithmetic and copies ran while one was open for 2% of the time, Pallas kernels for 2%

profile of v4, /device:TPU:56, one launch (start us, length us, event | category | flops | bytes accessed | tf_op | source)
XLA Modules:
  0.0 143.8 jit_solution(12180389858363489265)
XLA Ops:
  0.6 0.0 copy-start
  0.6 0.8 pad_maximum_fusion.2
  1.5 30.2 %all-gather = bf16[192,512]{1,0:T(8,128)(2,1)S(1)} all-gather(bf16[48,512]{1,0:T(8,128)(2,1)S(1)} %pad_maximum_fusion.2), channel_id=2, replica_groups=mesh['y'=8,'zh'=4,'core'=2,'zl'=4,'x'=4] {'zh'}, dimensions={0}, use_global_device_ids=true | all-gather | bytes 245760 | tf_op jit(solution)/shard_map/all_gather | solution.py:209
  31.7 2.2 %broadcast_in_dim.38 = bf16[16,16,3072]{2,1,0:T(8,128)(2,1)} broadcast(bf16[16,3072]{1,0:T(8,128)(2,1)} %bitcast.18), dimensions={1,2} | broadcast | bytes 1671168 | tf_op jit(solution)/shard_map/broadcast_in_dim | solution.py:17
  33.9 7.6 %all-to-all-start = ((bf16[16,16,3072]{2,1,0:T(8,128)(2,1)}), bf16[16,16,3072]{2,1,0:T(8,128)(2,1)S(1)}, u32[]{:S(2)}, u32[]{:S(2)}) async-start(bf16[16,16,3072]{2,1,0:T(8,128)(2,1)} %broadcast_in_dim.38), calls=%async_computation | async-start | bytes 3145728 | tf_op jit(solution)/shard_map/all_to_all | solution.py:18
  41.5 1.9 %collective-permute-start = (bf16[4,48,512]{2,1,0:T(8,128)(2,1)S(1)}, bf16[4,48,512]{2,1,0:T(8,128)(2,1)S(1)}, u32[]{:S(2)}, u32[]{:S(2)}) collective-permute-start(bf16[4,48,512]{2,1,0:T(8,128)(2,1)S(1)} %bitcast.22), channel_id=1, source_target_pairs={{0,128},{128,256},{256,384},{384,512},{512,640},{640,768},{768,896... | collective-permute-start | bytes 589832 | tf_op jit(solution)/shard_map/w_up/ppermute | solution.py:23
  43.5 3.9 %collective-permute-start.1 = (bf16[4,48,512]{2,1,0:T(8,128)(2,1)S(1)}, bf16[4,48,512]{2,1,0:T(8,128)(2,1)S(1)}, u32[]{:S(2)}, u32[]{:S(2)}) collective-permute-start(bf16[4,48,512]{2,1,0:T(8,128)(2,1)S(1)} %bitcast.23), channel_id=1, source_target_pairs={{0,896},{128,0},{256,128},{384,256},{512,384},{640,512},{768,640},... | collective-permute-start | bytes 589832 | tf_op jit(solution)/shard_map/w_down/ppermute | solution.py:23
  47.4 5.5 %collective-permute-start.2 = (bf16[4,48,512]{2,1,0:T(8,128)(2,1)S(1)}, bf16[4,48,512]{2,1,0:T(8,128)(2,1)S(1)}, u32[]{:S(2)}, u32[]{:S(2)}) collective-permute-start(bf16[4,48,512]{2,1,0:T(8,128)(2,1)S(1)} %bitcast.24), channel_id=1, source_target_pairs={{0,512},{128,640},{256,768},{384,896},{512,0},{640,128},{768,256},... | collective-permute-start | bytes 589832 | tf_op jit(solution)/shard_map/w_four/ppermute | solution.py:23
  52.9 0.0 collective-permute-done
  52.9 0.0 collective-permute-done.1
  52.9 10.0 %collective-permute-done.2 = bf16[4,48,512]{2,1,0:T(8,128)(2,1)S(1)} collective-permute-done((bf16[4,48,512]{2,1,0:T(8,128)(2,1)S(1)}, bf16[4,48,512]{2,1,0:T(8,128)(2,1)S(1)}, u32[]{:S(2)}, u32[]{:S(2)}) %collective-permute-start.2) | collective-permute-done | bytes 196640 | tf_op jit(solution)/shard_map/w_four/ppermute | solution.py:23
  62.9 0.9 pad_maximum_fusion
  63.9 1.9 %collective-permute-start.3 = (bf16[8,48,512]{2,1,0:T(8,128)(2,1)}, bf16[8,48,512]{2,1,0:T(8,128)(2,1)}, u32[]{:S(2)}, u32[]{:S(2)}) collective-permute-start(bf16[8,48,512]{2,1,0:T(8,128)(2,1)} %get-tuple-element.35), channel_id=1, source_target_pairs={{0,128},{128,256},{256,384},{384,512},{512,640},{640,768},{768,896... | collective-permute-start | bytes 1179656 | tf_op jit(solution)/shard_map/w_up2/ppermute | solution.py:23
  65.8 0.0 copy-start.3
  66.5 3.9 %collective-permute-start.4 = (bf16[8,48,512]{2,1,0:T(8,128)(2,1)}, bf16[8,48,512]{2,1,0:T(8,128)(2,1)S(1)}, u32[]{:S(2)}, u32[]{:S(2)}) collective-permute-start(bf16[8,48,512]{2,1,0:T(8,128)(2,1)} %get-tuple-element.34), channel_id=1, source_target_pairs={{0,896},{128,0},{256,128},{384,256},{512,384},{640,512},{768,640},... | collective-permute-start | bytes 1179656 | tf_op jit(solution)/shard_map/w_down2/ppermute | solution.py:23
  70.5 1.9 %collective-permute-start.5 = (bf16[16,48,512]{2,1,0:T(8,128)(2,1)S(1)}, bf16[16,48,512]{2,1,0:T(8,128)(2,1)}, u32[]{:S(2)}, u32[]{:S(2)}) collective-permute-start(bf16[16,48,512]{2,1,0:T(8,128)(2,1)S(1)} %constant_dynamic-update-slice_fusion.own0), channel_id=1, source_target_pairs={{0,16},{16,0},{1,17},{17,1},{2,18},{18,2},{3,19},{19,3},{4,20},{20... | collective-permute-start | bytes 2359304 | tf_op jit(solution)/shard_map/ppermute | solution.py:27
  72.4 2.3 %collective-permute-done.3 = bf16[8,48,512]{2,1,0:T(8,128)(2,1)} collective-permute-done((bf16[8,48,512]{2,1,0:T(8,128)(2,1)}, bf16[8,48,512]{2,1,0:T(8,128)(2,1)}, u32[]{:S(2)}, u32[]{:S(2)}) %collective-permute-start.3) | collective-permute-done | bytes 393248 | tf_op jit(solution)/shard_map/w_up2/ppermute | solution.py:23
  74.7 1.0 constant_dynamic-update-slice_fusion.5
  75.8 2.7 %collective-permute-done.4 = bf16[8,48,512]{2,1,0:T(8,128)(2,1)S(1)} collective-permute-done((bf16[8,48,512]{2,1,0:T(8,128)(2,1)}, bf16[8,48,512]{2,1,0:T(8,128)(2,1)S(1)}, u32[]{:S(2)}, u32[]{:S(2)}) %collective-permute-start.4) | collective-permute-done | bytes 393248 | tf_op jit(solution)/shard_map/w_down2/ppermute | solution.py:23
  78.5 1.9 %collective-permute-start.6 = (bf16[16,48,512]{2,1,0:T(8,128)(2,1)S(1)}, bf16[16,48,512]{2,1,0:T(8,128)(2,1)}, u32[]{:S(2)}, u32[]{:S(2)}) collective-permute-start(bf16[16,48,512]{2,1,0:T(8,128)(2,1)S(1)} %constant_dynamic-update-slice_fusion.4.own1), channel_id=1, source_target_pairs={{0,16},{16,0},{1,17},{17,1},{2,18},{18,2},{3,19},{19,3},{4,20},{20... | collective-permute-start | bytes 2359304 | tf_op jit(solution)/shard_map/ppermute | solution.py:27
  80.4 0.0 copy-done
  80.5 0.0 copy-done.3
  80.6 0.1 select_reduce_fusion.to_ref
  80.7 0.0 all-to-all-done
  80.7 2.3 %shard_map.86.x_ref = bf16[256,3072]{1,0:T(8,128)(2,1)S(1)} custom-call(bf16[256,3072]{1,0:T(8,128)(2,1)S(1)} %bitcast.17, f32[3,3072]{1,0:T(4,128)S(1)} %bitcast.20), custom_call_target="tpu_custom_call" | custom-call | flops 9437184 | bytes 3145728 | tf_op jit(solution)/shard_map/pallas_call | solution.py:60
  83.0 0.0 collective-permute-done.5.other0
  83.0 0.0 collective-permute-done.6.other1
  83.0 4.6 %shard_map.87 = (bf16[64,3072]{1,0:T(8,128)(2,1)S(1)}, bf16[64,3072]{1,0:T(8,128)(2,1)}, bf16[64,3072]{1,0:T(8,128)(2,1)}, bf16[64,3072]{1,0:T(8,128)(2,1)}) custom-call(s32[64]{0:T(128)S(1)} %select_reduce_fusion.to_ref, s32[16]{0:T(128)S(1)} %fusion.9.row_ref, bf16[256,3072]{1,0:T(8,128)(2,1)S(1)} %shard_map.86.x_ref, ...), custom_call_target="tpu_custom_call" | custom-call | flops 805306368 | bytes 6291456 | tf_op jit(solution)/shard_map/pallas_call | solution.py:110
  87.6 0.0 copy-start.1
  87.6 0.0 copy-start.2
  87.6 5.4 %collective-permute-start.7 = (bf16[64,3072]{1,0:T(8,128)(2,1)}, bf16[64,3072]{1,0:T(8,128)(2,1)S(1)}, u32[]{:S(2)}, u32[]{:S(2)}) collective-permute-start(bf16[64,3072]{1,0:T(8,128)(2,1)} %get-tuple-element.21), channel_id=1, source_target_pairs={{0,2},{1,3},{2,0},{3,1},{4,6},{5,7},{6,4},{7,5},{8,10},{9,11},{10,... | collective-permute-start | bytes 1179656 | tf_op jit(solution)/shard_map/ppermute | solution.py:232
  93.1 2.5 %collective-permute-start.8 = (bf16[64,3072]{1,0:T(8,128)(2,1)}, bf16[64,3072]{1,0:T(8,128)(2,1)S(1)}, u32[]{:S(2)}, u32[]{:S(2)}) collective-permute-start(bf16[64,3072]{1,0:T(8,128)(2,1)} %get-tuple-element.22), channel_id=1, source_target_pairs={{0,1},{1,2},{2,3},{3,0},{4,5},{5,6},{6,7},{7,4},{8,9},{9,10},{10,1... | collective-permute-start | bytes 1179656 | tf_op jit(solution)/shard_map/ppermute | solution.py:232
  95.6 4.6 %collective-permute-start.9 = (bf16[64,3072]{1,0:T(8,128)(2,1)}, bf16[64,3072]{1,0:T(8,128)(2,1)S(1)}, u32[]{:S(2)}, u32[]{:S(2)}) collective-permute-start(bf16[64,3072]{1,0:T(8,128)(2,1)} %get-tuple-element.23), channel_id=1, source_target_pairs={{0,3},{1,0},{2,1},{3,2},{4,7},{5,4},{6,5},{7,6},{8,11},{9,8},{10,9... | collective-permute-start | bytes 1179656 | tf_op jit(solution)/shard_map/ppermute | solution.py:232
  100.1 3.2 %collective-permute-done.7.refs_1_ = bf16[64,3072]{1,0:T(8,128)(2,1)S(1)} collective-permute-done((bf16[64,3072]{1,0:T(8,128)(2,1)}, bf16[64,3072]{1,0:T(8,128)(2,1)S(1)}, u32[]{:S(2)}, u32[]{:S(2)}) %collective-permute-start.7) | collective-permute-done | bytes 393248 | tf_op jit(solution)/shard_map/ppermute | solution.py:232
  103.4 8.1 %collective-permute-done.8.refs_2_ = bf16[64,3072]{1,0:T(8,128)(2,1)S(1)} collective-permute-done((bf16[64,3072]{1,0:T(8,128)(2,1)}, bf16[64,3072]{1,0:T(8,128)(2,1)S(1)}, u32[]{:S(2)}, u32[]{:S(2)}) %collective-permute-start.8) | collective-permute-done | bytes 393248 | tf_op jit(solution)/shard_map/ppermute | solution.py:232
  111.5 0.3 collective-permute-done.9.refs_3_
  111.7 0.2 shard_map.88
  111.9 4.3 %collective-permute-start.10 = (bf16[16,3072]{1,0:T(8,128)(2,1)S(1)}, bf16[16,3072]{1,0:T(8,128)(2,1)S(1)}, u32[]{:S(2)}, u32[]{:S(2)}) collective-permute-start(bf16[16,3072]{1,0:T(8,128)(2,1)S(1)} %get-tuple-element.25), channel_id=1, source_target_pairs={{0,8},{4,12},{8,0},{12,4},{1,9},{5,13},{9,1},{13,5},{2,10},{6,14},... | collective-permute-start | bytes 294920 | tf_op jit(solution)/shard_map/ppermute | solution.py:236
  116.2 3.4 %collective-permute-start.11 = (bf16[16,3072]{1,0:T(8,128)(2,1)S(1)}, bf16[16,3072]{1,0:T(8,128)(2,1)S(1)}, u32[]{:S(2)}, u32[]{:S(2)}) collective-permute-start(bf16[16,3072]{1,0:T(8,128)(2,1)S(1)} %get-tuple-element.26), channel_id=1, source_target_pairs={{0,12},{4,8},{8,4},{12,0},{1,13},{5,9},{9,5},{13,1},{2,14},{6,10},... | collective-permute-start | bytes 294920 | tf_op jit(solution)/shard_map/ppermute | solution.py:236
  119.6 1.9 %collective-permute-start.12 = (bf16[16,3072]{1,0:T(8,128)(2,1)S(1)}, bf16[16,3072]{1,0:T(8,128)(2,1)S(1)}, u32[]{:S(2)}, u32[]{:S(2)}) collective-permute-start(bf16[16,3072]{1,0:T(8,128)(2,1)S(1)} %get-tuple-element.27), channel_id=1, source_target_pairs={{0,4},{4,0},{8,12},{12,8},{1,5},{5,1},{9,13},{13,9},{2,6},{6,2},{1... | collective-permute-start | bytes 294920 | tf_op jit(solution)/shard_map/ppermute | solution.py:236
  121.6 0.0 collective-permute-done.10.p1
  121.6 3.0 %collective-permute-done.11.p2 = bf16[16,3072]{1,0:T(8,128)(2,1)S(1)} collective-permute-done((bf16[16,3072]{1,0:T(8,128)(2,1)S(1)}, bf16[16,3072]{1,0:T(8,128)(2,1)S(1)}, u32[]{:S(2)}, u32[]{:S(2)}) %collective-permute-start.11) | collective-permute-done | bytes 98336 | tf_op jit(solution)/shard_map/ppermute | solution.py:236
  124.6 2.0 %collective-permute-done.12.p3 = bf16[16,3072]{1,0:T(8,128)(2,1)S(1)} collective-permute-done((bf16[16,3072]{1,0:T(8,128)(2,1)S(1)}, bf16[16,3072]{1,0:T(8,128)(2,1)S(1)}, u32[]{:S(2)}, u32[]{:S(2)}) %collective-permute-start.12) | collective-permute-done | bytes 98336 | tf_op jit(solution)/shard_map/ppermute | solution.py:236
  126.6 0.0 copy-done.1
  126.6 0.0 copy-done.2
  126.6 0.7 shard_map.89
  127.4 14.0 %all_to_all.10 = f32[16,1,128]{2,1,0:T(1,128)S(1)} all-to-all(f32[16,1,128]{2,1,0:T(1,128)S(1)} %get-tuple-element.31), channel_id=1, replica_groups=mesh['y'=8,'zh'=4,'core'=2,'zl'=4,'x'=4] {'zl','x'}, dimensions={0} | all-to-all | bytes 16384 | tf_op jit(solution)/shard_map/all_to_all | solution.py:240
  141.3 0.6 slice_reduce_fusion
  (10 shorter events, 0.2 us)
Async XLA Ops:
  0.6 79.8 %copy-start = (f32[8,3,3072]{2,0,1:T(8,128)S(1)}, f32[8,3,3072]{2,0,1:T(8,128)}, u32[]{:S(2)}) copy-start(f32[8,3,3072]{2,0,1:T(8,128)} %param.11) | copy-start | bytes 884740
  33.9 46.7 %all-to-all-start = ((bf16[16,16,3072]{2,1,0:T(8,128)(2,1)}), bf16[16,16,3072]{2,1,0:T(8,128)(2,1)S(1)}, u32[]{:S(2)}, u32[]{:S(2)}) async-start(bf16[16,16,3072]{2,1,0:T(8,128)(2,1)} %broadcast_in_dim.38), calls=%async_computation | async-start | bytes 3145728 | tf_op jit(solution)/shard_map/all_to_all | solution.py:18
  41.5 11.4 %collective-permute-start = (bf16[4,48,512]{2,1,0:T(8,128)(2,1)S(1)}, bf16[4,48,512]{2,1,0:T(8,128)(2,1)S(1)}, u32[]{:S(2)}, u32[]{:S(2)}) collective-permute-start(bf16[4,48,512]{2,1,0:T(8,128)(2,1)S(1)} %bitcast.22), channel_id=1, source_target_pairs={{0,128},{128,256},{256,384},{384,512},{512,640},{640,768},{768,896... | collective-permute-start | bytes 589832 | tf_op jit(solution)/shard_map/w_up/ppermute | solution.py:23
  43.5 9.4 %collective-permute-start.1 = (bf16[4,48,512]{2,1,0:T(8,128)(2,1)S(1)}, bf16[4,48,512]{2,1,0:T(8,128)(2,1)S(1)}, u32[]{:S(2)}, u32[]{:S(2)}) collective-permute-start(bf16[4,48,512]{2,1,0:T(8,128)(2,1)S(1)} %bitcast.23), channel_id=1, source_target_pairs={{0,896},{128,0},{256,128},{384,256},{512,384},{640,512},{768,640},... | collective-permute-start | bytes 589832 | tf_op jit(solution)/shard_map/w_down/ppermute | solution.py:23
  47.4 15.5 %collective-permute-start.2 = (bf16[4,48,512]{2,1,0:T(8,128)(2,1)S(1)}, bf16[4,48,512]{2,1,0:T(8,128)(2,1)S(1)}, u32[]{:S(2)}, u32[]{:S(2)}) collective-permute-start(bf16[4,48,512]{2,1,0:T(8,128)(2,1)S(1)} %bitcast.24), channel_id=1, source_target_pairs={{0,512},{128,640},{256,768},{384,896},{512,0},{640,128},{768,256},... | collective-permute-start | bytes 589832 | tf_op jit(solution)/shard_map/w_four/ppermute | solution.py:23
  63.9 10.9 %collective-permute-start.3 = (bf16[8,48,512]{2,1,0:T(8,128)(2,1)}, bf16[8,48,512]{2,1,0:T(8,128)(2,1)}, u32[]{:S(2)}, u32[]{:S(2)}) collective-permute-start(bf16[8,48,512]{2,1,0:T(8,128)(2,1)} %get-tuple-element.35), channel_id=1, source_target_pairs={{0,128},{128,256},{256,384},{384,512},{512,640},{640,768},{768,896... | collective-permute-start | bytes 1179656 | tf_op jit(solution)/shard_map/w_up2/ppermute | solution.py:23
  65.8 14.7 %copy-start.3 = (s32[64]{0:T(128)S(1)}, s32[64]{0:T(128)}, u32[]{:S(2)}) copy-start(s32[64]{0:T(128)} %param.10) | copy-start | bytes 772
  66.5 12.0 %collective-permute-start.4 = (bf16[8,48,512]{2,1,0:T(8,128)(2,1)}, bf16[8,48,512]{2,1,0:T(8,128)(2,1)S(1)}, u32[]{:S(2)}, u32[]{:S(2)}) collective-permute-start(bf16[8,48,512]{2,1,0:T(8,128)(2,1)} %get-tuple-element.34), channel_id=1, source_target_pairs={{0,896},{128,0},{256,128},{384,256},{512,384},{640,512},{768,640},... | collective-permute-start | bytes 1179656 | tf_op jit(solution)/shard_map/w_down2/ppermute | solution.py:23
  70.5 12.5 %collective-permute-start.5 = (bf16[16,48,512]{2,1,0:T(8,128)(2,1)S(1)}, bf16[16,48,512]{2,1,0:T(8,128)(2,1)}, u32[]{:S(2)}, u32[]{:S(2)}) collective-permute-start(bf16[16,48,512]{2,1,0:T(8,128)(2,1)S(1)} %constant_dynamic-update-slice_fusion.own0), channel_id=1, source_target_pairs={{0,16},{16,0},{1,17},{17,1},{2,18},{18,2},{3,19},{19,3},{4,20},{20... | collective-permute-start | bytes 2359304 | tf_op jit(solution)/shard_map/ppermute | solution.py:27
  78.5 4.5 %collective-permute-start.6 = (bf16[16,48,512]{2,1,0:T(8,128)(2,1)S(1)}, bf16[16,48,512]{2,1,0:T(8,128)(2,1)}, u32[]{:S(2)}, u32[]{:S(2)}) collective-permute-start(bf16[16,48,512]{2,1,0:T(8,128)(2,1)S(1)} %constant_dynamic-update-slice_fusion.4.own1), channel_id=1, source_target_pairs={{0,16},{16,0},{1,17},{17,1},{2,18},{18,2},{3,19},{19,3},{4,20},{20... | collective-permute-start | bytes 2359304 | tf_op jit(solution)/shard_map/ppermute | solution.py:27
  87.6 39.0 %copy-start.1 = (bf16[1,16,3072]{2,1,0:T(8,128)(2,1)S(1)}, bf16[1,16,3072]{2,1,0:T(8,128)(2,1)}, u32[]{:S(2)}) copy-start(bf16[1,16,3072]{2,1,0:T(8,128)(2,1)} %param.7) | copy-start | bytes 294916
  87.6 39.0 %copy-start.2 = (bf16[1,16,3072]{2,1,0:T(8,128)(2,1)S(1)}, bf16[1,16,3072]{2,1,0:T(8,128)(2,1)}, u32[]{:S(2)}) copy-start(bf16[1,16,3072]{2,1,0:T(8,128)(2,1)} %param.8) | copy-start | bytes 294916
  87.6 15.8 %collective-permute-start.7 = (bf16[64,3072]{1,0:T(8,128)(2,1)}, bf16[64,3072]{1,0:T(8,128)(2,1)S(1)}, u32[]{:S(2)}, u32[]{:S(2)}) collective-permute-start(bf16[64,3072]{1,0:T(8,128)(2,1)} %get-tuple-element.21), channel_id=1, source_target_pairs={{0,2},{1,3},{2,0},{3,1},{4,6},{5,7},{6,4},{7,5},{8,10},{9,11},{10,... | collective-permute-start | bytes 1179656 | tf_op jit(solution)/shard_map/ppermute | solution.py:232
  93.1 18.4 %collective-permute-start.8 = (bf16[64,3072]{1,0:T(8,128)(2,1)}, bf16[64,3072]{1,0:T(8,128)(2,1)S(1)}, u32[]{:S(2)}, u32[]{:S(2)}) collective-permute-start(bf16[64,3072]{1,0:T(8,128)(2,1)} %get-tuple-element.22), channel_id=1, source_target_pairs={{0,1},{1,2},{2,3},{3,0},{4,5},{5,6},{6,7},{7,4},{8,9},{9,10},{10,1... | collective-permute-start | bytes 1179656 | tf_op jit(solution)/shard_map/ppermute | solution.py:232
  95.6 16.2 %collective-permute-start.9 = (bf16[64,3072]{1,0:T(8,128)(2,1)}, bf16[64,3072]{1,0:T(8,128)(2,1)S(1)}, u32[]{:S(2)}, u32[]{:S(2)}) collective-permute-start(bf16[64,3072]{1,0:T(8,128)(2,1)} %get-tuple-element.23), channel_id=1, source_target_pairs={{0,3},{1,0},{2,1},{3,2},{4,7},{5,4},{6,5},{7,6},{8,11},{9,8},{10,9... | collective-permute-start | bytes 1179656 | tf_op jit(solution)/shard_map/ppermute | solution.py:232
  111.9 9.7 %collective-permute-start.10 = (bf16[16,3072]{1,0:T(8,128)(2,1)S(1)}, bf16[16,3072]{1,0:T(8,128)(2,1)S(1)}, u32[]{:S(2)}, u32[]{:S(2)}) collective-permute-start(bf16[16,3072]{1,0:T(8,128)(2,1)S(1)} %get-tuple-element.25), channel_id=1, source_target_pairs={{0,8},{4,12},{8,0},{12,4},{1,9},{5,13},{9,1},{13,5},{2,10},{6,14},... | collective-permute-start | bytes 294920 | tf_op jit(solution)/shard_map/ppermute | solution.py:236
  116.2 8.4 %collective-permute-start.11 = (bf16[16,3072]{1,0:T(8,128)(2,1)S(1)}, bf16[16,3072]{1,0:T(8,128)(2,1)S(1)}, u32[]{:S(2)}, u32[]{:S(2)}) collective-permute-start(bf16[16,3072]{1,0:T(8,128)(2,1)S(1)} %get-tuple-element.26), channel_id=1, source_target_pairs={{0,12},{4,8},{8,4},{12,0},{1,13},{5,9},{9,5},{13,1},{2,14},{6,10},... | collective-permute-start | bytes 294920 | tf_op jit(solution)/shard_map/ppermute | solution.py:236
  119.6 7.0 %collective-permute-start.12 = (bf16[16,3072]{1,0:T(8,128)(2,1)S(1)}, bf16[16,3072]{1,0:T(8,128)(2,1)S(1)}, u32[]{:S(2)}, u32[]{:S(2)}) collective-permute-start(bf16[16,3072]{1,0:T(8,128)(2,1)S(1)} %get-tuple-element.27), channel_id=1, source_target_pairs={{0,4},{4,0},{8,12},{12,8},{1,5},{5,1},{9,13},{13,9},{2,6},{6,2},{1... | collective-permute-start | bytes 294920 | tf_op jit(solution)/shard_map/ppermute | solution.py:236

commit v5 on v4

v5 whole, which is shorter than its diff:
```python
import math

import jax
import jax.numpy as jnp
from jax import lax
from jax.experimental import pallas as pl
from jax.experimental.pallas import tpu as pltpu
from jax.sharding import Mesh, PartitionSpec as P


GROUP = ("y", "zh", "core")
TENSOR = ("zl", "x")
NY, NZH, NCORE, NZL, NX = 8, 4, 2, 4, 4
NT = (((1,), (1,)), ((), ()))


def shifted(x, by):
    return lax.ppermute(x, "y", [(i, (i + by) % NY) for i in range(NY)])


def swapped(x):
    return lax.ppermute(x, "core", [(0, 1), (1, 0)])


PLACE = (0, 2, 6, 5, 3, 7, 4, 1)


def around_y(x):
    below = shifted(x, 1)
    above = shifted(x, -1)
    across = shifted(x, 4)
    near = jnp.concatenate([x, below, above, across], axis=0)
    up = shifted(jnp.concatenate([below, across], axis=0), 1)
    down = shifted(jnp.concatenate([above, across], axis=0), -1)
    return near, jnp.concatenate([up, down], axis=0)


def norm_kernel(t_ref, x_ref, table_ref, o_ref):
    t = t_ref[0]
    x = x_ref[...].astype(jnp.float32)
    width = x.shape[1]
    centred = x - jnp.sum(x, axis=1, keepdims=True) / width
    variance = jnp.sum(centred * centred, axis=1, keepdims=True) / width
    normed = centred * lax.rsqrt(variance + 1e-06)
    shift, scale = table_ref[0, pl.ds(t, 1), :], table_ref[1, pl.ds(t, 1), :]
    modulated = (normed * (1.0 + scale) + shift).astype(jnp.bfloat16)
    for i in range(o_ref.shape[0]):
        o_ref[i] = modulated


def normalised_copies(t, tokens, table, copies):
    rows, width = tokens.shape
    vmem = pl.BlockSpec(memory_space=pltpu.VMEM)
    return pl.pallas_call(
        norm_kernel,
        out_shape=jax.ShapeDtypeStruct((copies, rows, width), jnp.bfloat16),
        in_specs=[pl.BlockSpec(memory_space=pltpu.SMEM), vmem, vmem],
        out_specs=vmem,
        compiler_params=pltpu.CompilerParams(vmem_limit_bytes=16 * 1024 * 1024),
        cost_estimate=pl.CostEstimate(
            flops=12 * rows * width, bytes_accessed=40 * rows * width, transcendentals=rows
        ),
    )(t, tokens, table)


def head_kernel(to_ref, row_ref, x_ref, own0, own1, other0, other1, *rest):
    outs, (w_ref, a_ref) = rest[:NX], rest[NX:]
    count, rows, columns = own0.shape
    width = x_ref.shape[1]
    hd = columns // 4
    for part, ref in enumerate((own0, own1, other0, other1)):
        for k in range(count):
            first = pl.multiple_of(to_ref[part * count + k] * rows, rows)
            w_ref[pl.ds(first, rows), :] = ref[k]

    qkv = jnp.dot(x_ref[...], w_ref[:, : 3 * hd], preferred_element_type=jnp.float32)
    qkv = qkv.astype(jnp.bfloat16)
    q, k, v = qkv[:, :hd], qkv[:, hd : 2 * hd], qkv[:, 2 * hd :]
    scores = lax.dot_general(q, k, NT, preferred_element_type=jnp.float32) / math.sqrt(hd)
    expo = jnp.exp(scores - jnp.max(scores, axis=1, keepdims=True))
    probs = (expo / jnp.sum(expo, axis=1, keepdims=True)).astype(jnp.bfloat16)
    attended = jnp.dot(probs, v, preferred_element_type=jnp.float32)
    a_ref[...] = attended.astype(jnp.bfloat16)
    blocks = row_ref.shape[0]
    tok = a_ref.shape[0] // blocks
    ordered = jnp.concatenate(
        [a_ref[pl.ds(pl.multiple_of(row_ref[i], tok), tok), :] for i in range(blocks)], axis=0
    )
    step = 512
    part = ordered.shape[0] // NX
    for c in range(0, width, step):
        w_out = w_ref[c : c + step, 3 * hd :]
        term = lax.dot_general(ordered, w_out, NT, preferred_element_type=jnp.float32)
        term = term.astype(jnp.bfloat16)
        for r, o_ref in enumerate(outs):
            o_ref[:, c : c + step] = term[r * part : (r + 1) * part]


def head_term(tokens, pieces, slots, first_rows):
    seq, width = tokens.shape
    smem = pl.BlockSpec(memory_space=pltpu.SMEM)
    vmem = pl.BlockSpec(memory_space=pltpu.VMEM)
    columns = pieces[0].shape[2]
    return pl.pallas_call(
        head_kernel,
        out_shape=[jax.ShapeDtypeStruct((seq // NX, width), jnp.bfloat16)] * NX,
        in_specs=[smem] * 2 + [vmem] * 5,
        out_specs=[vmem] * NX,
        scratch_shapes=[
            pltpu.VMEM((width, columns), jnp.bfloat16),
            pltpu.VMEM((seq, columns // 4), jnp.bfloat16),
        ],
        compiler_params=pltpu.CompilerParams(vmem_limit_bytes=40 * 1024 * 1024),
        cost_estimate=pl.CostEstimate(
            flops=2 * seq * width * columns,
            bytes_accessed=8 * seq * width,
            transcendentals=seq * seq,
        ),
    )(slots, first_rows, tokens, *pieces)


def sum_kernel(p0, p1, p2, p3, o_ref):
    step = 1024
    for c in range(0, o_ref.shape[1], step):
        here = slice(c, c + step)
        total = p0[:, here].astype(jnp.float32)
        for ref in (p1, p2, p3):
            total = total + ref[:, here].astype(jnp.float32)
        o_ref[:, here] = total.astype(o_ref.dtype)


def summed(blocks):
    rows, width = blocks[0].shape
    vmem = pl.BlockSpec(memory_space=pltpu.VMEM)
    return pl.pallas_call(
        sum_kernel,
        out_shape=jax.ShapeDtypeStruct((rows, width), jnp.bfloat16),
        in_specs=[vmem] * NX,
        out_specs=vmem,
        compiler_params=pltpu.CompilerParams(vmem_limit_bytes=16 * 1024 * 1024),
        cost_estimate=pl.CostEstimate(
            flops=4 * rows * width, bytes_accessed=10 * rows * width, transcendentals=0
        ),
    )(*blocks)


def mean_kernel(t_ref, parts_ref, latent_ref, stored_ref, table_ref, mean_ref, sum_ref):
    t = t_ref[0]
    dt = (t.astype(jnp.float32) + 1.0) / table_ref.shape[1]
    rows, width = latent_ref.shape
    step = 512
    squares = jnp.zeros((rows, step), jnp.float32)
    for c in range(0, width, step):
        here = slice(c, c + step)
        proj = parts_ref[0, :, here].astype(jnp.float32)
        for k in range(1, parts_ref.shape[0]):
            proj = proj + parts_ref[k, :, here].astype(jnp.float32)
        latent = latent_ref[:, here].astype(jnp.float32)
        mean = latent - dt * (latent + table_ref[2, pl.ds(t, 1), here] * proj)
        mean_ref[:, here] = mean.astype(jnp.bfloat16)
        residual = stored_ref[:, here].astype(jnp.float32) - mean
        squares = squares + residual * residual
    total = jnp.sum(squares, axis=(0, 1), keepdims=True)
    sum_ref[...] = jnp.broadcast_to(total[None], sum_ref.shape)


def mean_and_squares(t, parts, latent, stored, table):
    rows, width = latent.shape
    vmem = pl.BlockSpec(memory_space=pltpu.VMEM)
    return pl.pallas_call(
        mean_kernel,
        out_shape=(
            jax.ShapeDtypeStruct((rows, width), jnp.bfloat16),
            jax.ShapeDtypeStruct((NZL * NX, 1, 128), jnp.float32),
        ),
        in_specs=[pl.BlockSpec(memory_space=pltpu.SMEM)] + [vmem] * 4,
        out_specs=(vmem, vmem),
        compiler_params=pltpu.CompilerParams(vmem_limit_bytes=16 * 1024 * 1024),
        cost_estimate=pl.CostEstimate(
            flops=16 * rows * width, bytes_accessed=16 * rows * width, transcendentals=0
        ),
    )(t, parts, latent, stored, table)


def one_device(latents, stored_sample, timestep, owner_map, mod_table, qkv_weight, out_weight):
    _, tok_local, width = latents.shape
    seq_len = tok_local * NZL * NX
    table = jnp.swapaxes(mod_table, 0, 1)
    time_float = timestep[0].astype(jnp.float32)
    sigma = 0.3 + 0.1 * time_float
    spread = 2.0 * sigma * sigma * seq_len * width
    offset = jnp.log(sigma) + 0.5 * math.log(2.0 * math.pi)

    weights = jnp.concatenate([qkv_weight, out_weight.T], axis=1)
    plane = lax.all_gather(weights, "zh", tiled=False)
    sent, plane = lax.optimization_barrier((latents[0], plane))
    copies = normalised_copies(timestep, sent, table, NZL * NX)
    tokens = lax.all_to_all(copies, TENSOR, split_axis=0, concat_axis=0, tiled=True)
    near, far = around_y(plane)
    pieces = (near, far, swapped(near), swapped(far))

    ahead = (owner_map // (NZH * NCORE) - lax.axis_index("y")) % NY
    place = jnp.zeros_like(ahead)
    for distance, where in enumerate(PLACE):
        place = jnp.where(ahead == distance, where, place)
    side = (owner_map % NCORE != lax.axis_index("core")).astype(jnp.int32)
    at = (side * NY + place) * NZH + (owner_map // NCORE) % NZH
    slices = jnp.arange(at.shape[0], dtype=jnp.int32)
    slots = jnp.sum(jnp.where(at[None, :] == slices[:, None], slices[None, :], 0), axis=1)

    turn = jnp.arange(NX * NZL, dtype=jnp.int32)
    to_x = (lax.axis_index("x") + turn // NZL) % NX
    first_rows = ((turn % NZL * NX + to_x) * tok_local).astype(jnp.int32)

    terms = head_term(tokens.reshape(seq_len, width), pieces, slots, first_rows)
    by_x = [terms[0]] + [
        lax.ppermute(terms[r], "x", [(i, (i + r) % NX) for i in range(NX)]) for r in (2, 1, 3)
    ]
    some, latent, stored, table, spread, offset = lax.optimization_barrier(
        (summed(by_x), latents[0], stored_sample[0], table, spread, offset)
    )
    parts = lax.all_to_all(
        some.reshape(NZL, tok_local, width), "zl", split_axis=0, concat_axis=0, tiled=True
    )
    mean, squares = mean_and_squares(timestep, parts, latent, stored, table)
    mean, squares, spread, offset = lax.optimization_barrier((mean, squares, spread, offset))
    squares = lax.all_to_all(squares, TENSOR, split_axis=0, concat_axis=0, tiled=True)
    log_prob = -jnp.sum(squares[:, :, :1]) / spread - offset
    return (mean[None], log_prob[None])


def solution(mesh):
    fine = Mesh(mesh.devices.reshape(NY, NZH, NCORE, NZL, NX), GROUP + TENSOR)
    in_specs = (
        P(GROUP, TENSOR, None),
        P(GROUP, TENSOR, None),
        P(GROUP),
        P(),
        P(),
        P(GROUP, TENSOR),
        P(TENSOR, GROUP),
    )
    out_specs = (P(GROUP, TENSOR, None), P(GROUP))
    return jax.shard_map(one_device, mesh=fine, in_specs=in_specs, out_specs=out_specs, check_vma=False)
```

time: 145 us -> 144 us (level)
  blocking collectives: 44.2 us -> 59.4 us
  starting transfers between devices: 50.7 us -> 41.1 us
  waiting for transfers between devices: 31.6 us -> 29.2 us
  local copies, waits for them, and re-layouts: 3.44 us -> 1.98 us
    all_to_all x1 -> x2, blocking collectives: 14 us -> 29.2 us  [the longest x1 16.2 us: one_device(): lax.all_to_all(some.reshape(NZL, tok_local, width), 'zl', split_axis=0, c...]
    ppermute x6 -> x3, starting transfers between devices: 22.1 us -> 12.5 us  [one_device(): lax.ppermute(terms[r], 'x', [(i, (i + r) % NX) for i in range(NX)])]
    ppermute x6 -> x3, waiting for transfers between devices: 16.6 us -> 11.2 us  [one_device(): lax.ppermute(terms[r], 'x', [(i, (i + r) % NX) for i in range(NX)])]
    broadcast_in_dim x1 -> x0, local copies, waits for them, and re-layouts: 2.24 us -> none  [to_all(): copies = jnp.broadcast_to(x, (lax.axis_size(axis), *x.shape))]
    ppermute x2, waiting for transfers between devices: 0.01 us -> 2.2 us  [swapped(): return lax.ppermute(x, 'core', [(0, 1), (1, 0)])]
  transfers between devices with their start and end apart: 14 -> 11, of which waited for: 8 -> 7; matrix products, arithmetic and copies ran while one was open for 2% -> 0% of each run, Pallas kernels for 2% -> 0%
where the time goes in v5:
time: 144 us
  blocking collectives  59.4 us (41%)
  starting transfers between devices  41.1 us (29%)
  waiting for transfers between devices  29.2 us (20%)
  Pallas kernels  7.07 us (5%)
  between operations  3.36 us (2%)
  local copies, waits for them, and re-layouts  1.98 us (1%)
  other arithmetic  1.62 us (1%)
    all_gather x1, blocking collectives, one_device(): plane = lax.all_gather(weights, 'zh', tiled=False)  30.2 us
    ppermute x5, starting transfers between devices, shifted(): return lax.ppermute(x, 'y', [(i, (i + by) % NY) for i in range(NY)])  17.2 us
    all_to_all x1, blocking collectives, one_device(): lax.all_to_all(some.reshape(NZL, tok_local, width), 'zl', split_axis=0, c...  16.2 us
    ppermute x5, waiting for transfers between devices, shifted(): return lax.ppermute(x, 'y', [(i, (i + by) % NY) for i in range(NY)])  15.8 us
    all_to_all x1, blocking collectives, one_device(): lax.all_to_all(squares, TENSOR, split_axis=0, concat_axis=0, tiled=True)  13 us
    ppermute x3, starting transfers between devices, one_device(): lax.ppermute(terms[r], 'x', [(i, (i + r) % NX) for i in range(NX)])  12.5 us
    ppermute x3, waiting for transfers between devices, one_device(): lax.ppermute(terms[r], 'x', [(i, (i + r) % NX) for i in range(NX)])  11.2 us
    all_to_all x1, starting transfers between devices, one_device(): lax.all_to_all(copies, TENSOR, split_axis=0, concat_axis=0, tiled=True)  7.59 us
  transfers between devices with their start and end apart: 11, of which 7 were waited for; matrix products, arithmetic and copies ran while one was open for 0% of the time, Pallas kernels for 0%

profile of v5, /device:TPU:56, one launch (start us, length us, event | category | flops | bytes accessed | tf_op | source)
XLA Modules:
  0.0 143.8 jit_solution(3829575608728257096)
XLA Ops:
  1.3 0.8 pad_maximum_fusion.2
  2.1 30.2 %all-gather = bf16[192,512]{1,0:T(8,128)(2,1)S(1)} all-gather(bf16[48,512]{1,0:T(8,128)(2,1)S(1)} %pad_maximum_fusion.2), channel_id=2, replica_groups=mesh['y'=8,'zh'=4,'core'=2,'zl'=4,'x'=4] {'zh'}, dimensions={0}, use_global_device_ids=true | all-gather | bytes 245760 | tf_op jit(solution)/shard_map/all_gather | solution.py:195
  32.3 0.0 copy-start
  32.3 1.0 copy-done
  33.3 0.0 copy-start.2
  33.3 0.9 copy-done.2
  34.1 1.5 %shard_map.86 = bf16[16,16,3072]{2,1,0:T(8,128)(2,1)} custom-call(s32[1]{0:T(128)S(6)} %copy.13.t_ref, bf16[16,3072]{1,0:T(8,128)(2,1)S(1)} %bitcast.14, f32[3,8,3072]{2,1,0:T(8,128)S(1)} %bitcast.12), custom_call_target="tpu_custom_call" | custom-call | flops 589824 | bytes 1966080 | tf_op jit(solution)/shard_map/pallas_call | solution.py:54
  35.7 7.6 %all-to-all-start = ((bf16[16,16,3072]{2,1,0:T(8,128)(2,1)}), bf16[16,16,3072]{2,1,0:T(8,128)(2,1)S(1)}, u32[]{:S(2)}, u32[]{:S(2)}) async-start(bf16[16,16,3072]{2,1,0:T(8,128)(2,1)} %shard_map.86), calls=%async_computation | async-start | bytes 3145728 | tf_op jit(solution)/shard_map/all_to_all | solution.py:198
  43.3 1.9 %collective-permute-start = (bf16[4,48,512]{2,1,0:T(8,128)(2,1)S(1)}, bf16[4,48,512]{2,1,0:T(8,128)(2,1)S(1)}, u32[]{:S(2)}, u32[]{:S(2)}) collective-permute-start(bf16[4,48,512]{2,1,0:T(8,128)(2,1)S(1)} %bitcast.17), channel_id=1, source_target_pairs={{0,128},{128,256},{256,384},{384,512},{512,640},{640,768},{768,896... | collective-permute-start | bytes 589832 | tf_op jit(solution)/shard_map/ppermute | solution.py:18
  45.2 3.9 %collective-permute-start.1 = (bf16[4,48,512]{2,1,0:T(8,128)(2,1)S(1)}, bf16[4,48,512]{2,1,0:T(8,128)(2,1)S(1)}, u32[]{:S(2)}, u32[]{:S(2)}) collective-permute-start(bf16[4,48,512]{2,1,0:T(8,128)(2,1)S(1)} %bitcast.18), channel_id=1, source_target_pairs={{0,896},{128,0},{256,128},{384,256},{512,384},{640,512},{768,640},... | collective-permute-start | bytes 589832 | tf_op jit(solution)/shard_map/ppermute | solution.py:18
  49.1 5.5 %collective-permute-start.2 = (bf16[4,48,512]{2,1,0:T(8,128)(2,1)S(1)}, bf16[4,48,512]{2,1,0:T(8,128)(2,1)S(1)}, u32[]{:S(2)}, u32[]{:S(2)}) collective-permute-start(bf16[4,48,512]{2,1,0:T(8,128)(2,1)S(1)} %bitcast.19), channel_id=1, source_target_pairs={{0,512},{128,640},{256,768},{384,896},{512,0},{640,128},{768,256},... | collective-permute-start | bytes 589832 | tf_op jit(solution)/shard_map/ppermute | solution.py:18
  54.6 0.0 collective-permute-done
  54.6 0.0 collective-permute-done.1
  54.6 10.0 %collective-permute-done.2 = bf16[4,48,512]{2,1,0:T(8,128)(2,1)S(1)} collective-permute-done((bf16[4,48,512]{2,1,0:T(8,128)(2,1)S(1)}, bf16[4,48,512]{2,1,0:T(8,128)(2,1)S(1)}, u32[]{:S(2)}, u32[]{:S(2)}) %collective-permute-start.2) | collective-permute-done | bytes 196640 | tf_op jit(solution)/shard_map/ppermute | solution.py:18
  64.6 0.1 pad_maximum_fusion
  64.7 0.0 copy-start.5
  64.7 1.9 %collective-permute-start.3 = (bf16[8,48,512]{2,1,0:T(8,128)(2,1)S(1)}, bf16[8,48,512]{2,1,0:T(8,128)(2,1)S(1)}, u32[]{:S(2)}, u32[]{:S(2)}) collective-permute-start(bf16[8,48,512]{2,1,0:T(8,128)(2,1)S(1)} %get-tuple-element.39), channel_id=1, source_target_pairs={{0,128},{128,256},{256,384},{384,512},{512,640},{640,768},{768,896... | collective-permute-start | bytes 1179656 | tf_op jit(solution)/shard_map/ppermute | solution.py:18
  66.7 3.9 %collective-permute-start.4 = (bf16[8,48,512]{2,1,0:T(8,128)(2,1)S(1)}, bf16[8,48,512]{2,1,0:T(8,128)(2,1)S(1)}, u32[]{:S(2)}, u32[]{:S(2)}) collective-permute-start(bf16[8,48,512]{2,1,0:T(8,128)(2,1)S(1)} %get-tuple-element.38), channel_id=1, source_target_pairs={{0,896},{128,0},{256,128},{384,256},{512,384},{640,512},{768,640},... | collective-permute-start | bytes 1179656 | tf_op jit(solution)/shard_map/ppermute | solution.py:18
  70.7 1.9 %collective-permute-start.5 = (bf16[16,48,512]{2,1,0:T(8,128)(2,1)S(1)}, bf16[16,48,512]{2,1,0:T(8,128)(2,1)}, u32[]{:S(2)}, u32[]{:S(2)}) collective-permute-start(bf16[16,48,512]{2,1,0:T(8,128)(2,1)S(1)} %constant_dynamic-update-slice_fusion.own0), channel_id=1, source_target_pairs={{0,16},{16,0},{1,17},{17,1},{2,18},{18,2},{3,19},{19,3},{4,20},{20... | collective-permute-start | bytes 2359304 | tf_op jit(solution)/shard_map/ppermute | solution.py:22
  72.6 2.7 %collective-permute-done.3 = bf16[8,48,512]{2,1,0:T(8,128)(2,1)S(1)} collective-permute-done((bf16[8,48,512]{2,1,0:T(8,128)(2,1)S(1)}, bf16[8,48,512]{2,1,0:T(8,128)(2,1)S(1)}, u32[]{:S(2)}, u32[]{:S(2)}) %collective-permute-start.3) | collective-permute-done | bytes 393248 | tf_op jit(solution)/shard_map/ppermute | solution.py:18
  75.3 3.1 %collective-permute-done.4 = bf16[8,48,512]{2,1,0:T(8,128)(2,1)S(1)} collective-permute-done((bf16[8,48,512]{2,1,0:T(8,128)(2,1)S(1)}, bf16[8,48,512]{2,1,0:T(8,128)(2,1)S(1)}, u32[]{:S(2)}, u32[]{:S(2)}) %collective-permute-start.4) | collective-permute-done | bytes 393248 | tf_op jit(solution)/shard_map/ppermute | solution.py:18
  78.5 1.9 %collective-permute-start.6 = (bf16[16,48,512]{2,1,0:T(8,128)(2,1)S(1)}, bf16[16,48,512]{2,1,0:T(8,128)(2,1)}, u32[]{:S(2)}, u32[]{:S(2)}) collective-permute-start(bf16[16,48,512]{2,1,0:T(8,128)(2,1)S(1)} %constant_dynamic-update-slice_fusion.4.own1), channel_id=1, source_target_pairs={{0,16},{16,0},{1,17},{17,1},{2,18},{18,2},{3,19},{19,3},{4,20},{20... | collective-permute-start | bytes 2359304 | tf_op jit(solution)/shard_map/ppermute | solution.py:22
  80.4 0.0 copy-done.5
  80.5 0.1 select_reduce_fusion.to_ref
  80.6 0.0 collective-permute-done.5.other0
  80.6 2.2 %collective-permute-done.6.other1 = bf16[16,48,512]{2,1,0:T(8,128)(2,1)} collective-permute-done((bf16[16,48,512]{2,1,0:T(8,128)(2,1)S(1)}, bf16[16,48,512]{2,1,0:T(8,128)(2,1)}, u32[]{:S(2)}, u32[]{:S(2)}) %collective-permute-start.6) | collective-permute-done | bytes 786464 | tf_op jit(solution)/shard_map/ppermute | solution.py:22
  82.8 0.0 all-to-all-done
  82.8 4.6 %shard_map.87 = (bf16[64,3072]{1,0:T(8,128)(2,1)S(1)}, bf16[64,3072]{1,0:T(8,128)(2,1)}, bf16[64,3072]{1,0:T(8,128)(2,1)}, bf16[64,3072]{1,0:T(8,128)(2,1)}) custom-call(s32[64]{0:T(128)S(1)} %select_reduce_fusion.to_ref, s32[16]{0:T(128)S(1)} %fusion.8.row_ref, bf16[256,3072]{1,0:T(8,128)(2,1)S(1)} %bitcast.10, ...), custom_call_target="tpu_custom_call" | custom-call | flops 805306368 | bytes 6291456 | tf_op jit(solution)/shard_map/pallas_call | solution.py:104
  87.4 0.0 copy-start.1
  87.4 0.0 copy-start.3
  87.4 0.0 copy-start.4
  87.4 5.5 %collective-permute-start.7 = (bf16[64,3072]{1,0:T(8,128)(2,1)}, bf16[64,3072]{1,0:T(8,128)(2,1)S(1)}, u32[]{:S(2)}, u32[]{:S(2)}) collective-permute-start(bf16[64,3072]{1,0:T(8,128)(2,1)} %get-tuple-element.23), channel_id=1, source_target_pairs={{0,2},{1,3},{2,0},{3,1},{4,6},{5,7},{6,4},{7,5},{8,10},{9,11},{10,... | collective-permute-start | bytes 1179656 | tf_op jit(solution)/shard_map/ppermute | solution.py:217
  92.9 2.5 %collective-permute-start.8 = (bf16[64,3072]{1,0:T(8,128)(2,1)}, bf16[64,3072]{1,0:T(8,128)(2,1)S(1)}, u32[]{:S(2)}, u32[]{:S(2)}) collective-permute-start(bf16[64,3072]{1,0:T(8,128)(2,1)} %get-tuple-element.24), channel_id=1, source_target_pairs={{0,1},{1,2},{2,3},{3,0},{4,5},{5,6},{6,7},{7,4},{8,9},{9,10},{10,1... | collective-permute-start | bytes 1179656 | tf_op jit(solution)/shard_map/ppermute | solution.py:217
  95.4 4.6 %collective-permute-start.9 = (bf16[64,3072]{1,0:T(8,128)(2,1)}, bf16[64,3072]{1,0:T(8,128)(2,1)S(1)}, u32[]{:S(2)}, u32[]{:S(2)}) collective-permute-start(bf16[64,3072]{1,0:T(8,128)(2,1)} %get-tuple-element.25), channel_id=1, source_target_pairs={{0,3},{1,0},{2,1},{3,2},{4,7},{5,4},{6,5},{7,6},{8,11},{9,8},{10,9... | collective-permute-start | bytes 1179656 | tf_op jit(solution)/shard_map/ppermute | solution.py:217
  100.0 3.2 %collective-permute-done.7.p1 = bf16[64,3072]{1,0:T(8,128)(2,1)S(1)} collective-permute-done((bf16[64,3072]{1,0:T(8,128)(2,1)}, bf16[64,3072]{1,0:T(8,128)(2,1)S(1)}, u32[]{:S(2)}, u32[]{:S(2)}) %collective-permute-start.7) | collective-permute-done | bytes 393248 | tf_op jit(solution)/shard_map/ppermute | solution.py:217
  103.2 7.7 %collective-permute-done.8.p2 = bf16[64,3072]{1,0:T(8,128)(2,1)S(1)} collective-permute-done((bf16[64,3072]{1,0:T(8,128)(2,1)}, bf16[64,3072]{1,0:T(8,128)(2,1)S(1)}, u32[]{:S(2)}, u32[]{:S(2)}) %collective-permute-start.8) | collective-permute-done | bytes 393248 | tf_op jit(solution)/shard_map/ppermute | solution.py:217
  110.9 0.3 collective-permute-done.9.p3
  111.2 0.2 shard_map.88
  111.4 16.2 %all_to_all.15.parts_ref = bf16[4,16,3072]{2,1,0:T(8,128)(2,1)S(1)} all-to-all(bf16[4,16,3072]{2,1,0:T(8,128)(2,1)S(1)} %bitcast.11), channel_id=1, replica_groups=mesh['y'=8,'zh'=4,'core'=2,'zl'=4,'x'=4] {'zl'}, dimensions={0} | all-to-all | bytes 786432 | tf_op jit(solution)/shard_map/all_to_all | solution.py:222
  127.6 0.0 copy-done.1
  127.6 0.0 copy-done.3
  127.6 0.0 copy-done.4
  127.6 0.7 shard_map.89
  128.3 13.0 %all_to_all.16 = f32[16,1,128]{2,1,0:T(1,128)S(1)} all-to-all(f32[16,1,128]{2,1,0:T(1,128)S(1)} %get-tuple-element.35), channel_id=1, replica_groups=mesh['y'=8,'zh'=4,'core'=2,'zl'=4,'x'=4] {'zl','x'}, dimensions={0} | all-to-all | bytes 16384 | tf_op jit(solution)/shard_map/all_to_all | solution.py:227
  141.3 0.6 slice_reduce_fusion
  (8 shorter events, 0.2 us)
Async XLA Ops:
  32.3 1.0 copy-start
  33.3 0.9 copy-start.2
  35.7 47.1 %all-to-all-start = ((bf16[16,16,3072]{2,1,0:T(8,128)(2,1)}), bf16[16,16,3072]{2,1,0:T(8,128)(2,1)S(1)}, u32[]{:S(2)}, u32[]{:S(2)}) async-start(bf16[16,16,3072]{2,1,0:T(8,128)(2,1)} %shard_map.86), calls=%async_computation | async-start | bytes 3145728 | tf_op jit(solution)/shard_map/all_to_all | solution.py:198
  43.3 11.4 %collective-permute-start = (bf16[4,48,512]{2,1,0:T(8,128)(2,1)S(1)}, bf16[4,48,512]{2,1,0:T(8,128)(2,1)S(1)}, u32[]{:S(2)}, u32[]{:S(2)}) collective-permute-start(bf16[4,48,512]{2,1,0:T(8,128)(2,1)S(1)} %bitcast.17), channel_id=1, source_target_pairs={{0,128},{128,256},{256,384},{384,512},{512,640},{640,768},{768,896... | collective-permute-start | bytes 589832 | tf_op jit(solution)/shard_map/ppermute | solution.py:18
  45.2 9.4 %collective-permute-start.1 = (bf16[4,48,512]{2,1,0:T(8,128)(2,1)S(1)}, bf16[4,48,512]{2,1,0:T(8,128)(2,1)S(1)}, u32[]{:S(2)}, u32[]{:S(2)}) collective-permute-start(bf16[4,48,512]{2,1,0:T(8,128)(2,1)S(1)} %bitcast.18), channel_id=1, source_target_pairs={{0,896},{128,0},{256,128},{384,256},{512,384},{640,512},{768,640},... | collective-permute-start | bytes 589832 | tf_op jit(solution)/shard_map/ppermute | solution.py:18
  49.1 15.5 %collective-permute-start.2 = (bf16[4,48,512]{2,1,0:T(8,128)(2,1)S(1)}, bf16[4,48,512]{2,1,0:T(8,128)(2,1)S(1)}, u32[]{:S(2)}, u32[]{:S(2)}) collective-permute-start(bf16[4,48,512]{2,1,0:T(8,128)(2,1)S(1)} %bitcast.19), channel_id=1, source_target_pairs={{0,512},{128,640},{256,768},{384,896},{512,0},{640,128},{768,256},... | collective-permute-start | bytes 589832 | tf_op jit(solution)/shard_map/ppermute | solution.py:18
  64.7 15.7 %copy-start.5 = (s32[64]{0:T(128)S(1)}, s32[64]{0:T(128)}, u32[]{:S(2)}) copy-start(s32[64]{0:T(128)} %param.10) | copy-start | bytes 772
  64.7 10.5 %collective-permute-start.3 = (bf16[8,48,512]{2,1,0:T(8,128)(2,1)S(1)}, bf16[8,48,512]{2,1,0:T(8,128)(2,1)S(1)}, u32[]{:S(2)}, u32[]{:S(2)}) collective-permute-start(bf16[8,48,512]{2,1,0:T(8,128)(2,1)S(1)} %get-tuple-element.39), channel_id=1, source_target_pairs={{0,128},{128,256},{256,384},{384,512},{512,640},{640,768},{768,896... | collective-permute-start | bytes 1179656 | tf_op jit(solution)/shard_map/ppermute | solution.py:18
  66.7 11.8 %collective-permute-start.4 = (bf16[8,48,512]{2,1,0:T(8,128)(2,1)S(1)}, bf16[8,48,512]{2,1,0:T(8,128)(2,1)S(1)}, u32[]{:S(2)}, u32[]{:S(2)}) collective-permute-start(bf16[8,48,512]{2,1,0:T(8,128)(2,1)S(1)} %get-tuple-element.38), channel_id=1, source_target_pairs={{0,896},{128,0},{256,128},{384,256},{512,384},{640,512},{768,640},... | collective-permute-start | bytes 1179656 | tf_op jit(solution)/shard_map/ppermute | solution.py:18
  70.7 9.9 %collective-permute-start.5 = (bf16[16,48,512]{2,1,0:T(8,128)(2,1)S(1)}, bf16[16,48,512]{2,1,0:T(8,128)(2,1)}, u32[]{:S(2)}, u32[]{:S(2)}) collective-permute-start(bf16[16,48,512]{2,1,0:T(8,128)(2,1)S(1)} %constant_dynamic-update-slice_fusion.own0), channel_id=1, source_target_pairs={{0,16},{16,0},{1,17},{17,1},{2,18},{18,2},{3,19},{19,3},{4,20},{20... | collective-permute-start | bytes 2359304 | tf_op jit(solution)/shard_map/ppermute | solution.py:22
  78.5 4.3 %collective-permute-start.6 = (bf16[16,48,512]{2,1,0:T(8,128)(2,1)S(1)}, bf16[16,48,512]{2,1,0:T(8,128)(2,1)}, u32[]{:S(2)}, u32[]{:S(2)}) collective-permute-start(bf16[16,48,512]{2,1,0:T(8,128)(2,1)S(1)} %constant_dynamic-update-slice_fusion.4.own1), channel_id=1, source_target_pairs={{0,16},{16,0},{1,17},{17,1},{2,18},{18,2},{3,19},{19,3},{4,20},{20... | collective-permute-start | bytes 2359304 | tf_op jit(solution)/shard_map/ppermute | solution.py:22
  87.4 40.2 %copy-start.1 = (f32[8,3,3072]{2,0,1:T(8,128)S(1)}, f32[8,3,3072]{2,0,1:T(8,128)}, u32[]{:S(2)}) copy-start(f32[8,3,3072]{2,0,1:T(8,128)} %param.11) | copy-start | bytes 884740
  87.4 40.2 %copy-start.3 = (bf16[1,16,3072]{2,1,0:T(8,128)(2,1)S(1)}, bf16[1,16,3072]{2,1,0:T(8,128)(2,1)}, u32[]{:S(2)}) copy-start(bf16[1,16,3072]{2,1,0:T(8,128)(2,1)} %param.7) | copy-start | bytes 294916
  87.4 40.2 %copy-start.4 = (bf16[1,16,3072]{2,1,0:T(8,128)(2,1)S(1)}, bf16[1,16,3072]{2,1,0:T(8,128)(2,1)}, u32[]{:S(2)}) copy-start(bf16[1,16,3072]{2,1,0:T(8,128)(2,1)} %param.8) | copy-start | bytes 294916
  87.4 15.8 %collective-permute-start.7 = (bf16[64,3072]{1,0:T(8,128)(2,1)}, bf16[64,3072]{1,0:T(8,128)(2,1)S(1)}, u32[]{:S(2)}, u32[]{:S(2)}) collective-permute-start(bf16[64,3072]{1,0:T(8,128)(2,1)} %get-tuple-element.23), channel_id=1, source_target_pairs={{0,2},{1,3},{2,0},{3,1},{4,6},{5,7},{6,4},{7,5},{8,10},{9,11},{10,... | collective-permute-start | bytes 1179656 | tf_op jit(solution)/shard_map/ppermute | solution.py:217
  92.9 18.0 %collective-permute-start.8 = (bf16[64,3072]{1,0:T(8,128)(2,1)}, bf16[64,3072]{1,0:T(8,128)(2,1)S(1)}, u32[]{:S(2)}, u32[]{:S(2)}) collective-permute-start(bf16[64,3072]{1,0:T(8,128)(2,1)} %get-tuple-element.24), channel_id=1, source_target_pairs={{0,1},{1,2},{2,3},{3,0},{4,5},{5,6},{6,7},{7,4},{8,9},{9,10},{10,1... | collective-permute-start | bytes 1179656 | tf_op jit(solution)/shard_map/ppermute | solution.py:217
  95.4 15.8 %collective-permute-start.9 = (bf16[64,3072]{1,0:T(8,128)(2,1)}, bf16[64,3072]{1,0:T(8,128)(2,1)S(1)}, u32[]{:S(2)}, u32[]{:S(2)}) collective-permute-start(bf16[64,3072]{1,0:T(8,128)(2,1)} %get-tuple-element.25), channel_id=1, source_target_pairs={{0,3},{1,0},{2,1},{3,2},{4,7},{5,4},{6,5},{7,6},{8,11},{9,8},{10,9... | collective-permute-start | bytes 1179656 | tf_op jit(solution)/shard_map/ppermute | solution.py:217

commit v6 on v5

--- a/solution.py
+++ b/solution.py
@@ -35,32 +35,30 @@
     return near, jnp.concatenate([up, down], axis=0)
 
 
-def norm_kernel(t_ref, x_ref, table_ref, o_ref):
-    t = t_ref[0]
+def norm_kernel(x_ref, rows_ref, o_ref):
     x = x_ref[...].astype(jnp.float32)
     width = x.shape[1]
     centred = x - jnp.sum(x, axis=1, keepdims=True) / width
     variance = jnp.sum(centred * centred, axis=1, keepdims=True) / width
     normed = centred * lax.rsqrt(variance + 1e-06)
-    shift, scale = table_ref[0, pl.ds(t, 1), :], table_ref[1, pl.ds(t, 1), :]
-    modulated = (normed * (1.0 + scale) + shift).astype(jnp.bfloat16)
+    modulated = (normed * (1.0 + rows_ref[1:2, :]) + rows_ref[0:1, :]).astype(jnp.bfloat16)
     for i in range(o_ref.shape[0]):
         o_ref[i] = modulated
 
 
-def normalised_copies(t, tokens, table, copies):
+def normalised_copies(tokens, mod, copies):
     rows, width = tokens.shape
     vmem = pl.BlockSpec(memory_space=pltpu.VMEM)
     return pl.pallas_call(
         norm_kernel,
         out_shape=jax.ShapeDtypeStruct((copies, rows, width), jnp.bfloat16),
-        in_specs=[pl.BlockSpec(memory_space=pltpu.SMEM), vmem, vmem],
+        in_specs=[vmem, vmem],
         out_specs=vmem,
         compiler_params=pltpu.CompilerParams(vmem_limit_bytes=16 * 1024 * 1024),
         cost_estimate=pl.CostEstimate(
             flops=12 * rows * width, bytes_accessed=40 * rows * width, transcendentals=rows
         ),
-    )(t, tokens, table)
+    )(tokens, mod)
 
 
 def head_kernel(to_ref, row_ref, x_ref, own0, own1, other0, other1, *rest):
@@ -191,10 +189,10 @@
     spread = 2.0 * sigma * sigma * seq_len * width
     offset = jnp.log(sigma) + 0.5 * math.log(2.0 * math.pi)
 
+    mod = lax.dynamic_index_in_dim(mod_table, timestep[0], 0, keepdims=False)
     weights = jnp.concatenate([qkv_weight, out_weight.T], axis=1)
     plane = lax.all_gather(weights, "zh", tiled=False)
-    sent, plane = lax.optimization_barrier((latents[0], plane))
-    copies = normalised_copies(timestep, sent, table, NZL * NX)
+    copies = normalised_copies(latents[0], mod, NZL * NX)
     tokens = lax.all_to_all(copies, TENSOR, split_axis=0, concat_axis=0, tiled=True)
     near, far = around_y(plane)
     pieces = (near, far, swapped(near), swapped(far))

time: 144 us -> 175 us (1.22); the launches traced: 144 us -> 173 us
  blocking collectives: 59.4 us -> 89 us
    all_gather x1, blocking collectives: 30.2 us -> 50.4 us  [one_device(): plane = lax.all_gather(weights, 'zh', tiled=False)]
    all_to_all x1, blocking collectives: 16.2 us -> 25.5 us  [one_device(): lax.all_to_all(some.reshape(NZL, tok_local, width), 'zl', split_axis=0, c...]
    all_to_all x1, starting transfers between devices: 7.59 us -> 9.96 us  [one_device(): lax.all_to_all(copies, TENSOR, split_axis=0, concat_axis=0, tiled=True)]
    ppermute x5, waiting for transfers between devices: 15.8 us -> 13.5 us  [shifted(): return lax.ppermute(x, 'y', [(i, (i + by) % NY) for i in range(NY)])]
where the time goes in v6:
time: 175 us; the launch traced here: 173 us
  blocking collectives  89 us (51%)
  starting transfers between devices  42.6 us (24%)
  waiting for transfers between devices  27.7 us (16%)
  Pallas kernels  7.07 us (4%)
  between operations  3.36 us (2%)
  local copies, waits for them, and re-layouts  1.97 us (1%)
    all_gather x1, blocking collectives, one_device(): plane = lax.all_gather(weights, 'zh', tiled=False)  50.4 us
    all_to_all x1, blocking collectives, one_device(): lax.all_to_all(some.reshape(NZL, tok_local, width), 'zl', split_axis=0, c...  25.5 us
    ppermute x5, starting transfers between devices, shifted(): return lax.ppermute(x, 'y', [(i, (i + by) % NY) for i in range(NY)])  17.6 us
    ppermute x5, waiting for transfers between devices, shifted(): return lax.ppermute(x, 'y', [(i, (i + by) % NY) for i in range(NY)])  13.5 us
    all_to_all x1, blocking collectives, one_device(): lax.all_to_all(squares, TENSOR, split_axis=0, concat_axis=0, tiled=True)  13.1 us
    ppermute x3, waiting for transfers between devices, one_device(): lax.ppermute(terms[r], 'x', [(i, (i + r) % NX) for i in range(NX)])  12.1 us
    ppermute x3, starting transfers between devices, one_device(): lax.ppermute(terms[r], 'x', [(i, (i + r) % NX) for i in range(NX)])  11.2 us
    all_to_all x1, starting transfers between devices, one_device(): lax.all_to_all(copies, TENSOR, split_axis=0, concat_axis=0, tiled=True)  9.96 us
  transfers between devices with their start and end apart: 11, of which 7 were waited for; matrix products, arithmetic and copies ran while one was open for 0% of the time, Pallas kernels for 0%

profile of v6, /device:TPU:56, one launch (start us, length us, event | category | flops | bytes accessed | tf_op | source)
XLA Modules:
  0.0 172.7 jit_solution(9281940251708701513)
XLA Ops:
  1.3 1.0 constant_dynamic-slice_fusion
  2.3 0.0 copy-start
  2.3 0.9 copy-done
  3.2 1.5 shard_map.86
  4.7 0.0 copy-start.4
  4.7 0.0 copy-start.5
  4.7 10.0 %all-to-all-start = ((bf16[16,16,3072]{2,1,0:T(8,128)(2,1)}), bf16[16,16,3072]{2,1,0:T(8,128)(2,1)S(1)}, u32[]{:S(2)}, u32[]{:S(2)}) async-start(bf16[16,16,3072]{2,1,0:T(8,128)(2,1)} %shard_map.86), calls=%async_computation | async-start | bytes 3145728 | tf_op jit(solution)/shard_map/all_to_all | solution.py:196
  14.7 0.0 copy-done.4
  14.7 0.0 copy-done.5
  14.7 50.4 %all-gather = bf16[192,512]{1,0:T(8,128)(2,1)S(1)} all-gather(bf16[48,512]{1,0:T(8,128)(2,1)S(1)} %pad_maximum_fusion.3), channel_id=2, replica_groups=mesh['y'=8,'zh'=4,'core'=2,'zl'=4,'x'=4] {'zh'}, dimensions={0}, use_global_device_ids=true | all-gather | bytes 245760 | tf_op jit(solution)/shard_map/all_gather | solution.py:194
  65.1 4.7 %collective-permute-start.2 = (bf16[4,48,512]{2,1,0:T(8,128)(2,1)S(1)}, bf16[4,48,512]{2,1,0:T(8,128)(2,1)S(1)}, u32[]{:S(2)}, u32[]{:S(2)}) collective-permute-start(bf16[4,48,512]{2,1,0:T(8,128)(2,1)S(1)} %bitcast.24), channel_id=1, source_target_pairs={{0,512},{128,640},{256,768},{384,896},{512,0},{640,128},{768,256},... | collective-permute-start | bytes 589832 | tf_op jit(solution)/shard_map/ppermute | solution.py:18
  69.8 2.4 %collective-permute-start.1 = (bf16[4,48,512]{2,1,0:T(8,128)(2,1)S(1)}, bf16[4,48,512]{2,1,0:T(8,128)(2,1)S(1)}, u32[]{:S(2)}, u32[]{:S(2)}) collective-permute-start(bf16[4,48,512]{2,1,0:T(8,128)(2,1)S(1)} %bitcast.25), channel_id=1, source_target_pairs={{0,896},{128,0},{256,128},{384,256},{512,384},{640,512},{768,640},... | collective-permute-start | bytes 589832 | tf_op jit(solution)/shard_map/ppermute | solution.py:18
  72.2 4.7 %collective-permute-start = (bf16[4,48,512]{2,1,0:T(8,128)(2,1)S(1)}, bf16[4,48,512]{2,1,0:T(8,128)(2,1)S(1)}, u32[]{:S(2)}, u32[]{:S(2)}) collective-permute-start(bf16[4,48,512]{2,1,0:T(8,128)(2,1)S(1)} %bitcast.26), channel_id=1, source_target_pairs={{0,128},{128,256},{256,384},{384,512},{512,640},{640,768},{768,896... | collective-permute-start | bytes 589832 | tf_op jit(solution)/shard_map/ppermute | solution.py:18
  76.9 3.9 %collective-permute-done.2 = bf16[4,48,512]{2,1,0:T(8,128)(2,1)S(1)} collective-permute-done((bf16[4,48,512]{2,1,0:T(8,128)(2,1)S(1)}, bf16[4,48,512]{2,1,0:T(8,128)(2,1)S(1)}, u32[]{:S(2)}, u32[]{:S(2)}) %collective-permute-start.2) | collective-permute-done | bytes 196640 | tf_op jit(solution)/shard_map/ppermute | solution.py:18
  80.8 2.2 %collective-permute-done.1 = bf16[4,48,512]{2,1,0:T(8,128)(2,1)S(1)} collective-permute-done((bf16[4,48,512]{2,1,0:T(8,128)(2,1)S(1)}, bf16[4,48,512]{2,1,0:T(8,128)(2,1)S(1)}, u32[]{:S(2)}, u32[]{:S(2)}) %collective-permute-start.1) | collective-permute-done | bytes 196640 | tf_op jit(solution)/shard_map/ppermute | solution.py:18
  83.0 0.0 collective-permute-done
  83.0 0.1 pad_maximum_fusion.1
  83.0 2.7 %collective-permute-start.3 = (bf16[8,48,512]{2,1,0:T(8,128)(2,1)S(1)}, bf16[8,48,512]{2,1,0:T(8,128)(2,1)S(1)}, u32[]{:S(2)}, u32[]{:S(2)}) collective-permute-start(bf16[8,48,512]{2,1,0:T(8,128)(2,1)S(1)} %get-tuple-element.35), channel_id=1, source_target_pairs={{0,128},{128,256},{256,384},{384,512},{512,640},{640,768},{768,896... | collective-permute-start | bytes 1179656 | tf_op jit(solution)/shard_map/ppermute | solution.py:18
  85.8 0.0 copy-start.6
  85.8 3.1 %collective-permute-start.4 = (bf16[8,48,512]{2,1,0:T(8,128)(2,1)S(1)}, bf16[8,48,512]{2,1,0:T(8,128)(2,1)S(1)}, u32[]{:S(2)}, u32[]{:S(2)}) collective-permute-start(bf16[8,48,512]{2,1,0:T(8,128)(2,1)S(1)} %get-tuple-element.34), channel_id=1, source_target_pairs={{0,896},{128,0},{256,128},{384,256},{512,384},{640,512},{768,640},... | collective-permute-start | bytes 1179656 | tf_op jit(solution)/shard_map/ppermute | solution.py:18
  88.9 0.1 pad_maximum_fusion.own0
  89.0 1.9 %collective-permute-start.5 = (bf16[16,48,512]{2,1,0:T(8,128)(2,1)S(1)}, bf16[16,48,512]{2,1,0:T(8,128)(2,1)}, u32[]{:S(2)}, u32[]{:S(2)}) collective-permute-start(bf16[16,48,512]{2,1,0:T(8,128)(2,1)S(1)} %pad_maximum_fusion.own0), channel_id=1, source_target_pairs={{0,16},{16,0},{1,17},{17,1},{2,18},{18,2},{3,19},{19,3},{4,20},{20... | collective-permute-start | bytes 2359304 | tf_op jit(solution)/shard_map/ppermute | solution.py:22
  90.9 4.3 %collective-permute-done.3 = bf16[8,48,512]{2,1,0:T(8,128)(2,1)S(1)} collective-permute-done((bf16[8,48,512]{2,1,0:T(8,128)(2,1)S(1)}, bf16[8,48,512]{2,1,0:T(8,128)(2,1)S(1)}, u32[]{:S(2)}, u32[]{:S(2)}) %collective-permute-start.3) | collective-permute-done | bytes 393248 | tf_op jit(solution)/shard_map/ppermute | solution.py:18
  95.3 3.1 %collective-permute-done.4 = bf16[8,48,512]{2,1,0:T(8,128)(2,1)S(1)} collective-permute-done((bf16[8,48,512]{2,1,0:T(8,128)(2,1)S(1)}, bf16[8,48,512]{2,1,0:T(8,128)(2,1)S(1)}, u32[]{:S(2)}, u32[]{:S(2)}) %collective-permute-start.4) | collective-permute-done | bytes 393248 | tf_op jit(solution)/shard_map/ppermute | solution.py:18
  98.4 1.9 %collective-permute-start.6 = (bf16[16,48,512]{2,1,0:T(8,128)(2,1)S(1)}, bf16[16,48,512]{2,1,0:T(8,128)(2,1)}, u32[]{:S(2)}, u32[]{:S(2)}) collective-permute-start(bf16[16,48,512]{2,1,0:T(8,128)(2,1)S(1)} %constant_dynamic-update-slice_fusion.own1), channel_id=1, source_target_pairs={{0,16},{16,0},{1,17},{17,1},{2,18},{18,2},{3,19},{19,3},{4,20},{20... | collective-permute-start | bytes 2359304 | tf_op jit(solution)/shard_map/ppermute | solution.py:22
  100.4 0.0 copy-done.6
  100.4 0.1 select_reduce_fusion.to_ref
  100.5 0.0 collective-permute-done.5.other0
  100.5 2.2 %collective-permute-done.6.other1 = bf16[16,48,512]{2,1,0:T(8,128)(2,1)} collective-permute-done((bf16[16,48,512]{2,1,0:T(8,128)(2,1)S(1)}, bf16[16,48,512]{2,1,0:T(8,128)(2,1)}, u32[]{:S(2)}, u32[]{:S(2)}) %collective-permute-start.6) | collective-permute-done | bytes 786464 | tf_op jit(solution)/shard_map/ppermute | solution.py:22
  102.7 0.0 all-to-all-done
  102.7 4.6 %shard_map.87 = (bf16[64,3072]{1,0:T(8,128)(2,1)S(1)}, bf16[64,3072]{1,0:T(8,128)(2,1)}, bf16[64,3072]{1,0:T(8,128)(2,1)}, bf16[64,3072]{1,0:T(8,128)(2,1)}) custom-call(s32[64]{0:T(128)S(1)} %select_reduce_fusion.to_ref, s32[16]{0:T(128)S(1)} %fusion.8.row_ref, bf16[256,3072]{1,0:T(8,128)(2,1)S(1)} %bitcast.17, ...), custom_call_target="tpu_custom_call" | custom-call | flops 805306368 | bytes 6291456 | tf_op jit(solution)/shard_map/pallas_call | solution.py:102
  107.3 0.0 copy-start.1
  107.4 0.0 copy-start.2
  107.4 0.0 copy-start.3
  107.4 4.1 %collective-permute-start.7 = (bf16[64,3072]{1,0:T(8,128)(2,1)}, bf16[64,3072]{1,0:T(8,128)(2,1)S(1)}, u32[]{:S(2)}, u32[]{:S(2)}) collective-permute-start(bf16[64,3072]{1,0:T(8,128)(2,1)} %get-tuple-element.19), channel_id=1, source_target_pairs={{0,2},{1,3},{2,0},{3,1},{4,6},{5,7},{6,4},{7,5},{8,10},{9,11},{10,... | collective-permute-start | bytes 1179656 | tf_op jit(solution)/shard_map/ppermute | solution.py:215
  111.5 2.5 %collective-permute-start.8 = (bf16[64,3072]{1,0:T(8,128)(2,1)}, bf16[64,3072]{1,0:T(8,128)(2,1)S(1)}, u32[]{:S(2)}, u32[]{:S(2)}) collective-permute-start(bf16[64,3072]{1,0:T(8,128)(2,1)} %get-tuple-element.20), channel_id=1, source_target_pairs={{0,1},{1,2},{2,3},{3,0},{4,5},{5,6},{6,7},{7,4},{8,9},{9,10},{10,1... | collective-permute-start | bytes 1179656 | tf_op jit(solution)/shard_map/ppermute | solution.py:215
  114.0 4.6 %collective-permute-start.9 = (bf16[64,3072]{1,0:T(8,128)(2,1)}, bf16[64,3072]{1,0:T(8,128)(2,1)S(1)}, u32[]{:S(2)}, u32[]{:S(2)}) collective-permute-start(bf16[64,3072]{1,0:T(8,128)(2,1)} %get-tuple-element.21), channel_id=1, source_target_pairs={{0,3},{1,0},{2,1},{3,2},{4,7},{5,4},{6,5},{7,6},{8,11},{9,8},{10,9... | collective-permute-start | bytes 1179656 | tf_op jit(solution)/shard_map/ppermute | solution.py:215
  118.6 4.5 %collective-permute-done.7.p1 = bf16[64,3072]{1,0:T(8,128)(2,1)S(1)} collective-permute-done((bf16[64,3072]{1,0:T(8,128)(2,1)}, bf16[64,3072]{1,0:T(8,128)(2,1)S(1)}, u32[]{:S(2)}, u32[]{:S(2)}) %collective-permute-start.7) | collective-permute-done | bytes 393248 | tf_op jit(solution)/shard_map/ppermute | solution.py:215
  123.1 7.6 %collective-permute-done.8.p2 = bf16[64,3072]{1,0:T(8,128)(2,1)S(1)} collective-permute-done((bf16[64,3072]{1,0:T(8,128)(2,1)}, bf16[64,3072]{1,0:T(8,128)(2,1)S(1)}, u32[]{:S(2)}, u32[]{:S(2)}) %collective-permute-start.8) | collective-permute-done | bytes 393248 | tf_op jit(solution)/shard_map/ppermute | solution.py:215
  130.7 0.0 collective-permute-done.9.p3
  130.7 0.2 shard_map.88
  130.9 25.5 %all_to_all.15.parts_ref = bf16[4,16,3072]{2,1,0:T(8,128)(2,1)S(1)} all-to-all(bf16[4,16,3072]{2,1,0:T(8,128)(2,1)S(1)} %bitcast.18), channel_id=1, replica_groups=mesh['y'=8,'zh'=4,'core'=2,'zl'=4,'x'=4] {'zl'}, dimensions={0} | all-to-all | bytes 786432 | tf_op jit(solution)/shard_map/all_to_all | solution.py:220
  156.4 0.0 copy-done.1
  156.4 0.0 copy-done.2
  156.4 0.0 copy-done.3
  156.4 0.7 shard_map.89
  157.1 13.1 %all_to_all.16 = f32[16,1,128]{2,1,0:T(1,128)S(1)} all-to-all(f32[16,1,128]{2,1,0:T(1,128)S(1)} %get-tuple-element.31), channel_id=1, replica_groups=mesh['y'=8,'zh'=4,'core'=2,'zl'=4,'x'=4] {'zl','x'}, dimensions={0} | all-to-all | bytes 16384 | tf_op jit(solution)/shard_map/all_to_all | solution.py:225
  170.2 0.6 slice_reduce_fusion
  (6 shorter events, 0.1 us)
Async XLA Ops:
  2.3 0.9 copy-start
  4.7 10.0 %copy-start.4 = (bf16[48,384]{1,0:T(8,128)(2,1)S(1)}, bf16[48,384]{1,0:T(8,128)(2,1)}, u32[]{:S(2)}) copy-start(bf16[48,384]{1,0:T(8,128)(2,1)} %param.12) | copy-start | bytes 110596
  4.7 10.0 %copy-start.5 = (bf16[128,48]{0,1:T(8,128)(2,1)S(1)}, bf16[128,48]{0,1:T(8,128)(2,1)}, u32[]{:S(2)}) copy-start(bf16[128,48]{0,1:T(8,128)(2,1)} %param.13) | copy-start | bytes 36868
  4.7 98.0 %all-to-all-start = ((bf16[16,16,3072]{2,1,0:T(8,128)(2,1)}), bf16[16,16,3072]{2,1,0:T(8,128)(2,1)S(1)}, u32[]{:S(2)}, u32[]{:S(2)}) async-start(bf16[16,16,3072]{2,1,0:T(8,128)(2,1)} %shard_map.86), calls=%async_computation | async-start | bytes 3145728 | tf_op jit(solution)/shard_map/all_to_all | solution.py:196
  65.1 15.7 %collective-permute-start.2 = (bf16[4,48,512]{2,1,0:T(8,128)(2,1)S(1)}, bf16[4,48,512]{2,1,0:T(8,128)(2,1)S(1)}, u32[]{:S(2)}, u32[]{:S(2)}) collective-permute-start(bf16[4,48,512]{2,1,0:T(8,128)(2,1)S(1)} %bitcast.24), channel_id=1, source_target_pairs={{0,512},{128,640},{256,768},{384,896},{512,0},{640,128},{768,256},... | collective-permute-start | bytes 589832 | tf_op jit(solution)/shard_map/ppermute | solution.py:18
  69.8 13.1 %collective-permute-start.1 = (bf16[4,48,512]{2,1,0:T(8,128)(2,1)S(1)}, bf16[4,48,512]{2,1,0:T(8,128)(2,1)S(1)}, u32[]{:S(2)}, u32[]{:S(2)}) collective-permute-start(bf16[4,48,512]{2,1,0:T(8,128)(2,1)S(1)} %bitcast.25), channel_id=1, source_target_pairs={{0,896},{128,0},{256,128},{384,256},{512,384},{640,512},{768,640},... | collective-permute-start | bytes 589832 | tf_op jit(solution)/shard_map/ppermute | solution.py:18
  72.2 10.8 %collective-permute-start = (bf16[4,48,512]{2,1,0:T(8,128)(2,1)S(1)}, bf16[4,48,512]{2,1,0:T(8,128)(2,1)S(1)}, u32[]{:S(2)}, u32[]{:S(2)}) collective-permute-start(bf16[4,48,512]{2,1,0:T(8,128)(2,1)S(1)} %bitcast.26), channel_id=1, source_target_pairs={{0,128},{128,256},{256,384},{384,512},{512,640},{640,768},{768,896... | collective-permute-start | bytes 589832 | tf_op jit(solution)/shard_map/ppermute | solution.py:18
  83.0 12.2 %collective-permute-start.3 = (bf16[8,48,512]{2,1,0:T(8,128)(2,1)S(1)}, bf16[8,48,512]{2,1,0:T(8,128)(2,1)S(1)}, u32[]{:S(2)}, u32[]{:S(2)}) collective-permute-start(bf16[8,48,512]{2,1,0:T(8,128)(2,1)S(1)} %get-tuple-element.35), channel_id=1, source_target_pairs={{0,128},{128,256},{256,384},{384,512},{512,640},{640,768},{768,896... | collective-permute-start | bytes 1179656 | tf_op jit(solution)/shard_map/ppermute | solution.py:18
  85.8 14.6 %copy-start.6 = (s32[64]{0:T(128)S(1)}, s32[64]{0:T(128)}, u32[]{:S(2)}) copy-start(s32[64]{0:T(128)} %param.10) | copy-start | bytes 772
  85.8 12.6 %collective-permute-start.4 = (bf16[8,48,512]{2,1,0:T(8,128)(2,1)S(1)}, bf16[8,48,512]{2,1,0:T(8,128)(2,1)S(1)}, u32[]{:S(2)}, u32[]{:S(2)}) collective-permute-start(bf16[8,48,512]{2,1,0:T(8,128)(2,1)S(1)} %get-tuple-element.34), channel_id=1, source_target_pairs={{0,896},{128,0},{256,128},{384,256},{512,384},{640,512},{768,640},... | collective-permute-start | bytes 1179656 | tf_op jit(solution)/shard_map/ppermute | solution.py:18
  89.0 11.5 %collective-permute-start.5 = (bf16[16,48,512]{2,1,0:T(8,128)(2,1)S(1)}, bf16[16,48,512]{2,1,0:T(8,128)(2,1)}, u32[]{:S(2)}, u32[]{:S(2)}) collective-permute-start(bf16[16,48,512]{2,1,0:T(8,128)(2,1)S(1)} %pad_maximum_fusion.own0), channel_id=1, source_target_pairs={{0,16},{16,0},{1,17},{17,1},{2,18},{18,2},{3,19},{19,3},{4,20},{20... | collective-permute-start | bytes 2359304 | tf_op jit(solution)/shard_map/ppermute | solution.py:22
  98.4 4.3 %collective-permute-start.6 = (bf16[16,48,512]{2,1,0:T(8,128)(2,1)S(1)}, bf16[16,48,512]{2,1,0:T(8,128)(2,1)}, u32[]{:S(2)}, u32[]{:S(2)}) collective-permute-start(bf16[16,48,512]{2,1,0:T(8,128)(2,1)S(1)} %constant_dynamic-update-slice_fusion.own1), channel_id=1, source_target_pairs={{0,16},{16,0},{1,17},{17,1},{2,18},{18,2},{3,19},{19,3},{4,20},{20... | collective-permute-start | bytes 2359304 | tf_op jit(solution)/shard_map/ppermute | solution.py:22
  107.3 49.0 %copy-start.1 = (bf16[1,16,3072]{2,1,0:T(8,128)(2,1)S(1)}, bf16[1,16,3072]{2,1,0:T(8,128)(2,1)}, u32[]{:S(2)}) copy-start(bf16[1,16,3072]{2,1,0:T(8,128)(2,1)} %param.7) | copy-start | bytes 294916
  107.4 49.0 %copy-start.2 = (f32[8,3,3072]{2,0,1:T(8,128)S(1)}, f32[8,3,3072]{2,0,1:T(8,128)}, u32[]{:S(2)}) copy-start(f32[8,3,3072]{2,0,1:T(8,128)} %param.11) | copy-start | bytes 884740
  107.4 49.0 %copy-start.3 = (bf16[1,16,3072]{2,1,0:T(8,128)(2,1)S(1)}, bf16[1,16,3072]{2,1,0:T(8,128)(2,1)}, u32[]{:S(2)}) copy-start(bf16[1,16,3072]{2,1,0:T(8,128)(2,1)} %param.8) | copy-start | bytes 294916
  107.4 15.8 %collective-permute-start.7 = (bf16[64,3072]{1,0:T(8,128)(2,1)}, bf16[64,3072]{1,0:T(8,128)(2,1)S(1)}, u32[]{:S(2)}, u32[]{:S(2)}) collective-permute-start(bf16[64,3072]{1,0:T(8,128)(2,1)} %get-tuple-element.19), channel_id=1, source_target_pairs={{0,2},{1,3},{2,0},{3,1},{4,6},{5,7},{6,4},{7,5},{8,10},{9,11},{10,... | collective-permute-start | bytes 1179656 | tf_op jit(solution)/shard_map/ppermute | solution.py:215
  111.5 19.2 %collective-permute-start.8 = (bf16[64,3072]{1,0:T(8,128)(2,1)}, bf16[64,3072]{1,0:T(8,128)(2,1)S(1)}, u32[]{:S(2)}, u32[]{:S(2)}) collective-permute-start(bf16[64,3072]{1,0:T(8,128)(2,1)} %get-tuple-element.20), channel_id=1, source_target_pairs={{0,1},{1,2},{2,3},{3,0},{4,5},{5,6},{6,7},{7,4},{8,9},{9,10},{10,1... | collective-permute-start | bytes 1179656 | tf_op jit(solution)/shard_map/ppermute | solution.py:215
  114.0 16.7 %collective-permute-start.9 = (bf16[64,3072]{1,0:T(8,128)(2,1)}, bf16[64,3072]{1,0:T(8,128)(2,1)S(1)}, u32[]{:S(2)}, u32[]{:S(2)}) collective-permute-start(bf16[64,3072]{1,0:T(8,128)(2,1)} %get-tuple-element.21), channel_id=1, source_target_pairs={{0,3},{1,0},{2,1},{3,2},{4,7},{5,4},{6,5},{7,6},{8,11},{9,8},{10,9... | collective-permute-start | bytes 1179656 | tf_op jit(solution)/shard_map/ppermute | solution.py:215
